TPU v7x, 768 devices: a whole 4x8x12 slice. The times are simulated.
768 devices in a mesh: nodes: 128 (over x, y, z_hi), years: 6 (over z_lo, core).
Axes of the slice: x: 4, y: 8, z: 12 (z_hi: 4, z_lo: 3; z = z_hi * 3 + z_lo), core: 2. Of those that a mesh axis runs over, the one named last changes fastest.
Arguments:
- features: float32 [65536, 768], P('nodes', 'years'), may hold values from -6 to 6
- weight: float32 [768, 512], P('years'), may hold values from -0.21875 to 0.21875
- bias: float32 [512], replicated, may hold values from -3 to 3
- tile_weights: float32 [512, 4, 128, 128], P('nodes'), may hold values from 0.0001 to 0.5, as said below
- tile_offsets: int32 [512, 4], P('nodes'), may hold values from -8 to 8, as said below
- tile_counts: int32 [512], P('nodes'), may hold values from 1 to 4
- grad_out: float32 [65536, 512], P('nodes'), may hold values from -6 to 6
Outputs:
- output: float32 [65536, 512], P('nodes')
- grad_features: float32 [65536, 768], P('nodes', 'years')
- grad_weight: float32 [768, 512], P('years')
- grad_bias: float32 [512], replicated
Inputs may be any that keep to these rules, and one draw needn't show every extreme that they name: `tile_weights`: Positive. `tile_offsets`: the live slots of a row tile name distinct offsets; slots at or past tile_counts are ignored.
All inputs are finite; a program needn't handle non-finite values.
Results may differ from a plain program's by a relative error of at most 0.0001.
Values sent between devices are 32-bit elements; how exact they have to be, the bound alone decides.
No kernel may reach another device: no remote copies, remote signals or barrier semaphores. Data moves between devices by JAX's collectives and lax.ppermute only.
A program may use at most 64 MiB of HBM per device.

v0:
```python
import jax
import jax.numpy as jnp
from jax import lax
from jax.sharding import PartitionSpec as P

REACH = 2


def passed_along(block, axis, distance):
    devices = range(lax.axis_size(axis))
    route = [((i - distance) % len(devices), i) for i in devices]
    return lax.ppermute(block, axis, route)


def body(features, weight, bias, tile_weights, tile_offsets, tile_counts, grad_out):
    highest = lax.Precision.HIGHEST
    row_total, feat_width = features.shape
    tile_rows = tile_weights.shape[0]
    slot_total = tile_weights.shape[1]
    tile_size = tile_weights.shape[2]
    live = (jnp.arange(slot_total, dtype=jnp.int32)[None, :] < tile_counts[:, None]).astype(
        jnp.float32
    )
    masked = tile_weights * live[:, :, None, None]
    degree = 1.0 + jnp.sum(masked, axis=(1, 3))
    window_index = (
        jnp.arange(tile_rows, dtype=jnp.int32)[:, None] + tile_offsets + REACH * tile_rows
    )
    below = []
    above = []
    for hop in range(1, REACH + 1):
        below.append(passed_along(features, "nodes", hop))
        above.append(passed_along(features, "nodes", -hop))
    window = jnp.concatenate(below[::-1] + [features] + above, axis=0).reshape(
        -1, tile_size, feat_width
    )
    own_rows = features.reshape(tile_rows, tile_size, feat_width)
    gathered_sum = jnp.zeros_like(own_rows)
    for slot in range(slot_total):
        gathered_sum = gathered_sum + jnp.einsum(
            "tij,tjf->tif", masked[:, slot], window[window_index[:, slot]], precision=highest
        )
    mixed = ((gathered_sum + own_rows) / degree[:, :, None]).reshape(row_total, feat_width)
    partial_value = jnp.dot(mixed, weight, precision=highest, preferred_element_type=jnp.float32)
    pre = lax.psum(partial_value, "years") + bias
    sigma = jax.nn.sigmoid(pre)
    output = pre * sigma
    grad_pre = grad_out * sigma * (1.0 + pre * (1.0 - sigma))
    grad_weight, grad_bias = lax.psum(
        (
            jnp.dot(mixed.T, grad_pre, precision=highest, preferred_element_type=jnp.float32),
            jnp.sum(grad_pre, axis=0),
        ),
        "nodes",
    )
    col_width = grad_pre.shape[1]
    scaled = grad_pre.reshape(tile_rows, tile_size, col_width) / degree[:, :, None]
    back_window = jnp.zeros(((2 * REACH + 1) * tile_rows, tile_size, col_width), jnp.float32)
    for slot in range(slot_total):
        contrib = jnp.einsum("tij,tif->tjf", masked[:, slot], scaled, precision=highest)
        back_window = back_window.at[window_index[:, slot]].add(contrib)
    pieces = back_window.reshape(2 * REACH + 1, row_total, col_width)
    total = pieces[REACH] + scaled.reshape(row_total, col_width)
    for hop in range(1, REACH + 1):
        total = total + passed_along(pieces[REACH + hop], "nodes", hop)
        total = total + passed_along(pieces[REACH - hop], "nodes", -hop)
    grad_features = jnp.dot(total, weight.T, precision=highest, preferred_element_type=jnp.float32)
    return (output, grad_features, grad_weight, grad_bias)


def solution(mesh):
    placed = (
        P("nodes", "years"),
        P("years", None),
        P(),
        P("nodes", None, None, None),
        P("nodes", None),
        P("nodes"),
        P("nodes", None),
    )
    return jax.shard_map(
        body,
        mesh=mesh,
        in_specs=placed,
        out_specs=(P("nodes", None), P("nodes", "years"), P("years", None), P()),
        check_vma=False,
    )
```

profile of v0, /device:TPU:64, one launch (start us, length us, event | category | flops | bytes accessed | tf_op | source)
XLA Modules:
  0.0 1779.0 jit_solution(14453821735217232291)
XLA Ops:
  7.2 14.4 collective-permute-start
  21.6 5.8 collective-permute-start.1
  27.4 7.3 collective-permute-start.2
  34.7 4.9 collective-permute-start.3
  39.6 0.7 add_add_fusion
  40.3 0.7 fusion.20
  41.0 1.5 fusion.23
  42.5 0.2 fusion.16
  42.7 8.5 collective-permute-done
  51.3 0.7 constant_dynamic-update-slice_fusion.4
  52.0 14.4 collective-permute-done.1
  66.4 0.7 constant_dynamic-update-slice_fusion.3
  67.1 0.7 constant_dynamic-update-slice_fusion.2
  67.8 0.7 constant_dynamic-update-slice_fusion.1
  68.6 3.4 collective-permute-done.3
  71.9 0.7 constant_dynamic-update-slice_fusion
  72.7 1.9 gather_fusion.1
  74.6 1.9 gather_fusion.2
  76.4 0.4 fusion.11
  76.8 0.4 fusion.13
  77.2 1.9 gather_fusion.3
  79.1 0.4 fusion.15
  79.5 1.9 gather_fusion
  81.4 0.4 fusion.3
  81.9 1.9 fusion.25
  83.9 0.0 all-reduce.5.cloned.1.call-start
  83.9 73.4 %all-reduce.3.cloned.1.call-done = f32[512,512]{1,0:T(8,128)} async-done(((f32[512,512]{1,0:T(8,128)}), f32[512,512]{1,0:T(8,128)}) %all-reduce.3.cloned.1.call-update) | async-done | bytes 1048592 | tf_op jit(solution)/shard_map/psum | solution.py:45
  157.3 3.0 fusion.22
  160.3 2.2 fusion.9
  162.5 2.1 fusion.10
  164.6 2.2 fusion.12
  166.8 2.2 fusion.14
  169.0 3.0 broadcast_in_dim.2
  171.9 3.5 scatter_fusion
  175.5 3.1 scatter_fusion.1
  178.5 3.3 scatter_fusion.2
  181.9 3.0 scatter_fusion.3
  184.9 4.9 fusion.24
  189.8 9.4 collective-permute-start.4
  199.2 3.7 collective-permute-start.5
  202.9 5.3 collective-permute-start.6
  208.2 11.3 collective-permute-start.7
  219.4 1.5 fusion.27
  220.9 578.3 %psum.23 = f32[512]{0:T(512)} all-reduce(f32[512]{0:T(512)S(1)} %get-tuple-element.8), channel_id=1, replica_groups=mesh['nodes'=128,'years'=6] {'nodes'}, use_global_device_ids=true, to_apply=%region_8.0 | all-reduce | flops 512 | bytes 4096 | tf_op jit(solution)/shard_map/psum | solution.py:49
  799.2 2.5 fusion.7
  801.7 1.7 fusion.26
  803.4 967.0 %all-reduce.5.cloned.1.call-done = f32[128,512]{1,0:T(8,128)} async-done(((f32[128,512]{1,0:T(8,128)}), f32[128,512]{1,0:T(8,128)}) %all-reduce.5.cloned.1.call-update) | async-done | bytes 262160 | tf_op jit(solution)/shard_map/psum | solution.py:49
  1770.5 1.7 copy.32
  (21 shorter events, 0.1 us)
Async XLA Ops:
  7.2 74.7 %copy-start = (f32[128,512]{1,0:T(8,128)S(1)}, f32[128,512]{1,0:T(8,128)}, u32[]{:S(2)}) copy-start(f32[128,512]{1,0:T(8,128)} %param.8) | copy-start | bytes 786436
  7.2 150.1 %all-reduce.3.cloned.1.call-start = ((), (), s32[]{:S(2)}) async-start(), calls=%async_computation | async-start | bytes 2097152 | tf_op jit(solution)/shard_map/psum | solution.py:45
  7.2 44.0 %collective-permute-start = (f32[512,128]{1,0:T(8,128)}, f32[512,128]{1,0:T(8,128)S(1)}, u32[]{:S(2)}, u32[]{:S(2)}) collective-permute-start(f32[512,128]{1,0:T(8,128)} %param.7), channel_id=1, source_target_pairs={{756,0},{762,6},{0,12},{6,18},{12,24},{18,30},{24,36},{30,42},{36,... | collective-permute-start | bytes 786440 | tf_op jit(solution)/shard_map/ppermute | solution.py:12
  21.6 44.8 %collective-permute-start.1 = (f32[512,128]{1,0:T(8,128)}, f32[512,128]{1,0:T(8,128)S(1)}, u32[]{:S(2)}, u32[]{:S(2)}) collective-permute-start(f32[512,128]{1,0:T(8,128)} %param.7), channel_id=1, source_target_pairs={{762,0},{0,6},{6,12},{12,18},{18,24},{24,30},{30,36},{36,42},{42,4... | collective-permute-start | bytes 786440 | tf_op jit(solution)/shard_map/ppermute | solution.py:12
  27.4 40.4 %collective-permute-start.2 = (f32[512,128]{1,0:T(8,128)}, f32[512,128]{1,0:T(8,128)S(1)}, u32[]{:S(2)}, u32[]{:S(2)}) collective-permute-start(f32[512,128]{1,0:T(8,128)} %param.7), channel_id=1, source_target_pairs={{6,0},{12,6},{18,12},{24,18},{30,24},{36,30},{42,36},{48,42},{54,4... | collective-permute-start | bytes 786440 | tf_op jit(solution)/shard_map/ppermute | solution.py:12
  34.7 37.2 %collective-permute-start.3 = (f32[512,128]{1,0:T(8,128)}, f32[512,128]{1,0:T(8,128)S(1)}, u32[]{:S(2)}, u32[]{:S(2)}) collective-permute-start(f32[512,128]{1,0:T(8,128)} %param.7), channel_id=1, source_target_pairs={{12,0},{18,6},{24,12},{30,18},{36,24},{42,30},{48,36},{54,42},{60,... | collective-permute-start | bytes 786440 | tf_op jit(solution)/shard_map/ppermute | solution.py:12
  41.0 26.1 %copy-start.3 = (f32[512,128]{1,0:T(8,128)S(1)}, f32[512,128]{1,0:T(8,128)}, u32[]{:S(2)}) copy-start(f32[512,128]{1,0:T(8,128)} %param.7) | copy-start | bytes 786436
  81.9 75.4 %copy-start.4 = (f32[512]{0:T(512)S(1)}, f32[512]{0:T(512)}, u32[]{:S(2)}) copy-start(f32[512]{0:T(512)} %param.9) | copy-start | bytes 6148
  83.9 1686.6 %all-reduce.5.cloned.1.call-start = ((), (), s32[]{:S(2)}) async-start(), calls=%async_computation.1 | async-start | bytes 524288 | tf_op jit(solution)/shard_map/psum | solution.py:49
  171.9 3.5 copy-start.2
  178.5 3.4 copy-start.1
  189.8 609.4 %collective-permute-start.4 = (f32[512,512]{1,0:T(8,128)}, f32[512,512]{1,0:T(8,128)}, u32[]{:S(2)}, u32[]{:S(2)}) collective-permute-start(f32[512,512]{1,0:T(8,128)} %bitcast.10), channel_id=1, source_target_pairs={{762,0},{0,6},{6,12},{12,18},{18,24},{24,30},{30,36},{36,42},{42,4... | collective-permute-start | bytes 3145736 | tf_op jit(solution)/shard_map/ppermute | solution.py:12
  199.2 600.0 %collective-permute-start.5 = (f32[512,512]{1,0:T(8,128)}, f32[512,512]{1,0:T(8,128)}, u32[]{:S(2)}, u32[]{:S(2)}) collective-permute-start(f32[512,512]{1,0:T(8,128)} %bitcast.11), channel_id=1, source_target_pairs={{6,0},{12,6},{18,12},{24,18},{30,24},{36,30},{42,36},{48,42},{54,4... | collective-permute-start | bytes 3145736 | tf_op jit(solution)/shard_map/ppermute | solution.py:12
  202.9 596.3 %collective-permute-start.6 = (f32[512,512]{1,0:T(8,128)}, f32[512,512]{1,0:T(8,128)}, u32[]{:S(2)}, u32[]{:S(2)}) collective-permute-start(f32[512,512]{1,0:T(8,128)} %bitcast.12), channel_id=1, source_target_pairs={{756,0},{762,6},{0,12},{6,18},{12,24},{18,30},{24,36},{30,42},{36,... | collective-permute-start | bytes 3145736 | tf_op jit(solution)/shard_map/ppermute | solution.py:12
  208.2 591.0 %collective-permute-start.7 = (f32[512,512]{1,0:T(8,128)}, f32[512,512]{1,0:T(8,128)}, u32[]{:S(2)}, u32[]{:S(2)}) collective-permute-start(f32[512,512]{1,0:T(8,128)} %bitcast.13), channel_id=1, source_target_pairs={{12,0},{18,6},{24,12},{30,18},{36,24},{42,30},{48,36},{54,42},{60,... | collective-permute-start | bytes 3145736 | tf_op jit(solution)/shard_map/ppermute | solution.py:12
Sparse Core Ops, SparseCore 0:
  84.0 73.2 all-reduce.2
  221.0 1549.3 all-reduce.4
where the time goes:
time: 1780 us
  waiting for transfers between devices  1070 us (60%)
  blocking collectives  578 us (32%)
  starting transfers between devices  62.1 us (3%)
  other arithmetic  21.6 us (1%)
  local copies, waits for them, and re-layouts  20.7 us (1%)
    psum x1, waiting for transfers between devices, body(): lax.psum((jnp.dot(mixed.T, grad_pre, precision=highest, preferred_element...  967 us
    psum x1, blocking collectives, body(): lax.psum((jnp.dot(mixed.T, grad_pre, precision=highest, preferred_element...  578 us
    psum x1, waiting for transfers between devices, body(): pre = lax.psum(partial_value, 'years') + bias  73.4 us
    ppermute x8, starting transfers between devices, passed_along(): return lax.ppermute(block, axis, route)  62 us
  transfers between devices with their start and end apart: 10, of which 5 were waited for; matrix products, arithmetic and copies ran while one was open for 1% of the time, Pallas kernels for 0%

commit v1 on v0

v1 whole, which is shorter than its diff:
```python
import jax
import jax.numpy as jnp
from jax import lax
from jax.experimental import pallas as pl
from jax.experimental.pallas import tpu as pltpu
from jax.sharding import Mesh, PartitionSpec as P

NODES = ("x", "y", "zh")
YEARS = ("zl", "c")
PLANE = ("x", "y")
REACH = 2
T = 128
F32 = jnp.float32
BF = jnp.bfloat16
VMEM = pl.BlockSpec(memory_space=pltpu.VMEM)
SMEM = pl.BlockSpec(memory_space=pltpu.SMEM)


def shape_of(shape, dtype=F32):
    return jax.ShapeDtypeStruct(shape, dtype)


def call(kernel, ins, outs, scratch, flops, bytes_accessed, name):
    return pl.pallas_call(
        kernel,
        in_specs=ins,
        out_specs=[VMEM] * len(outs),
        out_shape=outs,
        scratch_shapes=scratch,
        name=name,
        cost_estimate=pl.CostEstimate(
            flops=flops, bytes_accessed=bytes_accessed, transcendentals=0
        ),
        compiler_params=pltpu.CompilerParams(vmem_limit_bytes=40 * 1024 * 1024),
    )


def split(v):
    hi = v.astype(BF)
    lo = (v - hi.astype(F32)).astype(BF)
    return hi, lo


def dot(a, b):
    return lax.dot_general(a, b, (((1,), (0,)), ((), ())), preferred_element_type=F32)


def prepare_kernel(count, tiles, weight, a_hi, a_lo, t_hi, t_lo, rdeg, wt):
    for t in range(tiles.shape[0]):
        total = jnp.zeros((T, T), F32)
        for s in range(tiles.shape[1]):
            live = jnp.where(s < count[t], 1.0, 0.0).astype(F32)
            a = tiles[t, s] * live
            total = total + a
            cols = slice(s * T, (s + 1) * T)
            hi, lo = split(a)
            a_hi[t, :, cols] = hi
            a_lo[t, :, cols] = lo
            hi, lo = split(a.T)
            t_hi[t, cols, :] = hi
            t_lo[t, cols, :] = lo
        degree = 1.0 + jnp.sum(total, axis=1, keepdims=True)
        rdeg[t * T : (t + 1) * T, :] = jnp.broadcast_to(1.0 / degree, (T, T))
    for k in range(weight.shape[1] // T):
        hi, lo = split(weight[:, k * T : (k + 1) * T].T)
        wt[k * T : (k + 1) * T, :T] = hi
        wt[k * T : (k + 1) * T, T:] = lo


def mix_kernel(index, m2, m1, own, p1, p2, a_hi, a_lo, rdeg, mixed, window):
    rows = own.shape[0]
    for q, ref in enumerate((m2, m1, own, p1, p2)):
        hi, lo = split(ref[...])
        window[q * rows : (q + 1) * rows, :T] = hi
        window[q * rows : (q + 1) * rows, T:] = lo
    for t in range(a_hi.shape[0]):
        picked = []
        for s in range(4):
            at = pl.multiple_of(index[t * 4 + s] * T, T)
            picked.append(window[pl.ds(at, T), :])
        b = jnp.concatenate(picked, axis=0)
        wide = dot(a_hi[t], b)
        total = wide[:, :T] + wide[:, T:] + dot(a_lo[t], b[:, :T])
        r = slice(t * T, (t + 1) * T)
        mixed[r, :] = (total + own[r, :]) * rdeg[r, :]


def layer_kernel(
    index, slot, x0, x1, x2, y, w0, w1, w2, v, bias, gout, rdeg, t_hi, t_lo, wt,
    output, gpre, q0, q1, q2, q3, q4, m_hi, m_lo, w_hi, w_lo, back,
):
    rows = gout.shape[0]
    for k in range(6):
        m = (x0, x1, x2)[k][...] if k < 3 else y[(k - 3) * rows : (k - 2) * rows, :]
        w = (w0, w1, w2)[k][...] if k < 3 else v[(k - 3) * T : (k - 2) * T, :]
        hi, lo = split(m)
        m_hi[slot[k]] = hi
        m_lo[slot[k]] = lo
        hi, lo = split(w)
        w_hi[pl.ds(pl.multiple_of(slot[k] * T, T), T), :] = hi
        w_lo[pl.ds(pl.multiple_of(slot[k] * T, T), T), :] = lo
    back[...] = jnp.zeros_like(back)
    wth = wt[:, :T]
    for t in range(rows // T):
        r = slice(t * T, (t + 1) * T)
        mh = jnp.concatenate([m_hi[k, r, :] for k in range(6)], axis=1)
        ml = jnp.concatenate([m_lo[k, r, :] for k in range(6)], axis=1)
        pre = dot(mh, w_hi[...]) + dot(mh, w_lo[...]) + dot(ml, w_hi[...]) + bias[...]
        sigma = 1.0 / (1.0 + jnp.exp(-pre))
        output[r, :] = pre * sigma
        g = gout[r, :] * sigma * (1.0 + pre * (1.0 - sigma))
        gpre[r, :] = g
        scale = rdeg[r, :]
        scaled = g * jnp.concatenate([scale] * 4, axis=1)
        sh, sl = split(scaled)
        wide = dot(sh, wt[...])
        z = wide[:, :T] + wide[:, T:] + dot(sl, wth)
        zh, zl = split(z)
        wide = dot(t_hi[t], jnp.concatenate([zh, zl], axis=1))
        contrib = wide[:, :T] + wide[:, T:] + dot(t_lo[t], zh)
        back[REACH * rows + t * T : REACH * rows + (t + 1) * T, :] += z
        for s in range(4):
            at = pl.multiple_of(index[t * 4 + s] * T, T)
            back[pl.ds(at, T), :] += contrib[s * T : (s + 1) * T, :]
    for q, ref in enumerate((q0, q1, q2, q3, q4)):
        ref[...] = back[q * rows : (q + 1) * rows, :]


def weight_kernel(mixed, gpre, pieces):
    rows = mixed.shape[0]
    m = jnp.concatenate([mixed[t * T : (t + 1) * T, :].T for t in range(rows // T)], axis=1)
    mh, ml = split(m)
    for k in range(4):
        g = gpre[:, k * T : (k + 1) * T]
        gh, gl = split(g)
        wide = dot(mh, jnp.concatenate([gh, gl], axis=1))
        total = wide[:, :T] + wide[:, T:] + dot(ml, gh)
        for b in range(8):
            pieces[b * 4 + k, 0:16, :] = total[b * 16 : (b + 1) * 16, :]
        line = jnp.sum(g, axis=0, keepdims=True)
        for p in range(32):
            pieces[p, 16 + k : 17 + k, :] = line
    for p in range(32):
        pieces[p, 20:24, :] = jnp.zeros((4, T), F32)


def passed_along(block, axis, distance):
    devices = range(lax.axis_size(axis))
    route = [((i - distance) % len(devices), i) for i in devices]
    return lax.ppermute(block, axis, route)


def body(features, weight, bias, tile_weights, tile_offsets, tile_counts, grad_out):
    rows, width = features.shape
    tiles = tile_weights.shape[0]
    index = jnp.arange(tiles, dtype=jnp.int32)[:, None] + tile_offsets + REACH * tiles
    index = jnp.clip(index, 0, (2 * REACH + 1) * tiles - 1).reshape(-1)
    zl = lax.axis_index("zl")
    c = lax.axis_index("c")
    place = [((zl - d) % 3) * 2 + c for d in range(3)]
    place += [((zl - d) % 3) * 2 + 1 - c for d in range(3)]
    slot = jnp.stack(place).astype(jnp.int32)

    with jax.named_scope("halo"):
        from_below = passed_along(features, NODES, 1)
        from_above = passed_along(features, NODES, -1)
        from_below2 = passed_along(from_below, NODES, 1)
        from_above2 = passed_along(from_above, NODES, -1)
    with jax.named_scope("weight_gather"):
        w1 = passed_along(weight, "zl", 1)
        w2 = passed_along(weight, "zl", 2)
        v = passed_along(jnp.concatenate([weight, w1, w2], axis=0), "c", 1)

    a_hi, a_lo, t_hi, t_lo, rdeg, wt = call(
        prepare_kernel,
        [SMEM, VMEM, VMEM],
        [
            shape_of((tiles, T, 4 * T), BF),
            shape_of((tiles, T, 4 * T), BF),
            shape_of((tiles, 4 * T, T), BF),
            shape_of((tiles, 4 * T, T), BF),
            shape_of((rows, T)),
            shape_of((4 * T, 2 * T), BF),
        ],
        [],
        10**6,
        4 * 10**6,
        "prepare",
    )(tile_counts, tile_weights, weight)
    (mixed,) = call(
        mix_kernel,
        [SMEM] + [VMEM] * 8,
        [shape_of((rows, width))],
        [pltpu.VMEM((5 * rows, 2 * T), BF)],
        2 * 10**8,
        3 * 10**6,
        "mix",
    )(index, from_below2, from_below, features, from_above, from_above2, a_hi, a_lo, rdeg)
    with jax.named_scope("mixed_gather"):
        x1 = passed_along(mixed, "zl", 1)
        x2 = passed_along(mixed, "zl", 2)
        y = passed_along(jnp.concatenate([mixed, x1, x2], axis=0), "c", 1)
    piece = shape_of((rows, width))
    output, gpre, q0, q1, q2, q3, q4 = call(
        layer_kernel,
        [SMEM] * 2 + [VMEM] * 14,
        [shape_of((rows, 4 * T)), shape_of((rows, 4 * T))] + [piece] * 5,
        [
            pltpu.VMEM((6, rows, T), BF),
            pltpu.VMEM((6, rows, T), BF),
            pltpu.VMEM((6 * T, 4 * T), BF),
            pltpu.VMEM((6 * T, 4 * T), BF),
            pltpu.VMEM((5 * rows, T), F32),
        ],
        15 * 10**8,
        10**7,
        "layer",
    )(
        index, slot, mixed, x1, x2, y, weight, w1, w2, v, bias.reshape(1, -1), grad_out, rdeg,
        t_hi, t_lo, wt,
    )
    with jax.named_scope("back_halo"):
        up = passed_along(q4, NODES, 1)
        down = passed_along(q0, NODES, -1)
    (pieces,) = call(
        weight_kernel,
        [VMEM] * 2,
        [shape_of((32, 24, T))],
        [],
        2 * 10**8,
        2 * 10**6,
        "weight_grad",
    )(mixed, gpre)
    with jax.named_scope("nodes_sum"):
        held = jnp.sum(lax.all_to_all(pieces, PLANE, 0, 0), axis=0)
    with jax.named_scope("back_halo"):
        up = passed_along(q3 + up, NODES, 1)
        down = passed_along(q1 + down, NODES, -1)
    with jax.named_scope("nodes_sum"):
        held = jnp.broadcast_to(held[None], (4, 24, T))
        held = jnp.sum(lax.all_to_all(held, "zh", 0, 0), axis=0)
        grad_bias = held[16:20].reshape(-1)
        whole = jnp.broadcast_to(held[None, :16], (32, 16, T))
        whole = lax.all_to_all(whole, PLANE, 0, 0)
        grad_weight = whole.reshape(8, 4, 16, T).transpose(0, 2, 1, 3).reshape(T, 4 * T)
    grad_features = q2 + up + down
    return output, grad_features, grad_weight, grad_bias


def solution(mesh):
    fine = Mesh(mesh.devices.reshape(4, 8, 4, 3, 2), NODES + YEARS)
    placed = (
        P(NODES, YEARS),
        P(YEARS, None),
        P(),
        P(NODES, None, None, None),
        P(NODES, None),
        P(NODES),
        P(NODES, None),
    )
    return jax.shard_map(
        body,
        mesh=fine,
        in_specs=placed,
        out_specs=(P(NODES, None), P(NODES, YEARS), P(YEARS, None), P()),
        check_vma=False,
    )
```

time: 1780 us -> 187 us (0.11)
  the two profiles are of different devices: /device:TPU:64 before, /device:TPU:72 now
where the time goes in v1:
time: 187 us; the launch traced here: 186 us
  starting transfers between devices  86.6 us (46%)
  waiting for transfers between devices  59.2 us (32%)
  blocking collectives  13.3 us (7%)
  local copies, waits for them, and re-layouts  12.7 us (7%)
  Pallas kernels  9.67 us (5%)
  other arithmetic  3.43 us (2%)
    ppermute x14, starting transfers between devices, passed_along(): return lax.ppermute(block, axis, route)  60.5 us
    ppermute x14, waiting for transfers between devices, passed_along(): return lax.ppermute(block, axis, route)  49.6 us
    all_to_all x1, starting transfers between devices, body(): whole = lax.all_to_all(whole, PLANE, 0, 0)  17.1 us
    all_to_all x1, blocking collectives, body(): held = jnp.sum(lax.all_to_all(held, 'zh', 0, 0), axis=0)  13.3 us
    unnamed x43, local copies, waits for them, and re-layouts  11.2 us
    all_to_all x1, waiting for transfers between devices, body(): whole = lax.all_to_all(whole, PLANE, 0, 0)  9.63 us
    all_to_all x1, starting transfers between devices, body(): held = jnp.sum(lax.all_to_all(pieces, PLANE, 0, 0), axis=0)  9.01 us
    pallas_call x1, Pallas kernels, body(): call(layer_kernel, [SMEM] * 2 + [VMEM] * 14, [shape_of((rows, 4 * T)), sh...  5.84 us
  transfers between devices with their start and end apart: 16, of which 7 were waited for; matrix products, arithmetic and copies ran while one was open for 3% of the time, Pallas kernels for 1%

profile of v1, /device:TPU:72, one launch (start us, length us, event | category | flops | bytes accessed | tf_op | source)
XLA Modules:
  0.0 185.9 jit_solution(8066805726990307164)
XLA Ops:
  0.6 9.1 %collective-permute-start = (f32[512,128]{1,0:T(8,128)}, f32[512,128]{1,0:T(8,128)S(1)}, u32[]{:S(2)}, u32[]{:S(2)}) collective-permute-start(f32[512,128]{1,0:T(8,128)} %own.1), channel_id=1, source_target_pairs={{762,0},{0,6},{6,12},{12,18},{18,24},{24,30},{30,36},{36,42},{42,4... | collective-permute-start | bytes 786440 | tf_op jit(solution)/shard_map/halo/ppermute | solution.py:150
  9.7 6.4 %collective-permute-start.2 = (f32[512,128]{1,0:T(8,128)}, f32[512,128]{1,0:T(8,128)S(1)}, u32[]{:S(2)}, u32[]{:S(2)}) collective-permute-start(f32[512,128]{1,0:T(8,128)} %own.1), channel_id=1, source_target_pairs={{6,0},{12,6},{18,12},{24,18},{30,24},{36,30},{42,36},{48,42},{54,4... | collective-permute-start | bytes 786440 | tf_op jit(solution)/shard_map/halo/ppermute | solution.py:150
  16.1 15.9 %collective-permute-done.m1 = f32[512,128]{1,0:T(8,128)S(1)} collective-permute-done((f32[512,128]{1,0:T(8,128)}, f32[512,128]{1,0:T(8,128)S(1)}, u32[]{:S(2)}, u32[]{:S(2)}) %collective-permute-start) | collective-permute-done | bytes 262176 | tf_op jit(solution)/shard_map/halo/ppermute | solution.py:150
  32.0 1.9 %collective-permute-start.1 = (f32[512,128]{1,0:T(8,128)S(1)}, f32[512,128]{1,0:T(8,128)S(1)}, u32[]{:S(2)}, u32[]{:S(2)}) collective-permute-start(f32[512,128]{1,0:T(8,128)S(1)} %collective-permute-done.m1), channel_id=1, source_target_pairs={{762,0},{0,6},{6,12},{12,18},{18,24},{24,30},{30,36},{36,42},{42,4... | collective-permute-start | bytes 786440 | tf_op jit(solution)/shard_map/halo/ppermute | solution.py:150
  34.0 7.8 %collective-permute-start.3 = (f32[512,128]{1,0:T(8,128)S(1)}, f32[512,128]{1,0:T(8,128)S(1)}, u32[]{:S(2)}, u32[]{:S(2)}) collective-permute-start(f32[512,128]{1,0:T(8,128)S(1)} %collective-permute-done.2.p1), channel_id=1, source_target_pairs={{6,0},{12,6},{18,12},{24,18},{30,24},{36,30},{42,36},{48,42},{54,4... | collective-permute-start | bytes 786440 | tf_op jit(solution)/shard_map/halo/ppermute | solution.py:150
  41.8 2.2 %collective-permute-start.8 = (f32[128,512]{1,0:T(8,128)}, f32[128,512]{1,0:T(8,128)S(1)}, u32[]{:S(2)}, u32[]{:S(2)}) collective-permute-start(f32[128,512]{1,0:T(8,128)} %w0.1), channel_id=1, source_target_pairs={{2,0},{4,2},{0,4},{3,1},{5,3},{1,5},{8,6},{10,8},{6,10},{9,7},{11,... | collective-permute-start | bytes 786440 | tf_op jit(solution)/shard_map/weight_gather/ppermute | solution.py:150
  44.1 3.6 %collective-permute-start.7 = (f32[128,512]{1,0:T(8,128)}, f32[128,512]{1,0:T(8,128)S(1)}, u32[]{:S(2)}, u32[]{:S(2)}) collective-permute-start(f32[128,512]{1,0:T(8,128)} %w0.1), channel_id=1, source_target_pairs={{4,0},{0,2},{2,4},{5,1},{1,3},{3,5},{10,6},{6,8},{8,10},{11,7},{7,... | collective-permute-start | bytes 786440 | tf_op jit(solution)/shard_map/weight_gather/ppermute | solution.py:150
  47.7 0.7 add_clamp_fusion
  48.5 0.6 copy-done.16
  49.0 0.9 copy-done
  50.0 1.2 copy-done.2
  51.2 1.2 prepare.1
  52.4 0.8 copy-done.4
  53.2 0.7 copy-done.7
  53.9 7.6 %collective-permute-done.1.m2 = f32[512,128]{1,0:T(8,128)S(1)} collective-permute-done((f32[512,128]{1,0:T(8,128)S(1)}, f32[512,128]{1,0:T(8,128)S(1)}, u32[]{:S(2)}, u32[]{:S(2)}) %collective-permute-start.1) | collective-permute-done | bytes 262176 | tf_op jit(solution)/shard_map/halo/ppermute | solution.py:150
  61.5 1.3 mix.1.x0.mixed
  62.9 1.9 %collective-permute-start.5 = (f32[512,128]{1,0:T(8,128)S(1)}, f32[512,128]{1,0:T(8,128)S(1)}, u32[]{:S(2)}, u32[]{:S(2)}) collective-permute-start(f32[512,128]{1,0:T(8,128)S(1)} %mix.1.x0.mixed), channel_id=1, source_target_pairs={{2,0},{4,2},{0,4},{3,1},{5,3},{1,5},{8,6},{10,8},{6,10},{9,7},{11,... | collective-permute-start | bytes 786440 | tf_op jit(solution)/shard_map/mixed_gather/ppermute | solution.py:150
  64.8 3.9 %collective-permute-start.4 = (f32[512,128]{1,0:T(8,128)S(1)}, f32[512,128]{1,0:T(8,128)S(1)}, u32[]{:S(2)}, u32[]{:S(2)}) collective-permute-start(f32[512,128]{1,0:T(8,128)S(1)} %mix.1.x0.mixed), channel_id=1, source_target_pairs={{4,0},{0,2},{2,4},{5,1},{1,3},{3,5},{10,6},{6,8},{8,10},{11,7},{7,... | collective-permute-start | bytes 786440 | tf_op jit(solution)/shard_map/mixed_gather/ppermute | solution.py:150
  68.7 1.0 collective-permute-done.8.w2
  69.7 1.0 pad_maximum_fusion.1
  70.7 2.0 %collective-permute-start.9 = (f32[384,512]{1,0:T(8,128)}, f32[384,512]{1,0:T(8,128)}, u32[]{:S(2)}, u32[]{:S(2)}) collective-permute-start(f32[384,512]{1,0:T(8,128)} %pad_maximum_fusion.1), channel_id=1, source_target_pairs={{1,0},{0,1},{3,2},{2,3},{5,4},{4,5},{7,6},{6,7},{9,8},{8,9},{11,10... | collective-permute-start | bytes 2359304 | tf_op jit(solution)/shard_map/weight_gather/ppermute | solution.py:150
  72.7 7.2 %collective-permute-done.5.x2 = f32[512,128]{1,0:T(8,128)S(1)} collective-permute-done((f32[512,128]{1,0:T(8,128)S(1)}, f32[512,128]{1,0:T(8,128)S(1)}, u32[]{:S(2)}, u32[]{:S(2)}) %collective-permute-start.5) | collective-permute-done | bytes 262176 | tf_op jit(solution)/shard_map/mixed_gather/ppermute | solution.py:150
  79.9 0.9 pad_maximum_fusion
  80.9 1.9 %collective-permute-start.6 = (f32[1536,128]{1,0:T(8,128)}, f32[1536,128]{1,0:T(8,128)}, u32[]{:S(2)}, u32[]{:S(2)}) collective-permute-start(f32[1536,128]{1,0:T(8,128)} %pad_maximum_fusion), channel_id=1, source_target_pairs={{1,0},{0,1},{3,2},{2,3},{5,4},{4,5},{7,6},{6,7},{9,8},{8,9},{11,10... | collective-permute-start | bytes 2359304 | tf_op jit(solution)/shard_map/mixed_gather/ppermute | solution.py:150
  82.9 2.4 %collective-permute-done.6.y = f32[1536,128]{1,0:T(8,128)} collective-permute-done((f32[1536,128]{1,0:T(8,128)}, f32[1536,128]{1,0:T(8,128)}, u32[]{:S(2)}, u32[]{:S(2)}) %collective-permute-start.6) | collective-permute-done | bytes 786464 | tf_op jit(solution)/shard_map/mixed_gather/ppermute | solution.py:150
  85.4 0.7 copy-done.15
  86.1 1.0 copy-done.5
  87.1 0.9 copy-done.8
  88.1 5.8 %layer.1 = (f32[512,512]{1,0:T(8,128)}, f32[512,512]{1,0:T(8,128)S(1)}, f32[512,128]{1,0:T(8,128)S(1)}, f32[512,128]{1,0:T(8,128)S(1)}, f32[512,128]{1,0:T(8,128...) custom-call(s32[16]{0:T(128)S(1)} %reshape.25.index, s32[6]{0:T(128)S(1)} %stack.27.slot, ...), custom_call_target="tpu_custom_call" | custom-call | flops 1500000000 | bytes 10000000 | tf_op jit(solution)/shard_map/layer/pallas_call | solution.py:204
  93.9 0.7 copy-done.9
  94.6 0.7 copy-done.11
  95.3 0.7 copy-done.13
  96.0 0.7 copy-done.17
  96.7 0.7 copy-done.19
  97.4 1.3 weight_grad.1
  98.7 9.0 %all-to-all-start = ((f32[32,24,128]{2,1,0:T(8,128)}), f32[32,24,128]{2,1,0:T(8,128)S(1)}, u32[]{:S(2)}, u32[]{:S(2)}) async-start(f32[32,24,128]{2,1,0:T(8,128)} %weight_grad.1), calls=%async_computation | async-start | bytes 786432 | tf_op jit(solution)/shard_map/nodes_sum/all_to_all | solution.py:235
  107.7 1.9 %collective-permute-start.10 = (f32[512,128]{1,0:T(8,128)S(1)}, f32[512,128]{1,0:T(8,128)S(1)}, u32[]{:S(2)}, u32[]{:S(2)}) collective-permute-start(f32[512,128]{1,0:T(8,128)S(1)} %copy-done.20), channel_id=1, source_target_pairs={{762,0},{0,6},{6,12},{12,18},{18,24},{24,30},{30,36},{36,42},{42,4... | collective-permute-start | bytes 786440 | tf_op jit(solution)/shard_map/back_halo/ppermute | solution.py:150
  109.7 7.8 %collective-permute-start.12 = (f32[512,128]{1,0:T(8,128)S(1)}, f32[512,128]{1,0:T(8,128)S(1)}, u32[]{:S(2)}, u32[]{:S(2)}) collective-permute-start(f32[512,128]{1,0:T(8,128)S(1)} %copy-done.18), channel_id=1, source_target_pairs={{6,0},{12,6},{18,12},{24,18},{30,24},{36,30},{42,36},{48,42},{54,4... | collective-permute-start | bytes 786440 | tf_op jit(solution)/shard_map/back_halo/ppermute | solution.py:150
  117.5 15.4 %collective-permute-done.10 = f32[512,128]{1,0:T(8,128)S(1)} collective-permute-done((f32[512,128]{1,0:T(8,128)S(1)}, f32[512,128]{1,0:T(8,128)S(1)}, u32[]{:S(2)}, u32[]{:S(2)}) %collective-permute-start.10) | collective-permute-done | bytes 262176 | tf_op jit(solution)/shard_map/back_halo/ppermute | solution.py:150
  132.9 2.1 %collective-permute-start.11 = (f32[512,128]{1,0:T(8,128)S(1)}, f32[512,128]{1,0:T(8,128)S(1)}, u32[]{:S(2)}, u32[]{:S(2)}) collective-permute-start(f32[512,128]{1,0:T(8,128)S(1)} %add.68), channel_id=1, source_target_pairs={{762,0},{0,6},{6,12},{12,18},{18,24},{24,30},{30,36},{36,42},{42,4... | collective-permute-start | bytes 786440 | tf_op jit(solution)/shard_map/back_halo/ppermute | solution.py:150
  135.0 7.8 %collective-permute-start.13 = (f32[512,128]{1,0:T(8,128)S(1)}, f32[512,128]{1,0:T(8,128)S(1)}, u32[]{:S(2)}, u32[]{:S(2)}) collective-permute-start(f32[512,128]{1,0:T(8,128)S(1)} %add.70), channel_id=1, source_target_pairs={{6,0},{12,6},{18,12},{24,18},{30,24},{36,30},{42,36},{48,42},{54,4... | collective-permute-start | bytes 786440 | tf_op jit(solution)/shard_map/back_halo/ppermute | solution.py:150
  142.9 13.3 %all_to_all.15 = f32[4,24,128]{2,1,0:T(8,128)S(1)} all-to-all(f32[4,24,128]{2,1,0:T(8,128)S(1)} %broadcast_in_dim.4), channel_id=1, replica_groups=mesh['x'=4,'y'=8,'zh'=4,'zl'=3,'c'=2] {'zh'}, dimensions={0} | all-to-all | bytes 98304 | tf_op jit(solution)/shard_map/nodes_sum/all_to_all | solution.py:241
  156.3 0.7 broadcast_in_dim.5
  157.0 17.1 %all-to-all-start.2 = ((f32[32,16,128]{2,1,0:T(8,128)}), f32[32,16,128]{2,1,0:T(8,128)S(1)}, u32[]{:S(2)}, u32[]{:S(2)}) async-start(f32[32,16,128]{2,1,0:T(8,128)} %broadcast_in_dim.5), calls=%async_computation.2 | async-start | bytes 524288 | tf_op jit(solution)/shard_map/nodes_sum/all_to_all | solution.py:244
  174.1 0.7 add_add_fusion
  174.8 0.6 slice_bitcast_fusion
  175.4 9.6 %all-to-all-done.2 = f32[32,16,128]{2,1,0:T(8,128)S(1)} async-done(((f32[32,16,128]{2,1,0:T(8,128)}), f32[32,16,128]{2,1,0:T(8,128)S(1)}, u32[]{:S(2)}, u32[]{:S(2)}) %all-to-all-start.2) | async-done | bytes 262176 | tf_op jit(solution)/shard_map/nodes_sum/all_to_all | solution.py:244
  185.2 0.7 copy.15
  (47 shorter events, 0.5 us)
Async XLA Ops:
  0.6 31.4 %collective-permute-start = (f32[512,128]{1,0:T(8,128)}, f32[512,128]{1,0:T(8,128)S(1)}, u32[]{:S(2)}, u32[]{:S(2)}) collective-permute-start(f32[512,128]{1,0:T(8,128)} %own.1), channel_id=1, source_target_pairs={{762,0},{0,6},{6,12},{12,18},{18,24},{24,30},{30,36},{36,42},{42,4... | collective-permute-start | bytes 786440 | tf_op jit(solution)/shard_map/halo/ppermute | solution.py:150
  9.7 24.2 %collective-permute-start.2 = (f32[512,128]{1,0:T(8,128)}, f32[512,128]{1,0:T(8,128)S(1)}, u32[]{:S(2)}, u32[]{:S(2)}) collective-permute-start(f32[512,128]{1,0:T(8,128)} %own.1), channel_id=1, source_target_pairs={{6,0},{12,6},{18,12},{24,18},{30,24},{36,30},{42,36},{48,42},{54,4... | collective-permute-start | bytes 786440 | tf_op jit(solution)/shard_map/halo/ppermute | solution.py:150
  32.0 29.5 %collective-permute-start.1 = (f32[512,128]{1,0:T(8,128)S(1)}, f32[512,128]{1,0:T(8,128)S(1)}, u32[]{:S(2)}, u32[]{:S(2)}) collective-permute-start(f32[512,128]{1,0:T(8,128)S(1)} %collective-permute-done.m1), channel_id=1, source_target_pairs={{762,0},{0,6},{6,12},{12,18},{18,24},{24,30},{30,36},{36,42},{42,4... | collective-permute-start | bytes 786440 | tf_op jit(solution)/shard_map/halo/ppermute | solution.py:150
  34.0 27.6 %collective-permute-start.3 = (f32[512,128]{1,0:T(8,128)S(1)}, f32[512,128]{1,0:T(8,128)S(1)}, u32[]{:S(2)}, u32[]{:S(2)}) collective-permute-start(f32[512,128]{1,0:T(8,128)S(1)} %collective-permute-done.2.p1), channel_id=1, source_target_pairs={{6,0},{12,6},{18,12},{24,18},{30,24},{36,30},{42,36},{48,42},{54,4... | collective-permute-start | bytes 786440 | tf_op jit(solution)/shard_map/halo/ppermute | solution.py:150
  41.8 27.9 %collective-permute-start.8 = (f32[128,512]{1,0:T(8,128)}, f32[128,512]{1,0:T(8,128)S(1)}, u32[]{:S(2)}, u32[]{:S(2)}) collective-permute-start(f32[128,512]{1,0:T(8,128)} %w0.1), channel_id=1, source_target_pairs={{2,0},{4,2},{0,4},{3,1},{5,3},{1,5},{8,6},{10,8},{6,10},{9,7},{11,... | collective-permute-start | bytes 786440 | tf_op jit(solution)/shard_map/weight_gather/ppermute | solution.py:150
  44.1 25.6 %collective-permute-start.7 = (f32[128,512]{1,0:T(8,128)}, f32[128,512]{1,0:T(8,128)S(1)}, u32[]{:S(2)}, u32[]{:S(2)}) collective-permute-start(f32[128,512]{1,0:T(8,128)} %w0.1), channel_id=1, source_target_pairs={{4,0},{0,2},{2,4},{5,1},{1,3},{3,5},{10,6},{6,8},{8,10},{11,7},{7,... | collective-permute-start | bytes 786440 | tf_op jit(solution)/shard_map/weight_gather/ppermute | solution.py:150
  48.4 0.7 copy-start.16
  49.0 0.9 copy-start
  50.0 1.2 copy-start.2
  51.2 10.3 %copy-start.6 = (f32[512,128]{1,0:T(8,128)S(1)}, f32[512,128]{1,0:T(8,128)}, u32[]{:S(2)}) copy-start(f32[512,128]{1,0:T(8,128)} %own.1) | copy-start | bytes 786436
  52.4 0.8 copy-start.4
  53.2 0.7 copy-start.7
  61.5 8.2 %copy-start.1 = (f32[128,512]{1,0:T(8,128)S(1)}, f32[128,512]{1,0:T(8,128)}, u32[]{:S(2)}) copy-start(f32[128,512]{1,0:T(8,128)} %w0.1) | copy-start | bytes 786436
  62.9 17.1 %collective-permute-start.5 = (f32[512,128]{1,0:T(8,128)S(1)}, f32[512,128]{1,0:T(8,128)S(1)}, u32[]{:S(2)}, u32[]{:S(2)}) collective-permute-start(f32[512,128]{1,0:T(8,128)S(1)} %mix.1.x0.mixed), channel_id=1, source_target_pairs={{2,0},{4,2},{0,4},{3,1},{5,3},{1,5},{8,6},{10,8},{6,10},{9,7},{11,... | collective-permute-start | bytes 786440 | tf_op jit(solution)/shard_map/mixed_gather/ppermute | solution.py:150
  64.8 15.2 %collective-permute-start.4 = (f32[512,128]{1,0:T(8,128)S(1)}, f32[512,128]{1,0:T(8,128)S(1)}, u32[]{:S(2)}, u32[]{:S(2)}) collective-permute-start(f32[512,128]{1,0:T(8,128)S(1)} %mix.1.x0.mixed), channel_id=1, source_target_pairs={{4,0},{0,2},{2,4},{5,1},{1,3},{3,5},{10,6},{6,8},{8,10},{11,7},{7,... | collective-permute-start | bytes 786440 | tf_op jit(solution)/shard_map/mixed_gather/ppermute | solution.py:150
  70.7 14.7 %copy-start.3 = (f32[512,512]{1,0:T(8,128)S(1)}, f32[512,512]{1,0:T(8,128)}, u32[]{:S(2)}) copy-start(f32[512,512]{1,0:T(8,128)} %gout.1) | copy-start | bytes 3145732
  70.7 12.3 %collective-permute-start.9 = (f32[384,512]{1,0:T(8,128)}, f32[384,512]{1,0:T(8,128)}, u32[]{:S(2)}, u32[]{:S(2)}) collective-permute-start(f32[384,512]{1,0:T(8,128)} %pad_maximum_fusion.1), channel_id=1, source_target_pairs={{1,0},{0,1},{3,2},{2,3},{5,4},{4,5},{7,6},{6,7},{9,8},{8,9},{11,10... | collective-permute-start | bytes 2359304 | tf_op jit(solution)/shard_map/weight_gather/ppermute | solution.py:150
  80.9 4.5 %collective-permute-start.6 = (f32[1536,128]{1,0:T(8,128)}, f32[1536,128]{1,0:T(8,128)}, u32[]{:S(2)}, u32[]{:S(2)}) collective-permute-start(f32[1536,128]{1,0:T(8,128)} %pad_maximum_fusion), channel_id=1, source_target_pairs={{1,0},{0,1},{3,2},{2,3},{5,4},{4,5},{7,6},{6,7},{9,8},{8,9},{11,10... | collective-permute-start | bytes 2359304 | tf_op jit(solution)/shard_map/mixed_gather/ppermute | solution.py:150
  85.4 0.7 copy-start.15
  86.1 1.0 copy-start.5
  87.1 0.9 copy-start.8
  93.9 0.7 copy-start.9
  94.6 0.7 copy-start.11
  95.3 0.7 copy-start.13
  96.0 0.7 copy-start.17
  96.7 0.7 copy-start.19
  98.7 9.0 %copy-start.20 = (f32[512,128]{1,0:T(8,128)S(1)}, f32[512,128]{1,0:T(8,128)}, u32[]{:S(2)}) copy-start(f32[512,128]{1,0:T(8,128)} %copy-done.19) | copy-start | bytes 786436
  98.7 11.0 %copy-start.18 = (f32[512,128]{1,0:T(8,128)S(1)}, f32[512,128]{1,0:T(8,128)}, u32[]{:S(2)}) copy-start(f32[512,128]{1,0:T(8,128)} %copy-done.17) | copy-start | bytes 786436
  98.7 34.2 %copy-start.12 = (f32[512,128]{1,0:T(8,128)S(1)}, f32[512,128]{1,0:T(8,128)}, u32[]{:S(2)}) copy-start(f32[512,128]{1,0:T(8,128)} %copy-done.11) | copy-start | bytes 786436
  98.7 44.2 %all-to-all-start = ((f32[32,24,128]{2,1,0:T(8,128)}), f32[32,24,128]{2,1,0:T(8,128)S(1)}, u32[]{:S(2)}, u32[]{:S(2)}) async-start(f32[32,24,128]{2,1,0:T(8,128)} %weight_grad.1), calls=%async_computation | async-start | bytes 786432 | tf_op jit(solution)/shard_map/nodes_sum/all_to_all | solution.py:235
  107.7 25.1 %collective-permute-start.10 = (f32[512,128]{1,0:T(8,128)S(1)}, f32[512,128]{1,0:T(8,128)S(1)}, u32[]{:S(2)}, u32[]{:S(2)}) collective-permute-start(f32[512,128]{1,0:T(8,128)S(1)} %copy-done.20), channel_id=1, source_target_pairs={{762,0},{0,6},{6,12},{12,18},{18,24},{24,30},{30,36},{36,42},{42,4... | collective-permute-start | bytes 786440 | tf_op jit(solution)/shard_map/back_halo/ppermute | solution.py:150
  109.7 25.3 %collective-permute-start.12 = (f32[512,128]{1,0:T(8,128)S(1)}, f32[512,128]{1,0:T(8,128)S(1)}, u32[]{:S(2)}, u32[]{:S(2)}) collective-permute-start(f32[512,128]{1,0:T(8,128)S(1)} %copy-done.18), channel_id=1, source_target_pairs={{6,0},{12,6},{18,12},{24,18},{30,24},{36,30},{42,36},{48,42},{54,4... | collective-permute-start | bytes 786440 | tf_op jit(solution)/shard_map/back_halo/ppermute | solution.py:150
  132.9 2.1 %copy-start.10 = (f32[512,128]{1,0:T(8,128)S(1)}, f32[512,128]{1,0:T(8,128)}, u32[]{:S(2)}) copy-start(f32[512,128]{1,0:T(8,128)} %copy-done.9) | copy-start | bytes 786436
  132.9 41.2 %collective-permute-start.11 = (f32[512,128]{1,0:T(8,128)S(1)}, f32[512,128]{1,0:T(8,128)S(1)}, u32[]{:S(2)}, u32[]{:S(2)}) collective-permute-start(f32[512,128]{1,0:T(8,128)S(1)} %add.68), channel_id=1, source_target_pairs={{762,0},{0,6},{6,12},{12,18},{18,24},{24,30},{30,36},{36,42},{42,4... | collective-permute-start | bytes 786440 | tf_op jit(solution)/shard_map/back_halo/ppermute | solution.py:150
  135.0 39.1 %collective-permute-start.13 = (f32[512,128]{1,0:T(8,128)S(1)}, f32[512,128]{1,0:T(8,128)S(1)}, u32[]{:S(2)}, u32[]{:S(2)}) collective-permute-start(f32[512,128]{1,0:T(8,128)S(1)} %add.70), channel_id=1, source_target_pairs={{6,0},{12,6},{18,12},{24,18},{30,24},{36,30},{42,36},{48,42},{54,4... | collective-permute-start | bytes 786440 | tf_op jit(solution)/shard_map/back_halo/ppermute | solution.py:150
  157.0 17.1 %copy-start.14 = (f32[512,128]{1,0:T(8,128)S(1)}, f32[512,128]{1,0:T(8,128)}, u32[]{:S(2)}) copy-start(f32[512,128]{1,0:T(8,128)} %copy-done.13) | copy-start | bytes 786436
  157.0 28.1 %all-to-all-start.2 = ((f32[32,16,128]{2,1,0:T(8,128)}), f32[32,16,128]{2,1,0:T(8,128)S(1)}, u32[]{:S(2)}, u32[]{:S(2)}) async-start(f32[32,16,128]{2,1,0:T(8,128)} %broadcast_in_dim.5), calls=%async_computation.2 | async-start | bytes 524288 | tf_op jit(solution)/shard_map/nodes_sum/all_to_all | solution.py:244

commit v2 on v1

v2 whole, which is shorter than its diff:
```python
import jax
import jax.numpy as jnp
from jax import lax
from jax.experimental import pallas as pl
from jax.experimental.pallas import tpu as pltpu
from jax.sharding import Mesh, PartitionSpec as P

NODES = ("x", "y", "zh")
YEARS = ("zl", "c")
PLANE = ("x", "y")
REACH = 2
T = 128
F32 = jnp.float32
BF = jnp.bfloat16
VMEM = pl.BlockSpec(memory_space=pltpu.VMEM)
SMEM = pl.BlockSpec(memory_space=pltpu.SMEM)


def shape_of(shape, dtype=F32):
    return jax.ShapeDtypeStruct(shape, dtype)


def call(kernel, ins, outs, scratch, flops, bytes_accessed, name, limit):
    return pl.pallas_call(
        kernel,
        in_specs=ins,
        out_specs=[VMEM] * len(outs),
        out_shape=outs,
        scratch_shapes=scratch,
        name=name,
        cost_estimate=pl.CostEstimate(
            flops=flops, bytes_accessed=bytes_accessed, transcendentals=0
        ),
        compiler_params=pltpu.CompilerParams(vmem_limit_bytes=limit * 2**20),
    )


def split(v):
    hi = v.astype(BF)
    lo = (v - hi.astype(F32)).astype(BF)
    return hi, lo


def dot(a, b):
    return lax.dot_general(a, b, (((1,), (0,)), ((), ())), preferred_element_type=F32)


def dot_t(a, b):
    return lax.dot_general(a, b, (((1,), (1,)), ((), ())), preferred_element_type=F32)


def prepare_kernel(count, tiles, a_hi, a_lo, t_hl, rdeg):
    for t in range(tiles.shape[0]):
        total = jnp.zeros((T, T), F32)
        for s in range(tiles.shape[1]):
            live = jnp.where(s < count[t], 1.0, 0.0).astype(F32)
            a = tiles[t, s] * live
            total = total + a
            cols = slice(s * T, (s + 1) * T)
            hi, lo = split(a)
            a_hi[t, :, cols] = hi
            a_lo[t, :, cols] = lo
            hi, lo = split(a.T)
            t_hl[t, cols, :T] = hi
            t_hl[t, cols, T:] = lo
        degree = 1.0 + jnp.sum(total, axis=1, keepdims=True)
        rdeg[t * T : (t + 1) * T, :] = jnp.broadcast_to(1.0 / degree, (T, T))


def window_index(offset, t, s):
    return jnp.clip(t + offset[t, s] + 2 * 4, 0, 19)


def mix_kernel(where, offset, far, near, own, a_hi, a_lo, partial, window):
    rows = own.shape[1]
    c = where[0]
    for ref, shard in ((far, 4 * c), (near, 1 + 2 * c), (own, 2)):
        at = pl.multiple_of(shard * rows, rows)
        for k in range(2):
            hi, lo = split(ref[k])
            window[pl.ds(at, rows), k * T : (k + 1) * T] = hi
            window[pl.ds(at, rows), (2 + k) * T : (3 + k) * T] = lo
    window[5 * rows :, :] = jnp.zeros((T, 4 * T), BF)
    low, high = 12 * c, 12 + 8 * c
    first = (1 - c).astype(F32)
    for t in range(a_hi.shape[0]):
        picked = []
        for s in range(4):
            w = window_index(offset, t, s)
            w = jnp.where((w >= low) & (w < high), w, 20)
            picked.append(window[pl.ds(pl.multiple_of(w * T, T), T), :])
        b = jnp.concatenate(picked, axis=0)
        wide = dot(a_hi[t], b)
        total = wide[:, : 2 * T] + wide[:, 2 * T :] + dot(a_lo[t], b[:, : 2 * T])
        r = slice(t * T, (t + 1) * T)
        for k in range(2):
            partial[k, r, :] = total[:, k * T : (k + 1) * T] + own[k, r, :] * first


def layer_kernel(
    where, offset, mixed, got, swapped, weight, weight_got, weight_swapped, bias, gout, rdeg, t_hl,
    output, parts, far, near, center, m_hi, m_lo, w_hi, w_lo, s_hi, s_lo, g_hi, g_lo, back,
):
    rows = gout.shape[0]
    c, zl = where[0], where[1]
    arrived = ((mixed, weight, 0), (got, weight_got, 1 + c), (swapped, weight_swapped, 2 - c))
    for ref, ref_w, back_by in arrived:
        chip = lax.rem(zl - back_by + 3, 3)
        for k in range(2):
            hi, lo = split(ref[k])
            m_hi[chip * 2 + k] = hi
            m_lo[chip * 2 + k] = lo
            hi, lo = split(ref_w[k])
            at = pl.ds(pl.multiple_of((chip * 2 + k) * T, T), T)
            w_hi[at, :] = hi
            w_lo[at, :] = lo
    back[...] = jnp.zeros_like(back)
    line = jnp.zeros((1, 4 * T), F32)
    for t in range(rows // T):
        r = slice(t * T, (t + 1) * T)
        mh = jnp.concatenate([m_hi[k, r, :] for k in range(6)], axis=1)
        ml = jnp.concatenate([m_lo[k, r, :] for k in range(6)], axis=1)
        pre = dot(mh, w_hi[...]) + dot(mh, w_lo[...]) + dot(ml, w_hi[...]) + bias[...]
        sigma = 1.0 / (1.0 + jnp.exp(-pre))
        output[r, :] = pre * sigma
        g = gout[r, :] * sigma * (1.0 + pre * (1.0 - sigma))
        line = line + jnp.sum(g, axis=0, keepdims=True)
        hi, lo = split(g)
        g_hi[r, :] = hi
        g_lo[r, :] = lo
        scale = rdeg[r, :]
        hi, lo = split(g * jnp.concatenate([scale] * 4, axis=1))
        s_hi[r, :] = hi
        s_lo[r, :] = lo
    mine = pl.ds(pl.multiple_of(zl * (2 * T), 2 * T), 2 * T)
    wh, wl = w_hi[mine, :], w_lo[mine, :]
    z = dot_t(s_hi[...], wh) + dot_t(s_hi[...], wl) + dot_t(s_lo[...], wh)
    back[REACH * rows : (REACH + 1) * rows, :] = z
    zh, zo = split(z)
    for t in range(rows // T):
        r = slice(t * T, (t + 1) * T)
        both = jnp.concatenate([zh[r, :], zh[r, :]], axis=0)
        contrib = dot(t_hl[t], both) + dot(t_hl[t, :, :T], zo[r, :])
        for s in range(4):
            at = pl.multiple_of(window_index(offset, t, s) * T, T)
            back[pl.ds(at, T), :] += contrib[s * T : (s + 1) * T, :]
    far[...] = back[pl.ds(pl.multiple_of((4 - 4 * c) * rows, rows), rows), :]
    near[...] = back[pl.ds(pl.multiple_of((3 - 2 * c) * rows, rows), rows), :]
    mid = back[REACH * rows : (REACH + 1) * rows, :]
    center[...] = jnp.where(c == 0, mid[:, :T], mid[:, T:])
    own = mixed[c]
    m = jnp.concatenate([own[t * T : (t + 1) * T, :].T for t in range(rows // T)], axis=1)
    mh, ml = split(m)
    total = dot(mh, g_hi[...]) + dot(mh, g_lo[...]) + dot(ml, g_hi[...])
    for p in range(32):
        cols = slice((p % 4) * T, (p % 4 + 1) * T)
        parts[p, 0:16, :] = total[(p // 4) * 16 : (p // 4 + 1) * 16, cols]
        for k in range(4):
            parts[p, 16 + k : 17 + k, :] = line[:, k * T : (k + 1) * T]
        parts[p, 20:24, :] = jnp.zeros((4, T), F32)


def arrange_kernel(pieces, out):
    for p in range(32):
        out[(p // 4) * 16 : (p // 4 + 1) * 16, (p % 4) * T : (p % 4 + 1) * T] = pieces[p]


def by_core(block, axis, first, second):
    n = lax.axis_size(axis)
    route = [(2 * i + c, 2 * ((i + d) % n) + c) for i in range(n) for c, d in ((0, first), (1, second))]
    axes = (axis if isinstance(axis, tuple) else (axis,)) + ("c",)
    return lax.ppermute(block, axes, route)


def swap(block):
    return lax.ppermute(block, "c", [(0, 1), (1, 0)])


def body(features, weight, bias, tile_weights, tile_offsets, tile_counts, grad_out):
    rows, width = features.shape
    tiles = tile_weights.shape[0]
    zl, c = lax.axis_index("zl"), lax.axis_index("c")
    where = jnp.stack([c, zl]).astype(jnp.int32)

    with jax.named_scope("halo"):
        other = swap(features)
        pair = jnp.where(c == 0, jnp.stack([features, other]), jnp.stack([other, features]))
        near = by_core(pair, NODES, 1, -1)
        far = by_core(near, NODES, 1, -1)
    with jax.named_scope("weight_gather"):
        other_weight = swap(weight)
        mine = jnp.where(c == 0, jnp.stack([weight, other_weight]), jnp.stack([other_weight, weight]))
        mine, near = lax.optimization_barrier((mine, near))
        weight_got = by_core(mine, "zl", 1, 2)
        weight_swapped = swap(weight_got)

    a_hi, a_lo, t_hl, rdeg = call(
        prepare_kernel,
        [SMEM, VMEM],
        [
            shape_of((tiles, T, 4 * T), BF),
            shape_of((tiles, T, 4 * T), BF),
            shape_of((tiles, 4 * T, 2 * T), BF),
            shape_of((rows, T)),
        ],
        [],
        10**6,
        4 * 10**6,
        "prepare",
        8,
    )(tile_counts, tile_weights)
    (partial,) = call(
        mix_kernel,
        [SMEM] * 2 + [VMEM] * 5,
        [shape_of((2, rows, width))],
        [pltpu.VMEM((5 * rows + T, 4 * T), BF)],
        2 * 10**8,
        3 * 10**6,
        "mix",
        12,
    )(where, tile_offsets, far, near, pair, a_hi, a_lo)
    with jax.named_scope("mixed_gather"):
        mixed = (partial + swap(partial)) * rdeg[None]
        got = by_core(mixed, "zl", 1, 2)
        swapped = swap(got)
    output, parts, q_far, q_near, center = call(
        layer_kernel,
        [SMEM] * 2 + [VMEM] * 10,
        [shape_of((rows, 4 * T)), shape_of((32, 24, T))] + [shape_of((rows, 2 * width))] * 2 + [shape_of((rows, width))],
        [
            pltpu.VMEM((6, rows, T), BF),
            pltpu.VMEM((6, rows, T), BF),
            pltpu.VMEM((6 * T, 4 * T), BF),
            pltpu.VMEM((6 * T, 4 * T), BF),
            pltpu.VMEM((rows, 4 * T), BF),
            pltpu.VMEM((rows, 4 * T), BF),
            pltpu.VMEM((rows, 4 * T), BF),
            pltpu.VMEM((rows, 4 * T), BF),
            pltpu.VMEM((5 * rows, 2 * T), F32),
        ],
        15 * 10**8,
        10**7,
        "layer",
        20,
    )(
        where, tile_offsets, mixed, got, swapped, mine, weight_got, weight_swapped,
        bias.reshape(1, -1), grad_out, rdeg, t_hl,
    )
    with jax.named_scope("nodes_sum"):
        held = jnp.sum(lax.all_to_all(parts, PLANE, 0, 0), axis=0)
    with jax.named_scope("back_halo"):
        came = by_core(q_far, NODES, 1, -1)
    with jax.named_scope("nodes_sum"):
        held = jnp.broadcast_to(held[None], (4, 24, T))
        held = jnp.sum(lax.all_to_all(held, "zh", 0, 0), axis=0)
    with jax.named_scope("back_halo"):
        came, held = lax.optimization_barrier((q_near + came, held))
        came = by_core(came, NODES, 1, -1)
        lent = swap(jnp.where(c == 0, came[:, width:], came[:, :width]))
        grad_features = center + (jnp.where(c == 0, came[:, :width], came[:, width:]) + lent)
    with jax.named_scope("nodes_sum"):
        grad_bias = held[16:20].reshape(-1)
        whole = jnp.broadcast_to(held[None, :16], (32, 16, T))
        whole = lax.all_to_all(whole, PLANE, 0, 0)
    (grad_weight,) = call(
        arrange_kernel, [VMEM], [shape_of((T, 4 * T))], [], 10**3, 5 * 10**5, "arrange", 4
    )(whole)
    return output, grad_features, grad_weight, grad_bias


def solution(mesh):
    fine = Mesh(mesh.devices.reshape(4, 8, 4, 3, 2), NODES + YEARS)
    placed = (
        P(NODES, YEARS),
        P(YEARS, None),
        P(),
        P(NODES, None, None, None),
        P(NODES, None),
        P(NODES),
        P(NODES, None),
    )
    return jax.shard_map(
        body,
        mesh=fine,
        in_specs=placed,
        out_specs=(P(NODES, None), P(NODES, YEARS), P(YEARS, None), P()),
        check_vma=False,
    )
```

time: 187 us -> 182 us (0.973)
  the two profiles are of different devices: /device:TPU:72 before, /device:TPU:1 now
where the time goes in v2:
time: 182 us
  starting transfers between devices  97.7 us (54%)
  waiting for transfers between devices  69.1 us (38%)
  Pallas kernels  9.12 us (5%)
  local copies, waits for them, and re-layouts  2.59 us (1%)
  other arithmetic  2.2 us (1%)
    ppermute x6, waiting for transfers between devices, by_core(): return lax.ppermute(block, axes, route)  65.2 us
    ppermute x6, starting transfers between devices, by_core(): return lax.ppermute(block, axes, route)  51.1 us
    ppermute x6, starting transfers between devices, swap(): return lax.ppermute(block, 'c', [(0, 1), (1, 0)])  32.6 us
    all_to_all x1, starting transfers between devices, body(): held = jnp.sum(lax.all_to_all(held, 'zh', 0, 0), axis=0)  6.2 us
    pallas_call x1, Pallas kernels, body(): call(layer_kernel, [SMEM] * 2 + [VMEM] * 10, [shape_of((rows, 4 * T)), sh...  5.76 us
    all_to_all x1, starting transfers between devices, body(): held = jnp.sum(lax.all_to_all(parts, PLANE, 0, 0), axis=0)  3.88 us
    all_to_all x1, starting transfers between devices, body(): whole = lax.all_to_all(whole, PLANE, 0, 0)  3.87 us
  transfers between devices with their start and end apart: 15, of which 10 were waited for; matrix products, arithmetic and copies ran while one was open for 1% of the time, Pallas kernels for 1%

profile of v2, /device:TPU:1, one launch (start us, length us, event | category | flops | bytes accessed | tf_op | source)
XLA Modules:
  0.0 181.5 jit_solution(2065181332171719978)
XLA Ops:
  0.6 0.0 copy-start
  0.6 12.6 %collective-permute-start = (f32[512,128]{1,0:T(8,128)}, f32[512,128]{1,0:T(8,128)S(1)}, u32[]{:S(2)}, u32[]{:S(2)}) collective-permute-start(f32[512,128]{1,0:T(8,128)} %param.7), channel_id=1, source_target_pairs={{0,1},{1,0},{2,3},{3,2},{4,5},{5,4},{6,7},{7,6},{8,9},{9,8},{10,11... | collective-permute-start | bytes 786440 | tf_op jit(solution)/shard_map/halo/ppermute | solution.py:176
  13.2 1.3 collective-permute-done
  14.6 1.1 maximum_select_fusion.own
  15.6 10.4 %collective-permute-start.1 = (f32[2,512,128]{2,1,0:T(8,128)S(1)}, f32[2,512,128]{2,1,0:T(8,128)S(1)}, u32[]{:S(2)}, u32[]{:S(2)}) collective-permute-start(f32[2,512,128]{2,1,0:T(8,128)S(1)} %maximum_select_fusion.own), channel_id=1, source_target_pairs={{0,6},{1,763},{6,12},{7,1},{12,18},{13,7},{18,24},{19,13},{24,30},... | collective-permute-start | bytes 1572872 | tf_op jit(solution)/shard_map/halo/ppermute | solution.py:172
  26.0 17.4 %collective-permute-done.1.near = f32[2,512,128]{2,1,0:T(8,128)S(1)} collective-permute-done((f32[2,512,128]{2,1,0:T(8,128)S(1)}, f32[2,512,128]{2,1,0:T(8,128)S(1)}, u32[]{:S(2)}, u32[]{:S(2)}) %collective-permute-start.1) | collective-permute-done | bytes 524320 | tf_op jit(solution)/shard_map/halo/ppermute | solution.py:172
  43.4 11.2 %collective-permute-start.2 = (f32[2,512,128]{2,1,0:T(8,128)S(1)}, f32[2,512,128]{2,1,0:T(8,128)S(1)}, u32[]{:S(2)}, u32[]{:S(2)}) collective-permute-start(f32[2,512,128]{2,1,0:T(8,128)S(1)} %collective-permute-done.1.near), channel_id=1, source_target_pairs={{0,6},{1,763},{6,12},{7,1},{12,18},{13,7},{18,24},{19,13},{24,30},... | collective-permute-start | bytes 1572872 | tf_op jit(solution)/shard_map/halo/ppermute | solution.py:172
  54.6 1.9 %collective-permute-start.3 = (f32[128,512]{1,0:T(8,128)}, f32[128,512]{1,0:T(8,128)S(1)}, u32[]{:S(2)}, u32[]{:S(2)}) collective-permute-start(f32[128,512]{1,0:T(8,128)} %param.8), channel_id=1, source_target_pairs={{0,1},{1,0},{2,3},{3,2},{4,5},{5,4},{6,7},{7,6},{8,9},{9,8},{10,11... | collective-permute-start | bytes 786440 | tf_op jit(solution)/shard_map/weight_gather/ppermute | solution.py:176
  56.5 0.0 copy-start.2
  56.5 0.0 copy-done
  56.6 0.6 copy-done.2
  57.2 1.0 prepare.1
  58.2 0.1 pad_add_fusion.where
  58.3 0.0 collective-permute-done.3
  58.4 0.0 copy-start.1
  58.4 12.7 %collective-permute-done.2.far = f32[2,512,128]{2,1,0:T(8,128)S(1)} collective-permute-done((f32[2,512,128]{2,1,0:T(8,128)S(1)}, f32[2,512,128]{2,1,0:T(8,128)S(1)}, u32[]{:S(2)}, u32[]{:S(2)}) %collective-permute-start.2) | collective-permute-done | bytes 524320 | tf_op jit(solution)/shard_map/halo/ppermute | solution.py:172
  71.1 1.6 mix.1
  72.7 0.0 copy-start.3
  72.7 2.1 %collective-permute-start.4 = (f32[2,512,128]{2,1,0:T(8,128)S(1)}, f32[2,512,128]{2,1,0:T(8,128)S(1)}, u32[]{:S(2)}, u32[]{:S(2)}) collective-permute-start(f32[2,512,128]{2,1,0:T(8,128)S(1)} %mix.1), channel_id=1, source_target_pairs={{0,1},{1,0},{2,3},{3,2},{4,5},{5,4},{6,7},{7,6},{8,9},{9,8},{10,11... | collective-permute-start | bytes 1572872 | tf_op jit(solution)/shard_map/mixed_gather/ppermute | solution.py:176
  74.7 5.2 %collective-permute-start.7 = (f32[2,128,512]{2,1,0:T(8,128)S(1)}, f32[2,128,512]{2,1,0:T(8,128)S(1)}, u32[]{:S(2)}, u32[]{:S(2)}) collective-permute-start(f32[2,128,512]{2,1,0:T(8,128)S(1)} %maximum_select_fusion.1.weight), channel_id=1, source_target_pairs={{0,2},{1,5},{2,4},{3,1},{4,0},{5,3},{6,8},{7,11},{8,10},{9,7},{10,... | collective-permute-start | bytes 1572872 | tf_op jit(solution)/shard_map/weight_gather/ppermute | solution.py:172
  79.9 0.0 collective-permute-done.4
  79.9 0.1 add_multiply_fusion.mixed
  80.1 1.9 %collective-permute-start.5 = (f32[2,512,128]{2,1,0:T(8,128)S(1)}, f32[2,512,128]{2,1,0:T(8,128)S(1)}, u32[]{:S(2)}, u32[]{:S(2)}) collective-permute-start(f32[2,512,128]{2,1,0:T(8,128)S(1)} %add_multiply_fusion.mixed), channel_id=1, source_target_pairs={{0,2},{1,5},{2,4},{3,1},{4,0},{5,3},{6,8},{7,11},{8,10},{9,7},{10,... | collective-permute-start | bytes 1572872 | tf_op jit(solution)/shard_map/mixed_gather/ppermute | solution.py:172
  82.0 9.7 %collective-permute-done.7.weight_got = f32[2,128,512]{2,1,0:T(8,128)S(1)} collective-permute-done((f32[2,128,512]{2,1,0:T(8,128)S(1)}, f32[2,128,512]{2,1,0:T(8,128)S(1)}, u32[]{:S(2)}, u32[]{:S(2)}) %collective-permute-start.7) | collective-permute-done | bytes 524320 | tf_op jit(solution)/shard_map/weight_gather/ppermute | solution.py:172
  91.7 3.2 %collective-permute-start.8 = (f32[2,128,512]{2,1,0:T(8,128)S(1)}, f32[2,128,512]{2,1,0:T(8,128)S(1)}, u32[]{:S(2)}, u32[]{:S(2)}) collective-permute-start(f32[2,128,512]{2,1,0:T(8,128)S(1)} %collective-permute-done.7.weight_got), channel_id=1, source_target_pairs={{0,1},{1,0},{2,3},{3,2},{4,5},{5,4},{6,7},{7,6},{8,9},{9,8},{10,11... | collective-permute-start | bytes 1572872 | tf_op jit(solution)/shard_map/weight_gather/ppermute | solution.py:176
  94.9 6.4 %collective-permute-done.5.got = f32[2,512,128]{2,1,0:T(8,128)S(1)} collective-permute-done((f32[2,512,128]{2,1,0:T(8,128)S(1)}, f32[2,512,128]{2,1,0:T(8,128)S(1)}, u32[]{:S(2)}, u32[]{:S(2)}) %collective-permute-start.5) | collective-permute-done | bytes 524320 | tf_op jit(solution)/shard_map/mixed_gather/ppermute | solution.py:172
  101.2 4.7 %collective-permute-start.6 = (f32[2,512,128]{2,1,0:T(8,128)S(1)}, f32[2,512,128]{2,1,0:T(8,128)S(1)}, u32[]{:S(2)}, u32[]{:S(2)}) collective-permute-start(f32[2,512,128]{2,1,0:T(8,128)S(1)} %collective-permute-done.5.got), channel_id=1, source_target_pairs={{0,1},{1,0},{2,3},{3,2},{4,5},{5,4},{6,7},{7,6},{8,9},{9,8},{10,11... | collective-permute-start | bytes 1572872 | tf_op jit(solution)/shard_map/mixed_gather/ppermute | solution.py:176
  105.9 0.0 collective-permute-done.8.weight_swapped
  105.9 1.5 collective-permute-done.6.swapped
  107.4 5.8 %layer.1 = (f32[512,512]{1,0:T(8,128)}, f32[32,24,128]{2,1,0:T(8,128)}, f32[512,256]{1,0:T(8,128)S(1)}, f32[512,256]{1,0:T(8,128)S(1)}, f32[512,128]{1,0:T(8,128)S(1)}) custom-call(s32[2]{0:T(128)S(1)} %pad_add_fusion.where, s32[4,4]{1,0:T(4,128)S(1)} %copy-done.1, f32[2,512,128]{2,1,0:T(8,128)S(1)} %add_multiply_fusion.mixed, ...), custom_call_target="tpu_custom_call" | custom-call | flops 1500000000 | bytes 10000000 | tf_op jit(solution)/shard_map/layer/pallas_call | solution.py:226
  113.2 3.9 %all-to-all-start = ((f32[32,24,128]{2,1,0:T(8,128)}), f32[32,24,128]{2,1,0:T(8,128)S(1)}, u32[]{:S(2)}, u32[]{:S(2)}) async-start(f32[32,24,128]{2,1,0:T(8,128)} %get-tuple-element.27), calls=%async_computation | async-start | bytes 786432 | tf_op jit(solution)/shard_map/nodes_sum/all_to_all | solution.py:250
  117.1 11.3 %collective-permute-start.9 = (f32[512,256]{1,0:T(8,128)S(1)}, f32[512,256]{1,0:T(8,128)S(1)}, u32[]{:S(2)}, u32[]{:S(2)}) collective-permute-start(f32[512,256]{1,0:T(8,128)S(1)} %get-tuple-element.26), channel_id=1, source_target_pairs={{0,6},{1,763},{6,12},{7,1},{12,18},{13,7},{18,24},{19,13},{24,30},... | collective-permute-start | bytes 1572872 | tf_op jit(solution)/shard_map/back_halo/ppermute | solution.py:172
  128.4 1.0 all-to-all-done
  129.4 0.6 broadcast_in_dim.4
  130.1 6.2 %all-to-all-start.1 = ((f32[4,24,128]{2,1,0:T(8,128)}), f32[4,24,128]{2,1,0:T(8,128)S(1)}, u32[]{:S(2)}, u32[]{:S(2)}) async-start(f32[4,24,128]{2,1,0:T(8,128)} %broadcast_in_dim.4), calls=%async_computation.1 | async-start | bytes 98304 | tf_op jit(solution)/shard_map/nodes_sum/all_to_all | solution.py:255
  136.3 11.0 %collective-permute-done.9 = f32[512,256]{1,0:T(8,128)S(1)} collective-permute-done((f32[512,256]{1,0:T(8,128)S(1)}, f32[512,256]{1,0:T(8,128)S(1)}, u32[]{:S(2)}, u32[]{:S(2)}) %collective-permute-start.9) | collective-permute-done | bytes 524320 | tf_op jit(solution)/shard_map/back_halo/ppermute | solution.py:172
  147.2 0.1 add.13
  147.3 0.1 all-to-all-done.1
  147.4 11.1 %collective-permute-start.10 = (f32[512,256]{1,0:T(8,128)S(1)}, f32[512,256]{1,0:T(8,128)S(1)}, u32[]{:S(2)}, u32[]{:S(2)}) collective-permute-start(f32[512,256]{1,0:T(8,128)S(1)} %add.13), channel_id=1, source_target_pairs={{0,6},{1,763},{6,12},{7,1},{12,18},{13,7},{18,24},{19,13},{24,30},... | collective-permute-start | bytes 1572872 | tf_op jit(solution)/shard_map/back_halo/ppermute | solution.py:172
  158.5 0.7 broadcast_in_dim.5
  159.2 3.9 %all-to-all-start.2 = ((f32[32,16,128]{2,1,0:T(8,128)}), f32[32,16,128]{2,1,0:T(8,128)S(1)}, u32[]{:S(2)}, u32[]{:S(2)}) async-start(f32[32,16,128]{2,1,0:T(8,128)} %broadcast_in_dim.5), calls=%async_computation.2 | async-start | bytes 524288 | tf_op jit(solution)/shard_map/nodes_sum/all_to_all | solution.py:264
  163.1 8.1 %collective-permute-done.10 = f32[512,256]{1,0:T(8,128)S(1)} collective-permute-done((f32[512,256]{1,0:T(8,128)S(1)}, f32[512,256]{1,0:T(8,128)S(1)}, u32[]{:S(2)}, u32[]{:S(2)}) %collective-permute-start.10) | collective-permute-done | bytes 524320 | tf_op jit(solution)/shard_map/back_halo/ppermute | solution.py:172
  171.2 8.3 %collective-permute-start.11 = (f32[512,128]{1,0:T(8,128)S(1)}, f32[512,128]{1,0:T(8,128)S(1)}, u32[]{:S(2)}, u32[]{:S(2)}) collective-permute-start(f32[512,128]{1,0:T(8,128)S(1)} %slice_select_fusion), channel_id=1, source_target_pairs={{0,1},{1,0},{2,3},{3,2},{4,5},{5,4},{6,7},{7,6},{8,9},{9,8},{10,11... | collective-permute-start | bytes 786440 | tf_op jit(solution)/shard_map/back_halo/ppermute | solution.py:176
  179.4 0.6 slice_bitcast_fusion
  180.0 0.0 all-to-all-done.2.pieces
  180.0 0.7 arrange.1
  180.7 0.0 collective-permute-done.11
  180.7 0.8 add_add_fusion
  (11 shorter events, 0.1 us)
Async XLA Ops:
  0.6 55.9 %copy-start = (f32[4,4,128,128]{3,2,1,0:T(8,128)S(1)}, f32[4,4,128,128]{3,2,1,0:T(8,128)}, u32[]{:S(2)}) copy-start(f32[4,4,128,128]{3,2,1,0:T(8,128)} %tiles.1) | copy-start | bytes 3145732
  0.6 13.9 %collective-permute-start = (f32[512,128]{1,0:T(8,128)}, f32[512,128]{1,0:T(8,128)S(1)}, u32[]{:S(2)}, u32[]{:S(2)}) collective-permute-start(f32[512,128]{1,0:T(8,128)} %param.7), channel_id=1, source_target_pairs={{0,1},{1,0},{2,3},{3,2},{4,5},{5,4},{6,7},{7,6},{8,9},{9,8},{10,11... | collective-permute-start | bytes 786440 | tf_op jit(solution)/shard_map/halo/ppermute | solution.py:176
  15.6 27.8 %collective-permute-start.1 = (f32[2,512,128]{2,1,0:T(8,128)S(1)}, f32[2,512,128]{2,1,0:T(8,128)S(1)}, u32[]{:S(2)}, u32[]{:S(2)}) collective-permute-start(f32[2,512,128]{2,1,0:T(8,128)S(1)} %maximum_select_fusion.own), channel_id=1, source_target_pairs={{0,6},{1,763},{6,12},{7,1},{12,18},{13,7},{18,24},{19,13},{24,30},... | collective-permute-start | bytes 1572872 | tf_op jit(solution)/shard_map/halo/ppermute | solution.py:172
  43.4 27.7 %collective-permute-start.2 = (f32[2,512,128]{2,1,0:T(8,128)S(1)}, f32[2,512,128]{2,1,0:T(8,128)S(1)}, u32[]{:S(2)}, u32[]{:S(2)}) collective-permute-start(f32[2,512,128]{2,1,0:T(8,128)S(1)} %collective-permute-done.1.near), channel_id=1, source_target_pairs={{0,6},{1,763},{6,12},{7,1},{12,18},{13,7},{18,24},{19,13},{24,30},... | collective-permute-start | bytes 1572872 | tf_op jit(solution)/shard_map/halo/ppermute | solution.py:172
  54.6 3.7 %collective-permute-start.3 = (f32[128,512]{1,0:T(8,128)}, f32[128,512]{1,0:T(8,128)S(1)}, u32[]{:S(2)}, u32[]{:S(2)}) collective-permute-start(f32[128,512]{1,0:T(8,128)} %param.8), channel_id=1, source_target_pairs={{0,1},{1,0},{2,3},{3,2},{4,5},{5,4},{6,7},{7,6},{8,9},{9,8},{10,11... | collective-permute-start | bytes 786440 | tf_op jit(solution)/shard_map/weight_gather/ppermute | solution.py:176
  56.5 0.7 copy-start.2
  57.2 1.1 copy-start.5
  58.4 12.7 %copy-start.1 = (s32[4,4]{1,0:T(4,128)S(1)}, s32[4,4]{1,0:T(4,128)}, u32[]{:S(2)}) copy-start(s32[4,4]{1,0:T(4,128)} %offset.3) | copy-start | bytes 196
  72.7 34.8 %copy-start.3 = (f32[512,512]{1,0:T(8,128)S(1)}, f32[512,512]{1,0:T(8,128)}, u32[]{:S(2)}) copy-start(f32[512,512]{1,0:T(8,128)} %gout.1) | copy-start | bytes 3145732
  72.7 7.3 %collective-permute-start.4 = (f32[2,512,128]{2,1,0:T(8,128)S(1)}, f32[2,512,128]{2,1,0:T(8,128)S(1)}, u32[]{:S(2)}, u32[]{:S(2)}) collective-permute-start(f32[2,512,128]{2,1,0:T(8,128)S(1)} %mix.1), channel_id=1, source_target_pairs={{0,1},{1,0},{2,3},{3,2},{4,5},{5,4},{6,7},{7,6},{8,9},{9,8},{10,11... | collective-permute-start | bytes 1572872 | tf_op jit(solution)/shard_map/mixed_gather/ppermute | solution.py:176
  74.7 17.0 %collective-permute-start.7 = (f32[2,128,512]{2,1,0:T(8,128)S(1)}, f32[2,128,512]{2,1,0:T(8,128)S(1)}, u32[]{:S(2)}, u32[]{:S(2)}) collective-permute-start(f32[2,128,512]{2,1,0:T(8,128)S(1)} %maximum_select_fusion.1.weight), channel_id=1, source_target_pairs={{0,2},{1,5},{2,4},{3,1},{4,0},{5,3},{6,8},{7,11},{8,10},{9,7},{10,... | collective-permute-start | bytes 1572872 | tf_op jit(solution)/shard_map/weight_gather/ppermute | solution.py:172
  80.0 27.4 %copy-start.4 = (f32[512]{0:T(512)S(1)}, f32[512]{0:T(512)}, u32[]{:S(2)}) copy-start(f32[512]{0:T(512)} %param.9) | copy-start | bytes 6148
  80.1 21.2 %collective-permute-start.5 = (f32[2,512,128]{2,1,0:T(8,128)S(1)}, f32[2,512,128]{2,1,0:T(8,128)S(1)}, u32[]{:S(2)}, u32[]{:S(2)}) collective-permute-start(f32[2,512,128]{2,1,0:T(8,128)S(1)} %add_multiply_fusion.mixed), channel_id=1, source_target_pairs={{0,2},{1,5},{2,4},{3,1},{4,0},{5,3},{6,8},{7,11},{8,10},{9,7},{10,... | collective-permute-start | bytes 1572872 | tf_op jit(solution)/shard_map/mixed_gather/ppermute | solution.py:172
  91.7 14.2 %collective-permute-start.8 = (f32[2,128,512]{2,1,0:T(8,128)S(1)}, f32[2,128,512]{2,1,0:T(8,128)S(1)}, u32[]{:S(2)}, u32[]{:S(2)}) collective-permute-start(f32[2,128,512]{2,1,0:T(8,128)S(1)} %collective-permute-done.7.weight_got), channel_id=1, source_target_pairs={{0,1},{1,0},{2,3},{3,2},{4,5},{5,4},{6,7},{7,6},{8,9},{9,8},{10,11... | collective-permute-start | bytes 1572872 | tf_op jit(solution)/shard_map/weight_gather/ppermute | solution.py:176
  101.2 6.2 %collective-permute-start.6 = (f32[2,512,128]{2,1,0:T(8,128)S(1)}, f32[2,512,128]{2,1,0:T(8,128)S(1)}, u32[]{:S(2)}, u32[]{:S(2)}) collective-permute-start(f32[2,512,128]{2,1,0:T(8,128)S(1)} %collective-permute-done.5.got), channel_id=1, source_target_pairs={{0,1},{1,0},{2,3},{3,2},{4,5},{5,4},{6,7},{7,6},{8,9},{9,8},{10,11... | collective-permute-start | bytes 1572872 | tf_op jit(solution)/shard_map/mixed_gather/ppermute | solution.py:176
  113.2 16.2 %all-to-all-start = ((f32[32,24,128]{2,1,0:T(8,128)}), f32[32,24,128]{2,1,0:T(8,128)S(1)}, u32[]{:S(2)}, u32[]{:S(2)}) async-start(f32[32,24,128]{2,1,0:T(8,128)} %get-tuple-element.27), calls=%async_computation | async-start | bytes 786432 | tf_op jit(solution)/shard_map/nodes_sum/all_to_all | solution.py:250
  117.1 30.1 %collective-permute-start.9 = (f32[512,256]{1,0:T(8,128)S(1)}, f32[512,256]{1,0:T(8,128)S(1)}, u32[]{:S(2)}, u32[]{:S(2)}) collective-permute-start(f32[512,256]{1,0:T(8,128)S(1)} %get-tuple-element.26), channel_id=1, source_target_pairs={{0,6},{1,763},{6,12},{7,1},{12,18},{13,7},{18,24},{19,13},{24,30},... | collective-permute-start | bytes 1572872 | tf_op jit(solution)/shard_map/back_halo/ppermute | solution.py:172
  130.1 17.3 %all-to-all-start.1 = ((f32[4,24,128]{2,1,0:T(8,128)}), f32[4,24,128]{2,1,0:T(8,128)S(1)}, u32[]{:S(2)}, u32[]{:S(2)}) async-start(f32[4,24,128]{2,1,0:T(8,128)} %broadcast_in_dim.4), calls=%async_computation.1 | async-start | bytes 98304 | tf_op jit(solution)/shard_map/nodes_sum/all_to_all | solution.py:255
  147.4 23.7 %collective-permute-start.10 = (f32[512,256]{1,0:T(8,128)S(1)}, f32[512,256]{1,0:T(8,128)S(1)}, u32[]{:S(2)}, u32[]{:S(2)}) collective-permute-start(f32[512,256]{1,0:T(8,128)S(1)} %add.13), channel_id=1, source_target_pairs={{0,6},{1,763},{6,12},{7,1},{12,18},{13,7},{18,24},{19,13},{24,30},... | collective-permute-start | bytes 1572872 | tf_op jit(solution)/shard_map/back_halo/ppermute | solution.py:172
  159.2 20.8 %all-to-all-start.2 = ((f32[32,16,128]{2,1,0:T(8,128)}), f32[32,16,128]{2,1,0:T(8,128)S(1)}, u32[]{:S(2)}, u32[]{:S(2)}) async-start(f32[32,16,128]{2,1,0:T(8,128)} %broadcast_in_dim.5), calls=%async_computation.2 | async-start | bytes 524288 | tf_op jit(solution)/shard_map/nodes_sum/all_to_all | solution.py:264
  171.2 9.6 %collective-permute-start.11 = (f32[512,128]{1,0:T(8,128)S(1)}, f32[512,128]{1,0:T(8,128)S(1)}, u32[]{:S(2)}, u32[]{:S(2)}) collective-permute-start(f32[512,128]{1,0:T(8,128)S(1)} %slice_select_fusion), channel_id=1, source_target_pairs={{0,1},{1,0},{2,3},{3,2},{4,5},{5,4},{6,7},{7,6},{8,9},{9,8},{10,11... | collective-permute-start | bytes 786440 | tf_op jit(solution)/shard_map/back_halo/ppermute | solution.py:176

commit v3 on v2

--- a/solution.py
+++ b/solution.py
@@ -71,13 +71,15 @@
     return jnp.clip(t + offset[t, s] + 2 * 4, 0, 19)
 
 
-def mix_kernel(where, offset, far, near, own, a_hi, a_lo, partial, window):
-    rows = own.shape[1]
+def mix_kernel(
+    where, offset, far, far2, near, near2, own, other, a_hi, a_lo, partial, sent, window
+):
+    rows = own.shape[0]
     c = where[0]
-    for ref, shard in ((far, 4 * c), (near, 1 + 2 * c), (own, 2)):
+    for refs, shard in (((far, far2), 4 * c), ((near, near2), 1 + 2 * c), ((own, other), 2)):
         at = pl.multiple_of(shard * rows, rows)
         for k in range(2):
-            hi, lo = split(ref[k])
+            hi, lo = split(refs[k][...])
             window[pl.ds(at, rows), k * T : (k + 1) * T] = hi
             window[pl.ds(at, rows), (2 + k) * T : (3 + k) * T] = lo
     window[5 * rows :, :] = jnp.zeros((T, 4 * T), BF)
@@ -94,7 +96,9 @@
         total = wide[:, : 2 * T] + wide[:, 2 * T :] + dot(a_lo[t], b[:, : 2 * T])
         r = slice(t * T, (t + 1) * T)
         for k in range(2):
-            partial[k, r, :] = total[:, k * T : (k + 1) * T] + own[k, r, :] * first
+            value = total[:, k * T : (k + 1) * T] + (own, other)[k][r, :] * first
+            partial[k, r, :] = value
+            sent[1 - k, r, :] = value
 
 
 def layer_kernel(
@@ -103,15 +107,20 @@
 ):
     rows = gout.shape[0]
     c, zl = where[0], where[1]
-    arrived = ((mixed, weight, 0), (got, weight_got, 1 + c), (swapped, weight_swapped, 2 - c))
-    for ref, ref_w, back_by in arrived:
+    arrived = (
+        (mixed, weight, 0, c),
+        (got, weight_got, 1 + c, c),
+        (swapped, weight_swapped, 2 - c, 1 - c),
+    )
+    for ref, ref_w, back_by, core in arrived:
         chip = lax.rem(zl - back_by + 3, 3)
         for k in range(2):
+            block = chip * 2 + (core if k == 0 else 1 - core)
             hi, lo = split(ref[k])
-            m_hi[chip * 2 + k] = hi
-            m_lo[chip * 2 + k] = lo
+            m_hi[block] = hi
+            m_lo[block] = lo
             hi, lo = split(ref_w[k])
-            at = pl.ds(pl.multiple_of((chip * 2 + k) * T, T), T)
+            at = pl.ds(pl.multiple_of(block * T, T), T)
             w_hi[at, :] = hi
             w_lo[at, :] = lo
     back[...] = jnp.zeros_like(back)
@@ -148,7 +157,7 @@
     near[...] = back[pl.ds(pl.multiple_of((3 - 2 * c) * rows, rows), rows), :]
     mid = back[REACH * rows : (REACH + 1) * rows, :]
     center[...] = jnp.where(c == 0, mid[:, :T], mid[:, T:])
-    own = mixed[c]
+    own = mixed[0]
     m = jnp.concatenate([own[t * T : (t + 1) * T, :].T for t in range(rows // T)], axis=1)
     mh, ml = split(m)
     total = dot(mh, g_hi[...]) + dot(mh, g_lo[...]) + dot(ml, g_hi[...])
@@ -184,14 +193,21 @@
 
     with jax.named_scope("halo"):
         other = swap(features)
-        pair = jnp.where(c == 0, jnp.stack([features, other]), jnp.stack([other, features]))
-        near = by_core(pair, NODES, 1, -1)
+        near = by_core(features, NODES, 1, -1)
+        near2 = by_core(other, NODES, 1, -1)
         far = by_core(near, NODES, 1, -1)
+        far2 = by_core(near2, NODES, 1, -1)
     with jax.named_scope("weight_gather"):
         other_weight = swap(weight)
-        mine = jnp.where(c == 0, jnp.stack([weight, other_weight]), jnp.stack([other_weight, weight]))
-        mine, near = lax.optimization_barrier((mine, near))
-        weight_got = by_core(mine, "zl", 1, 2)
+        mine = jnp.stack([weight, other_weight])
+        odd = lax.axis_index("x") % 2
+        half = lax.dynamic_slice(mine, (0, odd * (T // 2), 0), (2, T // 2, 4 * T))
+        half, near2 = lax.optimization_barrier((half, near2))
+        half = by_core(half, "zl", 1, 2)
+        theirs = lax.ppermute(half, "x", [(i, i ^ 1) for i in range(4)])
+        weight_got = jnp.where(
+            odd == 0, jnp.concatenate([half, theirs], 1), jnp.concatenate([theirs, half], 1)
+        )
         weight_swapped = swap(weight_got)
 
     a_hi, a_lo, t_hl, rdeg = call(
@@ -209,18 +225,18 @@
         "prepare",
         8,
     )(tile_counts, tile_weights)
-    (partial,) = call(
+    partial, sent = call(
         mix_kernel,
-        [SMEM] * 2 + [VMEM] * 5,
-        [shape_of((2, rows, width))],
+        [SMEM] * 2 + [VMEM] * 8,
+        [shape_of((2, rows, width))] * 2,
         [pltpu.VMEM((5 * rows + T, 4 * T), BF)],
         2 * 10**8,
         3 * 10**6,
         "mix",
         12,
-    )(where, tile_offsets, far, near, pair, a_hi, a_lo)
+    )(where, tile_offsets, far, far2, near, near2, features, other, a_hi, a_lo)
     with jax.named_scope("mixed_gather"):
-        mixed = (partial + swap(partial)) * rdeg[None]
+        mixed = (partial + swap(sent)) * rdeg[None]
         got = by_core(mixed, "zl", 1, 2)
         swapped = swap(got)
     output, parts, q_far, q_near, center = call(

time: 182 us -> 174 us (0.956)
  waiting for transfers between devices: 69.1 us -> 40.7 us
  starting transfers between devices: 97.7 us -> 115 us
  local copies, waits for them, and re-layouts: 2.59 us -> 5.3 us
    ppermute x6 -> x8, waiting for transfers between devices: 65.2 us -> 33.1 us  [by_core(): return lax.ppermute(block, axes, route)]
    ppermute x6 -> x8, starting transfers between devices: 51.1 us -> 65.6 us  [by_core(): return lax.ppermute(block, axes, route)]
    ppermute x0 -> x1, waiting for transfers between devices: none -> 5.66 us  [body(): theirs = lax.ppermute(half, 'x', [(i, i ^ 1) for i in range(4)])]
    unnamed x12 -> x22, local copies, waits for them, and re-layouts: 0.66 us -> 3.37 us
    ppermute x0 -> x1, starting transfers between devices: none -> 1.91 us  [body(): theirs = lax.ppermute(half, 'x', [(i, i ^ 1) for i in range(4)])]
  transfers between devices with their start and end apart: 15 -> 18, of which waited for: 10 -> 8; matrix products, arithmetic and copies ran while one was open for 1% -> 2% of each run, Pallas kernels for 1% -> 1%
where the time goes in v3:
time: 174 us; the launch traced here: 173 us
  starting transfers between devices  115 us (66%)
  waiting for transfers between devices  40.7 us (23%)
  Pallas kernels  9.07 us (5%)
  local copies, waits for them, and re-layouts  5.3 us (3%)
  other arithmetic  2.2 us (1%)
    ppermute x8, starting transfers between devices, by_core(): return lax.ppermute(block, axes, route)  65.6 us
    ppermute x8, waiting for transfers between devices, by_core(): return lax.ppermute(block, axes, route)  33.1 us
    ppermute x6, starting transfers between devices, swap(): return lax.ppermute(block, 'c', [(0, 1), (1, 0)])  32.3 us
    all_to_all x1, starting transfers between devices, body(): held = jnp.sum(lax.all_to_all(held, 'zh', 0, 0), axis=0)  7.13 us
    pallas_call x1, Pallas kernels, body(): call(layer_kernel, [SMEM] * 2 + [VMEM] * 10, [shape_of((rows, 4 * T)), sh...  5.72 us
    ppermute x1, waiting for transfers between devices, body(): theirs = lax.ppermute(half, 'x', [(i, i ^ 1) for i in range(4)])  5.66 us
    all_to_all x1, starting transfers between devices, body(): held = jnp.sum(lax.all_to_all(parts, PLANE, 0, 0), axis=0)  4.01 us
    all_to_all x1, starting transfers between devices, body(): whole = lax.all_to_all(whole, PLANE, 0, 0)  3.87 us
  transfers between devices with their start and end apart: 18, of which 8 were waited for; matrix products, arithmetic and copies ran while one was open for 2% of the time, Pallas kernels for 1%

profile of v3, /device:TPU:1, one launch (start us, length us, event | category | flops | bytes accessed | tf_op | source)
XLA Modules:
  0.0 173.0 jit_solution(5164873477524399686)
XLA Ops:
  0.6 12.4 %collective-permute-start.2 = (f32[512,128]{1,0:T(8,128)}, f32[512,128]{1,0:T(8,128)S(1)}, u32[]{:S(2)}, u32[]{:S(2)}) collective-permute-start(f32[512,128]{1,0:T(8,128)} %own.1), channel_id=1, source_target_pairs={{0,1},{1,0},{2,3},{3,2},{4,5},{5,4},{6,7},{7,6},{8,9},{9,8},{10,11... | collective-permute-start | bytes 786440 | tf_op jit(solution)/shard_map/halo/ppermute | solution.py:185
  13.1 10.4 %collective-permute-start = (f32[512,128]{1,0:T(8,128)}, f32[512,128]{1,0:T(8,128)S(1)}, u32[]{:S(2)}, u32[]{:S(2)}) collective-permute-start(f32[512,128]{1,0:T(8,128)} %own.1), channel_id=1, source_target_pairs={{0,6},{1,763},{6,12},{7,1},{12,18},{13,7},{18,24},{19,13},{24,30},... | collective-permute-start | bytes 786440 | tf_op jit(solution)/shard_map/halo/ppermute | solution.py:181
  23.4 0.0 collective-permute-done.2.other
  23.5 2.8 %collective-permute-start.3 = (f32[512,128]{1,0:T(8,128)S(1)}, f32[512,128]{1,0:T(8,128)S(1)}, u32[]{:S(2)}, u32[]{:S(2)}) collective-permute-start(f32[512,128]{1,0:T(8,128)S(1)} %collective-permute-done.2.other), channel_id=1, source_target_pairs={{0,6},{1,763},{6,12},{7,1},{12,18},{13,7},{18,24},{19,13},{24,30},... | collective-permute-start | bytes 786440 | tf_op jit(solution)/shard_map/halo/ppermute | solution.py:181
  26.2 1.9 %collective-permute-start.5 = (f32[128,512]{1,0:T(8,128)}, f32[128,512]{1,0:T(8,128)S(1)}, u32[]{:S(2)}, u32[]{:S(2)}) collective-permute-start(f32[128,512]{1,0:T(8,128)} %param.8), channel_id=1, source_target_pairs={{0,1},{1,0},{2,3},{3,2},{4,5},{5,4},{6,7},{7,6},{8,9},{9,8},{10,11... | collective-permute-start | bytes 786440 | tf_op jit(solution)/shard_map/weight_gather/ppermute | solution.py:185
  28.2 2.8 %collective-permute-done.near = f32[512,128]{1,0:T(8,128)S(1)} collective-permute-done((f32[512,128]{1,0:T(8,128)}, f32[512,128]{1,0:T(8,128)S(1)}, u32[]{:S(2)}, u32[]{:S(2)}) %collective-permute-start) | collective-permute-done | bytes 262176 | tf_op jit(solution)/shard_map/halo/ppermute | solution.py:181
  31.0 11.0 %collective-permute-start.1 = (f32[512,128]{1,0:T(8,128)S(1)}, f32[512,128]{1,0:T(8,128)S(1)}, u32[]{:S(2)}, u32[]{:S(2)}) collective-permute-start(f32[512,128]{1,0:T(8,128)S(1)} %collective-permute-done.near), channel_id=1, source_target_pairs={{0,6},{1,763},{6,12},{7,1},{12,18},{13,7},{18,24},{19,13},{24,30},... | collective-permute-start | bytes 786440 | tf_op jit(solution)/shard_map/halo/ppermute | solution.py:181
  42.0 0.0 collective-permute-done.3.near2
  42.0 11.2 %collective-permute-start.4 = (f32[512,128]{1,0:T(8,128)S(1)}, f32[512,128]{1,0:T(8,128)S(1)}, u32[]{:S(2)}, u32[]{:S(2)}) collective-permute-start(f32[512,128]{1,0:T(8,128)S(1)} %collective-permute-done.3.near2), channel_id=1, source_target_pairs={{0,6},{1,763},{6,12},{7,1},{12,18},{13,7},{18,24},{19,13},{24,30},... | collective-permute-start | bytes 786440 | tf_op jit(solution)/shard_map/halo/ppermute | solution.py:181
  53.3 0.6 copy-done.3
  53.9 1.2 copy-done
  55.2 1.0 prepare.1
  56.2 0.1 pad_add_fusion.where
  56.3 0.7 copy-done.9
  57.0 6.6 %collective-permute-done.4.far2 = f32[512,128]{1,0:T(8,128)S(1)} collective-permute-done((f32[512,128]{1,0:T(8,128)S(1)}, f32[512,128]{1,0:T(8,128)S(1)}, u32[]{:S(2)}, u32[]{:S(2)}) %collective-permute-start.4) | collective-permute-done | bytes 262176 | tf_op jit(solution)/shard_map/halo/ppermute | solution.py:181
  63.6 1.6 mix.1
  65.2 1.9 %collective-permute-start.6 = (f32[2,512,128]{2,1,0:T(8,128)S(1)}, f32[2,512,128]{2,1,0:T(8,128)S(1)}, u32[]{:S(2)}, u32[]{:S(2)}) collective-permute-start(f32[2,512,128]{2,1,0:T(8,128)S(1)} %get-tuple-element.23), channel_id=1, source_target_pairs={{0,1},{1,0},{2,3},{3,2},{4,5},{5,4},{6,7},{7,6},{8,9},{9,8},{10,11... | collective-permute-start | bytes 1572872 | tf_op jit(solution)/shard_map/mixed_gather/ppermute | solution.py:185
  67.1 3.9 %collective-permute-start.9 = (f32[2,64,512]{2,1,0:T(8,128)S(1)}, f32[2,64,512]{2,1,0:T(8,128)}, u32[]{:S(2)}, u32[]{:S(2)}) collective-permute-start(f32[2,64,512]{2,1,0:T(8,128)S(1)} %fusion), channel_id=1, source_target_pairs={{0,2},{1,5},{2,4},{3,1},{4,0},{5,3},{6,8},{7,11},{8,10},{9,7},{10,... | collective-permute-start | bytes 786440 | tf_op jit(solution)/shard_map/weight_gather/ppermute | solution.py:181
  71.0 0.1 add_multiply_fusion.mixed
  71.1 2.1 %collective-permute-start.7 = (f32[2,512,128]{2,1,0:T(8,128)S(1)}, f32[2,512,128]{2,1,0:T(8,128)S(1)}, u32[]{:S(2)}, u32[]{:S(2)}) collective-permute-start(f32[2,512,128]{2,1,0:T(8,128)S(1)} %add_multiply_fusion.mixed), channel_id=1, source_target_pairs={{0,2},{1,5},{2,4},{3,1},{4,0},{5,3},{6,8},{7,11},{8,10},{9,7},{10,... | collective-permute-start | bytes 1572872 | tf_op jit(solution)/shard_map/mixed_gather/ppermute | solution.py:181
  73.2 3.8 %collective-permute-done.9 = f32[2,64,512]{2,1,0:T(8,128)} collective-permute-done((f32[2,64,512]{2,1,0:T(8,128)S(1)}, f32[2,64,512]{2,1,0:T(8,128)}, u32[]{:S(2)}, u32[]{:S(2)}) %collective-permute-start.9) | collective-permute-done | bytes 262176 | tf_op jit(solution)/shard_map/weight_gather/ppermute | solution.py:181
  77.0 1.9 %collective-permute-start.10 = (f32[2,64,512]{2,1,0:T(8,128)}, f32[2,64,512]{2,1,0:T(8,128)S(1)}, u32[]{:S(2)}, u32[]{:S(2)}) collective-permute-start(f32[2,64,512]{2,1,0:T(8,128)} %collective-permute-done.9), channel_id=1, source_target_pairs={{0,192},{192,0},{384,576},{576,384},{1,193},{193,1},{385,577},{577... | collective-permute-start | bytes 786440 | tf_op jit(solution)/shard_map/weight_gather/ppermute | solution.py:207
  79.0 0.0 copy-start.10
  79.0 0.0 copy-start.4
  79.0 5.7 %collective-permute-done.10 = f32[2,64,512]{2,1,0:T(8,128)S(1)} collective-permute-done((f32[2,64,512]{2,1,0:T(8,128)}, f32[2,64,512]{2,1,0:T(8,128)S(1)}, u32[]{:S(2)}, u32[]{:S(2)}) %collective-permute-start.10) | collective-permute-done | bytes 262176 | tf_op jit(solution)/shard_map/weight_gather/ppermute | solution.py:207
  84.7 1.1 maximum_select_fusion.weight_got
  85.7 5.4 %collective-permute-start.11 = (f32[2,128,512]{2,1,0:T(8,128)S(1)}, f32[2,128,512]{2,1,0:T(8,128)S(1)}, u32[]{:S(2)}, u32[]{:S(2)}) collective-permute-start(f32[2,128,512]{2,1,0:T(8,128)S(1)} %maximum_select_fusion.weight_got), channel_id=1, source_target_pairs={{0,1},{1,0},{2,3},{3,2},{4,5},{5,4},{6,7},{7,6},{8,9},{9,8},{10,11... | collective-permute-start | bytes 1572872 | tf_op jit(solution)/shard_map/weight_gather/ppermute | solution.py:185
  91.2 0.0 collective-permute-done.7.got
  91.2 1.9 %collective-permute-start.8 = (f32[2,512,128]{2,1,0:T(8,128)S(1)}, f32[2,512,128]{2,1,0:T(8,128)S(1)}, u32[]{:S(2)}, u32[]{:S(2)}) collective-permute-start(f32[2,512,128]{2,1,0:T(8,128)S(1)} %collective-permute-done.7.got), channel_id=1, source_target_pairs={{0,1},{1,0},{2,3},{3,2},{4,5},{5,4},{6,7},{7,6},{8,9},{9,8},{10,11... | collective-permute-start | bytes 1572872 | tf_op jit(solution)/shard_map/mixed_gather/ppermute | solution.py:185
  93.2 0.0 copy-start.7
  93.2 1.8 %collective-permute-done.8.swapped = f32[2,512,128]{2,1,0:T(8,128)S(1)} collective-permute-done((f32[2,512,128]{2,1,0:T(8,128)S(1)}, f32[2,512,128]{2,1,0:T(8,128)S(1)}, u32[]{:S(2)}, u32[]{:S(2)}) %collective-permute-start.8) | collective-permute-done | bytes 524320 | tf_op jit(solution)/shard_map/mixed_gather/ppermute | solution.py:185
  95.0 5.7 %layer.1 = (f32[512,512]{1,0:T(8,128)}, f32[32,24,128]{2,1,0:T(8,128)}, f32[512,256]{1,0:T(8,128)S(1)}, f32[512,256]{1,0:T(8,128)S(1)}, f32[512,128]{1,0:T(8,128)S(1)}) custom-call(s32[2]{0:T(128)S(1)} %pad_add_fusion.where, s32[4,4]{1,0:T(4,128)S(1)} %copy-done.2, f32[2,512,128]{2,1,0:T(8,128)S(1)} %add_multiply_fusion.mixed, ...), custom_call_target="tpu_custom_call" | custom-call | flops 1500000000 | bytes 10000000 | tf_op jit(solution)/shard_map/layer/pallas_call | solution.py:242
  100.7 0.8 copy-done.5
  101.5 4.0 %all-to-all-start = ((f32[32,24,128]{2,1,0:T(8,128)}), f32[32,24,128]{2,1,0:T(8,128)S(1)}, u32[]{:S(2)}, u32[]{:S(2)}) async-start(f32[32,24,128]{2,1,0:T(8,128)} %get-tuple-element.31), calls=%async_computation | async-start | bytes 786432 | tf_op jit(solution)/shard_map/nodes_sum/all_to_all | solution.py:266
  105.5 13.1 %collective-permute-start.12 = (f32[512,256]{1,0:T(8,128)S(1)}, f32[512,256]{1,0:T(8,128)S(1)}, u32[]{:S(2)}, u32[]{:S(2)}) collective-permute-start(f32[512,256]{1,0:T(8,128)S(1)} %copy-done.6), channel_id=1, source_target_pairs={{0,6},{1,763},{6,12},{7,1},{12,18},{13,7},{18,24},{19,13},{24,30},... | collective-permute-start | bytes 1572872 | tf_op jit(solution)/shard_map/back_halo/ppermute | solution.py:181
  118.7 0.6 broadcast_in_dim.4
  119.3 7.1 %all-to-all-start.1 = ((f32[4,24,128]{2,1,0:T(8,128)}), f32[4,24,128]{2,1,0:T(8,128)S(1)}, u32[]{:S(2)}, u32[]{:S(2)}) async-start(f32[4,24,128]{2,1,0:T(8,128)} %broadcast_in_dim.4), calls=%async_computation.1 | async-start | bytes 98304 | tf_op jit(solution)/shard_map/nodes_sum/all_to_all | solution.py:271
  126.5 9.9 %collective-permute-done.12 = f32[512,256]{1,0:T(8,128)S(1)} collective-permute-done((f32[512,256]{1,0:T(8,128)S(1)}, f32[512,256]{1,0:T(8,128)S(1)}, u32[]{:S(2)}, u32[]{:S(2)}) %collective-permute-start.12) | collective-permute-done | bytes 524320 | tf_op jit(solution)/shard_map/back_halo/ppermute | solution.py:181
  136.3 0.1 add.22
  136.4 0.1 all-to-all-done.1
  136.5 11.1 %collective-permute-start.13 = (f32[512,256]{1,0:T(8,128)S(1)}, f32[512,256]{1,0:T(8,128)S(1)}, u32[]{:S(2)}, u32[]{:S(2)}) collective-permute-start(f32[512,256]{1,0:T(8,128)S(1)} %add.22), channel_id=1, source_target_pairs={{0,6},{1,763},{6,12},{7,1},{12,18},{13,7},{18,24},{19,13},{24,30},... | collective-permute-start | bytes 1572872 | tf_op jit(solution)/shard_map/back_halo/ppermute | solution.py:181
  147.6 0.7 broadcast_in_dim.5
  148.3 3.9 %all-to-all-start.2 = ((f32[32,16,128]{2,1,0:T(8,128)}), f32[32,16,128]{2,1,0:T(8,128)S(1)}, u32[]{:S(2)}, u32[]{:S(2)}) async-start(f32[32,16,128]{2,1,0:T(8,128)} %broadcast_in_dim.5), calls=%async_computation.2 | async-start | bytes 524288 | tf_op jit(solution)/shard_map/nodes_sum/all_to_all | solution.py:280
  152.2 10.1 %collective-permute-done.13 = f32[512,256]{1,0:T(8,128)S(1)} collective-permute-done((f32[512,256]{1,0:T(8,128)S(1)}, f32[512,256]{1,0:T(8,128)S(1)}, u32[]{:S(2)}, u32[]{:S(2)}) %collective-permute-start.13) | collective-permute-done | bytes 524320 | tf_op jit(solution)/shard_map/back_halo/ppermute | solution.py:181
  162.3 8.7 %collective-permute-start.14 = (f32[512,128]{1,0:T(8,128)S(1)}, f32[512,128]{1,0:T(8,128)S(1)}, u32[]{:S(2)}, u32[]{:S(2)}) collective-permute-start(f32[512,128]{1,0:T(8,128)S(1)} %slice_select_fusion), channel_id=1, source_target_pairs={{0,1},{1,0},{2,3},{3,2},{4,5},{5,4},{6,7},{7,6},{8,9},{9,8},{10,11... | collective-permute-start | bytes 786440 | tf_op jit(solution)/shard_map/back_halo/ppermute | solution.py:185
  171.0 0.6 slice_bitcast_fusion
  171.6 0.7 arrange.1
  172.3 0.8 add_add_fusion
  (28 shorter events, 0.2 us)
Async XLA Ops:
  0.6 22.8 %collective-permute-start.2 = (f32[512,128]{1,0:T(8,128)}, f32[512,128]{1,0:T(8,128)S(1)}, u32[]{:S(2)}, u32[]{:S(2)}) collective-permute-start(f32[512,128]{1,0:T(8,128)} %own.1), channel_id=1, source_target_pairs={{0,1},{1,0},{2,3},{3,2},{4,5},{5,4},{6,7},{7,6},{8,9},{9,8},{10,11... | collective-permute-start | bytes 786440 | tf_op jit(solution)/shard_map/halo/ppermute | solution.py:185
  13.1 17.9 %collective-permute-start = (f32[512,128]{1,0:T(8,128)}, f32[512,128]{1,0:T(8,128)S(1)}, u32[]{:S(2)}, u32[]{:S(2)}) collective-permute-start(f32[512,128]{1,0:T(8,128)} %own.1), channel_id=1, source_target_pairs={{0,6},{1,763},{6,12},{7,1},{12,18},{13,7},{18,24},{19,13},{24,30},... | collective-permute-start | bytes 786440 | tf_op jit(solution)/shard_map/halo/ppermute | solution.py:181
  23.5 18.5 %collective-permute-start.3 = (f32[512,128]{1,0:T(8,128)S(1)}, f32[512,128]{1,0:T(8,128)S(1)}, u32[]{:S(2)}, u32[]{:S(2)}) collective-permute-start(f32[512,128]{1,0:T(8,128)S(1)} %collective-permute-done.2.other), channel_id=1, source_target_pairs={{0,6},{1,763},{6,12},{7,1},{12,18},{13,7},{18,24},{19,13},{24,30},... | collective-permute-start | bytes 786440 | tf_op jit(solution)/shard_map/halo/ppermute | solution.py:181
  26.2 30.0 %collective-permute-start.5 = (f32[128,512]{1,0:T(8,128)}, f32[128,512]{1,0:T(8,128)S(1)}, u32[]{:S(2)}, u32[]{:S(2)}) collective-permute-start(f32[128,512]{1,0:T(8,128)} %param.8), channel_id=1, source_target_pairs={{0,1},{1,0},{2,3},{3,2},{4,5},{5,4},{6,7},{7,6},{8,9},{9,8},{10,11... | collective-permute-start | bytes 786440 | tf_op jit(solution)/shard_map/weight_gather/ppermute | solution.py:185
  31.0 26.0 %collective-permute-start.1 = (f32[512,128]{1,0:T(8,128)S(1)}, f32[512,128]{1,0:T(8,128)S(1)}, u32[]{:S(2)}, u32[]{:S(2)}) collective-permute-start(f32[512,128]{1,0:T(8,128)S(1)} %collective-permute-done.near), channel_id=1, source_target_pairs={{0,6},{1,763},{6,12},{7,1},{12,18},{13,7},{18,24},{19,13},{24,30},... | collective-permute-start | bytes 786440 | tf_op jit(solution)/shard_map/halo/ppermute | solution.py:181
  42.0 21.6 %collective-permute-start.4 = (f32[512,128]{1,0:T(8,128)S(1)}, f32[512,128]{1,0:T(8,128)S(1)}, u32[]{:S(2)}, u32[]{:S(2)}) collective-permute-start(f32[512,128]{1,0:T(8,128)S(1)} %collective-permute-done.3.near2), channel_id=1, source_target_pairs={{0,6},{1,763},{6,12},{7,1},{12,18},{13,7},{18,24},{19,13},{24,30},... | collective-permute-start | bytes 786440 | tf_op jit(solution)/shard_map/halo/ppermute | solution.py:181
  53.3 0.7 copy-start.3
  53.9 1.2 copy-start
  55.1 1.1 copy-start.8
  56.3 0.7 copy-start.9
  56.3 7.3 %copy-start.1 = (f32[512,128]{1,0:T(8,128)S(1)}, f32[512,128]{1,0:T(8,128)}, u32[]{:S(2)}) copy-start(f32[512,128]{1,0:T(8,128)} %own.1) | copy-start | bytes 786436
  57.0 6.6 %copy-start.2 = (s32[4,4]{1,0:T(4,128)S(1)}, s32[4,4]{1,0:T(4,128)}, u32[]{:S(2)}) copy-start(s32[4,4]{1,0:T(4,128)} %offset.3) | copy-start | bytes 196
  65.2 5.8 %collective-permute-start.6 = (f32[2,512,128]{2,1,0:T(8,128)S(1)}, f32[2,512,128]{2,1,0:T(8,128)S(1)}, u32[]{:S(2)}, u32[]{:S(2)}) collective-permute-start(f32[2,512,128]{2,1,0:T(8,128)S(1)} %get-tuple-element.23), channel_id=1, source_target_pairs={{0,1},{1,0},{2,3},{3,2},{4,5},{5,4},{6,7},{7,6},{8,9},{9,8},{10,11... | collective-permute-start | bytes 1572872 | tf_op jit(solution)/shard_map/mixed_gather/ppermute | solution.py:185
  67.1 9.9 %collective-permute-start.9 = (f32[2,64,512]{2,1,0:T(8,128)S(1)}, f32[2,64,512]{2,1,0:T(8,128)}, u32[]{:S(2)}, u32[]{:S(2)}) collective-permute-start(f32[2,64,512]{2,1,0:T(8,128)S(1)} %fusion), channel_id=1, source_target_pairs={{0,2},{1,5},{2,4},{3,1},{4,0},{5,3},{6,8},{7,11},{8,10},{9,7},{10,... | collective-permute-start | bytes 786440 | tf_op jit(solution)/shard_map/weight_gather/ppermute | solution.py:181
  71.1 20.1 %collective-permute-start.7 = (f32[2,512,128]{2,1,0:T(8,128)S(1)}, f32[2,512,128]{2,1,0:T(8,128)S(1)}, u32[]{:S(2)}, u32[]{:S(2)}) collective-permute-start(f32[2,512,128]{2,1,0:T(8,128)S(1)} %add_multiply_fusion.mixed), channel_id=1, source_target_pairs={{0,2},{1,5},{2,4},{3,1},{4,0},{5,3},{6,8},{7,11},{8,10},{9,7},{10,... | collective-permute-start | bytes 1572872 | tf_op jit(solution)/shard_map/mixed_gather/ppermute | solution.py:181
  77.0 7.6 %collective-permute-start.10 = (f32[2,64,512]{2,1,0:T(8,128)}, f32[2,64,512]{2,1,0:T(8,128)S(1)}, u32[]{:S(2)}, u32[]{:S(2)}) collective-permute-start(f32[2,64,512]{2,1,0:T(8,128)} %collective-permute-done.9), channel_id=1, source_target_pairs={{0,192},{192,0},{384,576},{576,384},{1,193},{193,1},{385,577},{577... | collective-permute-start | bytes 786440 | tf_op jit(solution)/shard_map/weight_gather/ppermute | solution.py:207
  79.0 14.1 %copy-start.10 = (f32[128,512]{1,0:T(8,128)S(1)}, f32[128,512]{1,0:T(8,128)}, u32[]{:S(2)}) copy-start(f32[128,512]{1,0:T(8,128)} %copy-done.9) | copy-start | bytes 786436
  79.0 16.0 %copy-start.4 = (f32[512,512]{1,0:T(8,128)S(1)}, f32[512,512]{1,0:T(8,128)}, u32[]{:S(2)}) copy-start(f32[512,512]{1,0:T(8,128)} %gout.1) | copy-start | bytes 3145732
  85.7 7.4 %collective-permute-start.11 = (f32[2,128,512]{2,1,0:T(8,128)S(1)}, f32[2,128,512]{2,1,0:T(8,128)S(1)}, u32[]{:S(2)}, u32[]{:S(2)}) collective-permute-start(f32[2,128,512]{2,1,0:T(8,128)S(1)} %maximum_select_fusion.weight_got), channel_id=1, source_target_pairs={{0,1},{1,0},{2,3},{3,2},{4,5},{5,4},{6,7},{7,6},{8,9},{9,8},{10,11... | collective-permute-start | bytes 1572872 | tf_op jit(solution)/shard_map/weight_gather/ppermute | solution.py:185
  91.2 3.8 %collective-permute-start.8 = (f32[2,512,128]{2,1,0:T(8,128)S(1)}, f32[2,512,128]{2,1,0:T(8,128)S(1)}, u32[]{:S(2)}, u32[]{:S(2)}) collective-permute-start(f32[2,512,128]{2,1,0:T(8,128)S(1)} %collective-permute-done.7.got), channel_id=1, source_target_pairs={{0,1},{1,0},{2,3},{3,2},{4,5},{5,4},{6,7},{7,6},{8,9},{9,8},{10,11... | collective-permute-start | bytes 1572872 | tf_op jit(solution)/shard_map/mixed_gather/ppermute | solution.py:185
  93.2 1.8 %copy-start.7 = (f32[512]{0:T(512)S(1)}, f32[512]{0:T(512)}, u32[]{:S(2)}) copy-start(f32[512]{0:T(512)} %param.9) | copy-start | bytes 6148
  100.7 0.8 copy-start.5
  101.5 4.0 %copy-start.6 = (f32[512,256]{1,0:T(8,128)S(1)}, f32[512,256]{1,0:T(8,128)}, u32[]{:S(2)}) copy-start(f32[512,256]{1,0:T(8,128)} %copy-done.5) | copy-start | bytes 1572868
  101.5 17.1 %all-to-all-start = ((f32[32,24,128]{2,1,0:T(8,128)}), f32[32,24,128]{2,1,0:T(8,128)S(1)}, u32[]{:S(2)}, u32[]{:S(2)}) async-start(f32[32,24,128]{2,1,0:T(8,128)} %get-tuple-element.31), calls=%async_computation | async-start | bytes 786432 | tf_op jit(solution)/shard_map/nodes_sum/all_to_all | solution.py:266
  105.5 30.8 %collective-permute-start.12 = (f32[512,256]{1,0:T(8,128)S(1)}, f32[512,256]{1,0:T(8,128)S(1)}, u32[]{:S(2)}, u32[]{:S(2)}) collective-permute-start(f32[512,256]{1,0:T(8,128)S(1)} %copy-done.6), channel_id=1, source_target_pairs={{0,6},{1,763},{6,12},{7,1},{12,18},{13,7},{18,24},{19,13},{24,30},... | collective-permute-start | bytes 1572872 | tf_op jit(solution)/shard_map/back_halo/ppermute | solution.py:181
  119.3 17.1 %all-to-all-start.1 = ((f32[4,24,128]{2,1,0:T(8,128)}), f32[4,24,128]{2,1,0:T(8,128)S(1)}, u32[]{:S(2)}, u32[]{:S(2)}) async-start(f32[4,24,128]{2,1,0:T(8,128)} %broadcast_in_dim.4), calls=%async_computation.1 | async-start | bytes 98304 | tf_op jit(solution)/shard_map/nodes_sum/all_to_all | solution.py:271
  136.5 25.7 %collective-permute-start.13 = (f32[512,256]{1,0:T(8,128)S(1)}, f32[512,256]{1,0:T(8,128)S(1)}, u32[]{:S(2)}, u32[]{:S(2)}) collective-permute-start(f32[512,256]{1,0:T(8,128)S(1)} %add.22), channel_id=1, source_target_pairs={{0,6},{1,763},{6,12},{7,1},{12,18},{13,7},{18,24},{19,13},{24,30},... | collective-permute-start | bytes 1572872 | tf_op jit(solution)/shard_map/back_halo/ppermute | solution.py:181
  148.3 23.3 %all-to-all-start.2 = ((f32[32,16,128]{2,1,0:T(8,128)}), f32[32,16,128]{2,1,0:T(8,128)S(1)}, u32[]{:S(2)}, u32[]{:S(2)}) async-start(f32[32,16,128]{2,1,0:T(8,128)} %broadcast_in_dim.5), calls=%async_computation.2 | async-start | bytes 524288 | tf_op jit(solution)/shard_map/nodes_sum/all_to_all | solution.py:280
  162.3 10.0 %collective-permute-start.14 = (f32[512,128]{1,0:T(8,128)S(1)}, f32[512,128]{1,0:T(8,128)S(1)}, u32[]{:S(2)}, u32[]{:S(2)}) collective-permute-start(f32[512,128]{1,0:T(8,128)S(1)} %slice_select_fusion), channel_id=1, source_target_pairs={{0,1},{1,0},{2,3},{3,2},{4,5},{5,4},{6,7},{7,6},{8,9},{9,8},{10,11... | collective-permute-start | bytes 786440 | tf_op jit(solution)/shard_map/back_halo/ppermute | solution.py:185

commit v4 on v3

--- a/solution.py
+++ b/solution.py
@@ -103,7 +103,7 @@
 
 def layer_kernel(
     where, offset, mixed, got, swapped, weight, weight_got, weight_swapped, bias, gout, rdeg, t_hl,
-    output, parts, far, near, center, m_hi, m_lo, w_hi, w_lo, s_hi, s_lo, g_hi, g_lo, back,
+    output, parts, far, near, beyond, center, m_hi, m_lo, w_hi, w_lo, s_hi, s_lo, g_hi, g_lo, back,
 ):
     rows = gout.shape[0]
     c, zl = where[0], where[1]
@@ -154,7 +154,9 @@
             at = pl.multiple_of(window_index(offset, t, s) * T, T)
             back[pl.ds(at, T), :] += contrib[s * T : (s + 1) * T, :]
     far[...] = back[pl.ds(pl.multiple_of((4 - 4 * c) * rows, rows), rows), :]
-    near[...] = back[pl.ds(pl.multiple_of((3 - 2 * c) * rows, rows), rows), :]
+    side = back[pl.ds(pl.multiple_of((3 - 2 * c) * rows, rows), rows), :]
+    near[...] = jnp.where(c == 0, side[:, :T], side[:, T:])
+    beyond[...] = jnp.where(c == 0, side[:, T:], side[:, :T])
     mid = back[REACH * rows : (REACH + 1) * rows, :]
     center[...] = jnp.where(c == 0, mid[:, :T], mid[:, T:])
     own = mixed[0]
@@ -174,9 +176,13 @@
         out[(p // 4) * 16 : (p // 4 + 1) * 16, (p % 4) * T : (p % 4 + 1) * T] = pieces[p]
 
 
-def by_core(block, axis, first, second):
+def by_core(block, axis, first, second, cross=False):
     n = lax.axis_size(axis)
-    route = [(2 * i + c, 2 * ((i + d) % n) + c) for i in range(n) for c, d in ((0, first), (1, second))]
+    route = [
+        (2 * i + c, 2 * ((i + d) % n) + (1 - c if cross else c))
+        for i in range(n)
+        for c, d in ((0, first), (1, second))
+    ]
     axes = (axis if isinstance(axis, tuple) else (axis,)) + ("c",)
     return lax.ppermute(block, axes, route)
 
@@ -239,10 +245,10 @@
         mixed = (partial + swap(sent)) * rdeg[None]
         got = by_core(mixed, "zl", 1, 2)
         swapped = swap(got)
-    output, parts, q_far, q_near, center = call(
+    output, parts, q_far, q_near, q_other, center = call(
         layer_kernel,
         [SMEM] * 2 + [VMEM] * 10,
-        [shape_of((rows, 4 * T)), shape_of((32, 24, T))] + [shape_of((rows, 2 * width))] * 2 + [shape_of((rows, width))],
+        [shape_of((rows, 4 * T)), shape_of((32, 24, T))] + [shape_of((rows, 2 * width))] + [shape_of((rows, width))] * 3,
         [
             pltpu.VMEM((6, rows, T), BF),
             pltpu.VMEM((6, rows, T), BF),
@@ -270,10 +276,10 @@
         held = jnp.broadcast_to(held[None], (4, 24, T))
         held = jnp.sum(lax.all_to_all(held, "zh", 0, 0), axis=0)
     with jax.named_scope("back_halo"):
-        came, held = lax.optimization_barrier((q_near + came, held))
-        came = by_core(came, NODES, 1, -1)
-        lent = swap(jnp.where(c == 0, came[:, width:], came[:, :width]))
-        grad_features = center + (jnp.where(c == 0, came[:, :width], came[:, width:]) + lent)
+        came, held = lax.optimization_barrier((came, held))
+        kept = q_near + jnp.where(c == 0, came[:, :width], came[:, width:])
+        lent = q_other + jnp.where(c == 0, came[:, width:], came[:, :width])
+        grad_features = center + (by_core(kept, NODES, 1, -1) + by_core(lent, NODES, 1, -1, True))
     with jax.named_scope("nodes_sum"):
         grad_bias = held[16:20].reshape(-1)
         whole = jnp.broadcast_to(held[None, :16], (32, 16, T))

time: 174 us -> 170 us (0.977)
  starting transfers between devices: 115 us -> 108 us
  waiting for transfers between devices: 40.7 us -> 43.5 us
    ppermute x8 -> x9, waiting for transfers between devices: 33.1 us -> 20.7 us  [by_core(): return lax.ppermute(block, axes, route)]
    all_to_all x1, waiting for transfers between devices: 0.07 us -> 9.99 us  [body(): held = jnp.sum(lax.all_to_all(held, 'zh', 0, 0), axis=0)]
    ppermute x6 -> x5, starting transfers between devices: 32.3 us -> 23.6 us  [swap(): return lax.ppermute(block, 'c', [(0, 1), (1, 0)])]
    all_to_all x1, waiting for transfers between devices: 0.01 us -> 5.31 us  [body(): whole = lax.all_to_all(whole, PLANE, 0, 0)]
    ppermute x8 -> x9, starting transfers between devices: 65.6 us -> 67.4 us  [by_core(): return lax.ppermute(block, axes, route)]
where the time goes in v4:
time: 170 us; the launch traced here: 169 us
  starting transfers between devices  108 us (64%)
  waiting for transfers between devices  43.5 us (26%)
  Pallas kernels  9.1 us (5%)
  local copies, waits for them, and re-layouts  5.31 us (3%)
  other arithmetic  2.15 us (1%)
    ppermute x9, starting transfers between devices, by_core(): return lax.ppermute(block, axes, route)  67.4 us
    ppermute x5, starting transfers between devices, swap(): return lax.ppermute(block, 'c', [(0, 1), (1, 0)])  23.6 us
    ppermute x9, waiting for transfers between devices, by_core(): return lax.ppermute(block, axes, route)  20.7 us
    all_to_all x1, waiting for transfers between devices, body(): held = jnp.sum(lax.all_to_all(held, 'zh', 0, 0), axis=0)  9.99 us
    all_to_all x1, starting transfers between devices, body(): held = jnp.sum(lax.all_to_all(held, 'zh', 0, 0), axis=0)  7.13 us
    pallas_call x1, Pallas kernels, body(): call(layer_kernel, [SMEM] * 2 + [VMEM] * 10, [shape_of((rows, 4 * T)), sh...  5.74 us
    ppermute x1, waiting for transfers between devices, body(): theirs = lax.ppermute(half, 'x', [(i, i ^ 1) for i in range(4)])  5.66 us
    all_to_all x1, waiting for transfers between devices, body(): whole = lax.all_to_all(whole, PLANE, 0, 0)  5.31 us
  transfers between devices with their start and end apart: 18, of which 8 were waited for; matrix products, arithmetic and copies ran while one was open for 2% of the time, Pallas kernels for 1%

profile of v4, /device:TPU:1, one launch (start us, length us, event | category | flops | bytes accessed | tf_op | source)
XLA Modules:
  0.0 168.9 jit_solution(2373425319069777378)
XLA Ops:
  0.6 12.4 %collective-permute-start.2 = (f32[512,128]{1,0:T(8,128)}, f32[512,128]{1,0:T(8,128)S(1)}, u32[]{:S(2)}, u32[]{:S(2)}) collective-permute-start(f32[512,128]{1,0:T(8,128)} %own.1), channel_id=1, source_target_pairs={{0,1},{1,0},{2,3},{3,2},{4,5},{5,4},{6,7},{7,6},{8,9},{9,8},{10,11... | collective-permute-start | bytes 786440 | tf_op jit(solution)/shard_map/halo/ppermute | solution.py:191
  13.1 10.4 %collective-permute-start = (f32[512,128]{1,0:T(8,128)}, f32[512,128]{1,0:T(8,128)S(1)}, u32[]{:S(2)}, u32[]{:S(2)}) collective-permute-start(f32[512,128]{1,0:T(8,128)} %own.1), channel_id=1, source_target_pairs={{0,6},{1,763},{6,12},{7,1},{12,18},{13,7},{18,24},{19,13},{24,30},... | collective-permute-start | bytes 786440 | tf_op jit(solution)/shard_map/halo/ppermute | solution.py:187
  23.4 0.0 collective-permute-done.2.other
  23.5 2.8 %collective-permute-start.3 = (f32[512,128]{1,0:T(8,128)S(1)}, f32[512,128]{1,0:T(8,128)S(1)}, u32[]{:S(2)}, u32[]{:S(2)}) collective-permute-start(f32[512,128]{1,0:T(8,128)S(1)} %collective-permute-done.2.other), channel_id=1, source_target_pairs={{0,6},{1,763},{6,12},{7,1},{12,18},{13,7},{18,24},{19,13},{24,30},... | collective-permute-start | bytes 786440 | tf_op jit(solution)/shard_map/halo/ppermute | solution.py:187
  26.2 1.9 %collective-permute-start.5 = (f32[128,512]{1,0:T(8,128)}, f32[128,512]{1,0:T(8,128)S(1)}, u32[]{:S(2)}, u32[]{:S(2)}) collective-permute-start(f32[128,512]{1,0:T(8,128)} %param.8), channel_id=1, source_target_pairs={{0,1},{1,0},{2,3},{3,2},{4,5},{5,4},{6,7},{7,6},{8,9},{9,8},{10,11... | collective-permute-start | bytes 786440 | tf_op jit(solution)/shard_map/weight_gather/ppermute | solution.py:191
  28.2 2.8 %collective-permute-done.near = f32[512,128]{1,0:T(8,128)S(1)} collective-permute-done((f32[512,128]{1,0:T(8,128)}, f32[512,128]{1,0:T(8,128)S(1)}, u32[]{:S(2)}, u32[]{:S(2)}) %collective-permute-start) | collective-permute-done | bytes 262176 | tf_op jit(solution)/shard_map/halo/ppermute | solution.py:187
  31.0 11.0 %collective-permute-start.1 = (f32[512,128]{1,0:T(8,128)S(1)}, f32[512,128]{1,0:T(8,128)S(1)}, u32[]{:S(2)}, u32[]{:S(2)}) collective-permute-start(f32[512,128]{1,0:T(8,128)S(1)} %collective-permute-done.near), channel_id=1, source_target_pairs={{0,6},{1,763},{6,12},{7,1},{12,18},{13,7},{18,24},{19,13},{24,30},... | collective-permute-start | bytes 786440 | tf_op jit(solution)/shard_map/halo/ppermute | solution.py:187
  42.0 0.0 collective-permute-done.3.near2
  42.0 11.2 %collective-permute-start.4 = (f32[512,128]{1,0:T(8,128)S(1)}, f32[512,128]{1,0:T(8,128)S(1)}, u32[]{:S(2)}, u32[]{:S(2)}) collective-permute-start(f32[512,128]{1,0:T(8,128)S(1)} %collective-permute-done.3.near2), channel_id=1, source_target_pairs={{0,6},{1,763},{6,12},{7,1},{12,18},{13,7},{18,24},{19,13},{24,30},... | collective-permute-start | bytes 786440 | tf_op jit(solution)/shard_map/halo/ppermute | solution.py:187
  53.3 0.6 copy-done.3
  53.9 1.2 copy-done
  55.2 1.0 prepare.1
  56.2 0.1 pad_add_fusion.where
  56.3 0.7 copy-done.9
  57.0 6.6 %collective-permute-done.4.far2 = f32[512,128]{1,0:T(8,128)S(1)} collective-permute-done((f32[512,128]{1,0:T(8,128)S(1)}, f32[512,128]{1,0:T(8,128)S(1)}, u32[]{:S(2)}, u32[]{:S(2)}) %collective-permute-start.4) | collective-permute-done | bytes 262176 | tf_op jit(solution)/shard_map/halo/ppermute | solution.py:187
  63.6 1.6 mix.1
  65.2 1.9 %collective-permute-start.6 = (f32[2,512,128]{2,1,0:T(8,128)S(1)}, f32[2,512,128]{2,1,0:T(8,128)S(1)}, u32[]{:S(2)}, u32[]{:S(2)}) collective-permute-start(f32[2,512,128]{2,1,0:T(8,128)S(1)} %get-tuple-element.24), channel_id=1, source_target_pairs={{0,1},{1,0},{2,3},{3,2},{4,5},{5,4},{6,7},{7,6},{8,9},{9,8},{10,11... | collective-permute-start | bytes 1572872 | tf_op jit(solution)/shard_map/mixed_gather/ppermute | solution.py:191
  67.1 3.9 %collective-permute-start.9 = (f32[2,64,512]{2,1,0:T(8,128)S(1)}, f32[2,64,512]{2,1,0:T(8,128)}, u32[]{:S(2)}, u32[]{:S(2)}) collective-permute-start(f32[2,64,512]{2,1,0:T(8,128)S(1)} %fusion), channel_id=1, source_target_pairs={{0,2},{1,5},{2,4},{3,1},{4,0},{5,3},{6,8},{7,11},{8,10},{9,7},{10,... | collective-permute-start | bytes 786440 | tf_op jit(solution)/shard_map/weight_gather/ppermute | solution.py:187
  71.0 0.1 add_multiply_fusion.mixed
  71.1 2.1 %collective-permute-start.7 = (f32[2,512,128]{2,1,0:T(8,128)S(1)}, f32[2,512,128]{2,1,0:T(8,128)S(1)}, u32[]{:S(2)}, u32[]{:S(2)}) collective-permute-start(f32[2,512,128]{2,1,0:T(8,128)S(1)} %add_multiply_fusion.mixed), channel_id=1, source_target_pairs={{0,2},{1,5},{2,4},{3,1},{4,0},{5,3},{6,8},{7,11},{8,10},{9,7},{10,... | collective-permute-start | bytes 1572872 | tf_op jit(solution)/shard_map/mixed_gather/ppermute | solution.py:187
  73.2 3.8 %collective-permute-done.9 = f32[2,64,512]{2,1,0:T(8,128)} collective-permute-done((f32[2,64,512]{2,1,0:T(8,128)S(1)}, f32[2,64,512]{2,1,0:T(8,128)}, u32[]{:S(2)}, u32[]{:S(2)}) %collective-permute-start.9) | collective-permute-done | bytes 262176 | tf_op jit(solution)/shard_map/weight_gather/ppermute | solution.py:187
  77.0 1.9 %collective-permute-start.10 = (f32[2,64,512]{2,1,0:T(8,128)}, f32[2,64,512]{2,1,0:T(8,128)S(1)}, u32[]{:S(2)}, u32[]{:S(2)}) collective-permute-start(f32[2,64,512]{2,1,0:T(8,128)} %collective-permute-done.9), channel_id=1, source_target_pairs={{0,192},{192,0},{384,576},{576,384},{1,193},{193,1},{385,577},{577... | collective-permute-start | bytes 786440 | tf_op jit(solution)/shard_map/weight_gather/ppermute | solution.py:213
  79.0 0.0 copy-start.10
  79.0 0.0 copy-start.4
  79.0 5.7 %collective-permute-done.10 = f32[2,64,512]{2,1,0:T(8,128)S(1)} collective-permute-done((f32[2,64,512]{2,1,0:T(8,128)}, f32[2,64,512]{2,1,0:T(8,128)S(1)}, u32[]{:S(2)}, u32[]{:S(2)}) %collective-permute-start.10) | collective-permute-done | bytes 262176 | tf_op jit(solution)/shard_map/weight_gather/ppermute | solution.py:213
  84.7 1.1 maximum_select_fusion.weight_got
  85.7 5.4 %collective-permute-start.11 = (f32[2,128,512]{2,1,0:T(8,128)S(1)}, f32[2,128,512]{2,1,0:T(8,128)S(1)}, u32[]{:S(2)}, u32[]{:S(2)}) collective-permute-start(f32[2,128,512]{2,1,0:T(8,128)S(1)} %maximum_select_fusion.weight_got), channel_id=1, source_target_pairs={{0,1},{1,0},{2,3},{3,2},{4,5},{5,4},{6,7},{7,6},{8,9},{9,8},{10,11... | collective-permute-start | bytes 1572872 | tf_op jit(solution)/shard_map/weight_gather/ppermute | solution.py:191
  91.2 0.0 collective-permute-done.7.got
  91.2 1.9 %collective-permute-start.8 = (f32[2,512,128]{2,1,0:T(8,128)S(1)}, f32[2,512,128]{2,1,0:T(8,128)S(1)}, u32[]{:S(2)}, u32[]{:S(2)}) collective-permute-start(f32[2,512,128]{2,1,0:T(8,128)S(1)} %collective-permute-done.7.got), channel_id=1, source_target_pairs={{0,1},{1,0},{2,3},{3,2},{4,5},{5,4},{6,7},{7,6},{8,9},{9,8},{10,11... | collective-permute-start | bytes 1572872 | tf_op jit(solution)/shard_map/mixed_gather/ppermute | solution.py:191
  93.2 0.0 copy-start.7
  93.2 1.8 %collective-permute-done.8.swapped = f32[2,512,128]{2,1,0:T(8,128)S(1)} collective-permute-done((f32[2,512,128]{2,1,0:T(8,128)S(1)}, f32[2,512,128]{2,1,0:T(8,128)S(1)}, u32[]{:S(2)}, u32[]{:S(2)}) %collective-permute-start.8) | collective-permute-done | bytes 524320 | tf_op jit(solution)/shard_map/mixed_gather/ppermute | solution.py:191
  95.0 5.7 %layer.1 = (f32[512,512]{1,0:T(8,128)}, f32[32,24,128]{2,1,0:T(8,128)}, f32[512,256]{1,0:T(8,128)S(1)}, f32[512,128]{1,0:T(8,128)S(1)}, f32[512,128]{1,0:T(8,128)S(1)}, /*index=5*/f32[512,128]{1,0:T(8,128)S(1)}) custom-call(s32[2]{0:T(128)S(1)} %pad_add_fusion.where, s32[4,4]{1,0:T(4,128)S(1)} %copy-done.2, f32[2,512,128]{2,1,0:T(8,128)S(1)} %add_multiply_fusion.mixed, ...), custom_call_target="tpu_custom_call" | custom-call | flops 1500000000 | bytes 10000000 | tf_op jit(solution)/shard_map/layer/pallas_call | solution.py:248
  100.7 0.8 copy-done.5
  101.6 4.0 %all-to-all-start = ((f32[32,24,128]{2,1,0:T(8,128)}), f32[32,24,128]{2,1,0:T(8,128)S(1)}, u32[]{:S(2)}, u32[]{:S(2)}) async-start(f32[32,24,128]{2,1,0:T(8,128)} %get-tuple-element.32), calls=%async_computation | async-start | bytes 786432 | tf_op jit(solution)/shard_map/nodes_sum/all_to_all | solution.py:272
  105.6 13.1 %collective-permute-start.12 = (f32[512,256]{1,0:T(8,128)S(1)}, f32[512,256]{1,0:T(8,128)S(1)}, u32[]{:S(2)}, u32[]{:S(2)}) collective-permute-start(f32[512,256]{1,0:T(8,128)S(1)} %copy-done.6), channel_id=1, source_target_pairs={{0,6},{1,763},{6,12},{7,1},{12,18},{13,7},{18,24},{19,13},{24,30},... | collective-permute-start | bytes 1572872 | tf_op jit(solution)/shard_map/back_halo/ppermute | solution.py:187
  118.8 0.6 broadcast_in_dim.4
  119.4 7.1 %all-to-all-start.1 = ((f32[4,24,128]{2,1,0:T(8,128)}), f32[4,24,128]{2,1,0:T(8,128)S(1)}, u32[]{:S(2)}, u32[]{:S(2)}) async-start(f32[4,24,128]{2,1,0:T(8,128)} %broadcast_in_dim.4), calls=%async_computation.1 | async-start | bytes 98304 | tf_op jit(solution)/shard_map/nodes_sum/all_to_all | solution.py:277
  126.5 10.0 %all-to-all-done.1 = f32[4,24,128]{2,1,0:T(8,128)S(1)} async-done(((f32[4,24,128]{2,1,0:T(8,128)}), f32[4,24,128]{2,1,0:T(8,128)S(1)}, u32[]{:S(2)}, u32[]{:S(2)}) %all-to-all-start.1) | async-done | bytes 49184 | tf_op jit(solution)/shard_map/nodes_sum/all_to_all | solution.py:277
  136.5 0.1 select_add_fusion
  136.6 7.7 %collective-permute-start.14 = (f32[512,128]{1,0:T(8,128)S(1)}, f32[512,128]{1,0:T(8,128)S(1)}, u32[]{:S(2)}, u32[]{:S(2)}) collective-permute-start(f32[512,128]{1,0:T(8,128)S(1)} %get-tuple-element.36), channel_id=1, source_target_pairs={{0,7},{1,762},{6,13},{7,0},{12,19},{13,6},{18,25},{19,12},{24,31},... | collective-permute-start | bytes 786440 | tf_op jit(solution)/shard_map/back_halo/ppermute | solution.py:187
  144.3 5.2 %collective-permute-start.13 = (f32[512,128]{1,0:T(8,128)S(1)}, f32[512,128]{1,0:T(8,128)S(1)}, u32[]{:S(2)}, u32[]{:S(2)}) collective-permute-start(f32[512,128]{1,0:T(8,128)S(1)} %get-tuple-element.37), channel_id=1, source_target_pairs={{0,6},{1,763},{6,12},{7,1},{12,18},{13,7},{18,24},{19,13},{24,30},... | collective-permute-start | bytes 786440 | tf_op jit(solution)/shard_map/back_halo/ppermute | solution.py:187
  149.5 0.7 broadcast_in_dim.5
  150.2 3.9 %all-to-all-start.2 = ((f32[32,16,128]{2,1,0:T(8,128)}), f32[32,16,128]{2,1,0:T(8,128)S(1)}, u32[]{:S(2)}, u32[]{:S(2)}) async-start(f32[32,16,128]{2,1,0:T(8,128)} %broadcast_in_dim.5), calls=%async_computation.2 | async-start | bytes 524288 | tf_op jit(solution)/shard_map/nodes_sum/all_to_all | solution.py:286
  154.1 0.6 slice_bitcast_fusion
  154.7 7.5 %collective-permute-done.14 = f32[512,128]{1,0:T(8,128)S(1)} collective-permute-done((f32[512,128]{1,0:T(8,128)S(1)}, f32[512,128]{1,0:T(8,128)S(1)}, u32[]{:S(2)}, u32[]{:S(2)}) %collective-permute-start.14) | collective-permute-done | bytes 262176 | tf_op jit(solution)/shard_map/back_halo/ppermute | solution.py:187
  162.2 0.7 add_add_fusion
  162.9 5.3 %all-to-all-done.2.pieces = f32[32,16,128]{2,1,0:T(8,128)S(1)} async-done(((f32[32,16,128]{2,1,0:T(8,128)}), f32[32,16,128]{2,1,0:T(8,128)S(1)}, u32[]{:S(2)}, u32[]{:S(2)}) %all-to-all-start.2) | async-done | bytes 262176 | tf_op jit(solution)/shard_map/nodes_sum/all_to_all | solution.py:286
  168.2 0.7 arrange.1
  (27 shorter events, 0.2 us)
Async XLA Ops:
  0.6 22.8 %collective-permute-start.2 = (f32[512,128]{1,0:T(8,128)}, f32[512,128]{1,0:T(8,128)S(1)}, u32[]{:S(2)}, u32[]{:S(2)}) collective-permute-start(f32[512,128]{1,0:T(8,128)} %own.1), channel_id=1, source_target_pairs={{0,1},{1,0},{2,3},{3,2},{4,5},{5,4},{6,7},{7,6},{8,9},{9,8},{10,11... | collective-permute-start | bytes 786440 | tf_op jit(solution)/shard_map/halo/ppermute | solution.py:191
  13.1 17.9 %collective-permute-start = (f32[512,128]{1,0:T(8,128)}, f32[512,128]{1,0:T(8,128)S(1)}, u32[]{:S(2)}, u32[]{:S(2)}) collective-permute-start(f32[512,128]{1,0:T(8,128)} %own.1), channel_id=1, source_target_pairs={{0,6},{1,763},{6,12},{7,1},{12,18},{13,7},{18,24},{19,13},{24,30},... | collective-permute-start | bytes 786440 | tf_op jit(solution)/shard_map/halo/ppermute | solution.py:187
  23.5 18.5 %collective-permute-start.3 = (f32[512,128]{1,0:T(8,128)S(1)}, f32[512,128]{1,0:T(8,128)S(1)}, u32[]{:S(2)}, u32[]{:S(2)}) collective-permute-start(f32[512,128]{1,0:T(8,128)S(1)} %collective-permute-done.2.other), channel_id=1, source_target_pairs={{0,6},{1,763},{6,12},{7,1},{12,18},{13,7},{18,24},{19,13},{24,30},... | collective-permute-start | bytes 786440 | tf_op jit(solution)/shard_map/halo/ppermute | solution.py:187
  26.2 30.0 %collective-permute-start.5 = (f32[128,512]{1,0:T(8,128)}, f32[128,512]{1,0:T(8,128)S(1)}, u32[]{:S(2)}, u32[]{:S(2)}) collective-permute-start(f32[128,512]{1,0:T(8,128)} %param.8), channel_id=1, source_target_pairs={{0,1},{1,0},{2,3},{3,2},{4,5},{5,4},{6,7},{7,6},{8,9},{9,8},{10,11... | collective-permute-start | bytes 786440 | tf_op jit(solution)/shard_map/weight_gather/ppermute | solution.py:191
  31.0 26.0 %collective-permute-start.1 = (f32[512,128]{1,0:T(8,128)S(1)}, f32[512,128]{1,0:T(8,128)S(1)}, u32[]{:S(2)}, u32[]{:S(2)}) collective-permute-start(f32[512,128]{1,0:T(8,128)S(1)} %collective-permute-done.near), channel_id=1, source_target_pairs={{0,6},{1,763},{6,12},{7,1},{12,18},{13,7},{18,24},{19,13},{24,30},... | collective-permute-start | bytes 786440 | tf_op jit(solution)/shard_map/halo/ppermute | solution.py:187
  42.0 21.6 %collective-permute-start.4 = (f32[512,128]{1,0:T(8,128)S(1)}, f32[512,128]{1,0:T(8,128)S(1)}, u32[]{:S(2)}, u32[]{:S(2)}) collective-permute-start(f32[512,128]{1,0:T(8,128)S(1)} %collective-permute-done.3.near2), channel_id=1, source_target_pairs={{0,6},{1,763},{6,12},{7,1},{12,18},{13,7},{18,24},{19,13},{24,30},... | collective-permute-start | bytes 786440 | tf_op jit(solution)/shard_map/halo/ppermute | solution.py:187
  53.3 0.7 copy-start.3
  53.9 1.2 copy-start
  55.1 1.1 copy-start.8
  56.3 0.7 copy-start.9
  56.3 7.3 %copy-start.1 = (f32[512,128]{1,0:T(8,128)S(1)}, f32[512,128]{1,0:T(8,128)}, u32[]{:S(2)}) copy-start(f32[512,128]{1,0:T(8,128)} %own.1) | copy-start | bytes 786436
  57.0 6.6 %copy-start.2 = (s32[4,4]{1,0:T(4,128)S(1)}, s32[4,4]{1,0:T(4,128)}, u32[]{:S(2)}) copy-start(s32[4,4]{1,0:T(4,128)} %offset.3) | copy-start | bytes 196
  65.2 5.8 %collective-permute-start.6 = (f32[2,512,128]{2,1,0:T(8,128)S(1)}, f32[2,512,128]{2,1,0:T(8,128)S(1)}, u32[]{:S(2)}, u32[]{:S(2)}) collective-permute-start(f32[2,512,128]{2,1,0:T(8,128)S(1)} %get-tuple-element.24), channel_id=1, source_target_pairs={{0,1},{1,0},{2,3},{3,2},{4,5},{5,4},{6,7},{7,6},{8,9},{9,8},{10,11... | collective-permute-start | bytes 1572872 | tf_op jit(solution)/shard_map/mixed_gather/ppermute | solution.py:191
  67.1 9.9 %collective-permute-start.9 = (f32[2,64,512]{2,1,0:T(8,128)S(1)}, f32[2,64,512]{2,1,0:T(8,128)}, u32[]{:S(2)}, u32[]{:S(2)}) collective-permute-start(f32[2,64,512]{2,1,0:T(8,128)S(1)} %fusion), channel_id=1, source_target_pairs={{0,2},{1,5},{2,4},{3,1},{4,0},{5,3},{6,8},{7,11},{8,10},{9,7},{10,... | collective-permute-start | bytes 786440 | tf_op jit(solution)/shard_map/weight_gather/ppermute | solution.py:187
  71.1 20.1 %collective-permute-start.7 = (f32[2,512,128]{2,1,0:T(8,128)S(1)}, f32[2,512,128]{2,1,0:T(8,128)S(1)}, u32[]{:S(2)}, u32[]{:S(2)}) collective-permute-start(f32[2,512,128]{2,1,0:T(8,128)S(1)} %add_multiply_fusion.mixed), channel_id=1, source_target_pairs={{0,2},{1,5},{2,4},{3,1},{4,0},{5,3},{6,8},{7,11},{8,10},{9,7},{10,... | collective-permute-start | bytes 1572872 | tf_op jit(solution)/shard_map/mixed_gather/ppermute | solution.py:187
  77.0 7.6 %collective-permute-start.10 = (f32[2,64,512]{2,1,0:T(8,128)}, f32[2,64,512]{2,1,0:T(8,128)S(1)}, u32[]{:S(2)}, u32[]{:S(2)}) collective-permute-start(f32[2,64,512]{2,1,0:T(8,128)} %collective-permute-done.9), channel_id=1, source_target_pairs={{0,192},{192,0},{384,576},{576,384},{1,193},{193,1},{385,577},{577... | collective-permute-start | bytes 786440 | tf_op jit(solution)/shard_map/weight_gather/ppermute | solution.py:213
  79.0 14.1 %copy-start.10 = (f32[128,512]{1,0:T(8,128)S(1)}, f32[128,512]{1,0:T(8,128)}, u32[]{:S(2)}) copy-start(f32[128,512]{1,0:T(8,128)} %copy-done.9) | copy-start | bytes 786436
  79.0 16.0 %copy-start.4 = (f32[512,512]{1,0:T(8,128)S(1)}, f32[512,512]{1,0:T(8,128)}, u32[]{:S(2)}) copy-start(f32[512,512]{1,0:T(8,128)} %gout.1) | copy-start | bytes 3145732
  85.7 7.4 %collective-permute-start.11 = (f32[2,128,512]{2,1,0:T(8,128)S(1)}, f32[2,128,512]{2,1,0:T(8,128)S(1)}, u32[]{:S(2)}, u32[]{:S(2)}) collective-permute-start(f32[2,128,512]{2,1,0:T(8,128)S(1)} %maximum_select_fusion.weight_got), channel_id=1, source_target_pairs={{0,1},{1,0},{2,3},{3,2},{4,5},{5,4},{6,7},{7,6},{8,9},{9,8},{10,11... | collective-permute-start | bytes 1572872 | tf_op jit(solution)/shard_map/weight_gather/ppermute | solution.py:191
  91.2 3.8 %collective-permute-start.8 = (f32[2,512,128]{2,1,0:T(8,128)S(1)}, f32[2,512,128]{2,1,0:T(8,128)S(1)}, u32[]{:S(2)}, u32[]{:S(2)}) collective-permute-start(f32[2,512,128]{2,1,0:T(8,128)S(1)} %collective-permute-done.7.got), channel_id=1, source_target_pairs={{0,1},{1,0},{2,3},{3,2},{4,5},{5,4},{6,7},{7,6},{8,9},{9,8},{10,11... | collective-permute-start | bytes 1572872 | tf_op jit(solution)/shard_map/mixed_gather/ppermute | solution.py:191
  93.2 1.8 %copy-start.7 = (f32[512]{0:T(512)S(1)}, f32[512]{0:T(512)}, u32[]{:S(2)}) copy-start(f32[512]{0:T(512)} %param.9) | copy-start | bytes 6148
  100.7 0.8 copy-start.5
  101.6 4.0 %copy-start.6 = (f32[512,256]{1,0:T(8,128)S(1)}, f32[512,256]{1,0:T(8,128)}, u32[]{:S(2)}) copy-start(f32[512,256]{1,0:T(8,128)} %copy-done.5) | copy-start | bytes 1572868
  101.6 17.1 %all-to-all-start = ((f32[32,24,128]{2,1,0:T(8,128)}), f32[32,24,128]{2,1,0:T(8,128)S(1)}, u32[]{:S(2)}, u32[]{:S(2)}) async-start(f32[32,24,128]{2,1,0:T(8,128)} %get-tuple-element.32), calls=%async_computation | async-start | bytes 786432 | tf_op jit(solution)/shard_map/nodes_sum/all_to_all | solution.py:272
  105.6 30.9 %collective-permute-start.12 = (f32[512,256]{1,0:T(8,128)S(1)}, f32[512,256]{1,0:T(8,128)S(1)}, u32[]{:S(2)}, u32[]{:S(2)}) collective-permute-start(f32[512,256]{1,0:T(8,128)S(1)} %copy-done.6), channel_id=1, source_target_pairs={{0,6},{1,763},{6,12},{7,1},{12,18},{13,7},{18,24},{19,13},{24,30},... | collective-permute-start | bytes 1572872 | tf_op jit(solution)/shard_map/back_halo/ppermute | solution.py:187
  119.4 17.1 %all-to-all-start.1 = ((f32[4,24,128]{2,1,0:T(8,128)}), f32[4,24,128]{2,1,0:T(8,128)S(1)}, u32[]{:S(2)}, u32[]{:S(2)}) async-start(f32[4,24,128]{2,1,0:T(8,128)} %broadcast_in_dim.4), calls=%async_computation.1 | async-start | bytes 98304 | tf_op jit(solution)/shard_map/nodes_sum/all_to_all | solution.py:277
  136.6 25.6 %collective-permute-start.14 = (f32[512,128]{1,0:T(8,128)S(1)}, f32[512,128]{1,0:T(8,128)S(1)}, u32[]{:S(2)}, u32[]{:S(2)}) collective-permute-start(f32[512,128]{1,0:T(8,128)S(1)} %get-tuple-element.36), channel_id=1, source_target_pairs={{0,7},{1,762},{6,13},{7,0},{12,19},{13,6},{18,25},{19,12},{24,31},... | collective-permute-start | bytes 786440 | tf_op jit(solution)/shard_map/back_halo/ppermute | solution.py:187
  144.3 17.9 %collective-permute-start.13 = (f32[512,128]{1,0:T(8,128)S(1)}, f32[512,128]{1,0:T(8,128)S(1)}, u32[]{:S(2)}, u32[]{:S(2)}) collective-permute-start(f32[512,128]{1,0:T(8,128)S(1)} %get-tuple-element.37), channel_id=1, source_target_pairs={{0,6},{1,763},{6,12},{7,1},{12,18},{13,7},{18,24},{19,13},{24,30},... | collective-permute-start | bytes 786440 | tf_op jit(solution)/shard_map/back_halo/ppermute | solution.py:187
  150.2 18.0 %all-to-all-start.2 = ((f32[32,16,128]{2,1,0:T(8,128)}), f32[32,16,128]{2,1,0:T(8,128)S(1)}, u32[]{:S(2)}, u32[]{:S(2)}) async-start(f32[32,16,128]{2,1,0:T(8,128)} %broadcast_in_dim.5), calls=%async_computation.2 | async-start | bytes 524288 | tf_op jit(solution)/shard_map/nodes_sum/all_to_all | solution.py:286

commit v5 on v4

--- a/solution.py
+++ b/solution.py
@@ -273,11 +273,12 @@
     with jax.named_scope("back_halo"):
         came = by_core(q_far, NODES, 1, -1)
     with jax.named_scope("nodes_sum"):
+        plane = held
         held = jnp.broadcast_to(held[None], (4, 24, T))
         held = jnp.sum(lax.all_to_all(held, "zh", 0, 0), axis=0)
     with jax.named_scope("back_halo"):
+        kept = q_near + plane[:1, :1] * 0.0 + jnp.where(c == 0, came[:, :width], came[:, width:])
         came, held = lax.optimization_barrier((came, held))
-        kept = q_near + jnp.where(c == 0, came[:, :width], came[:, width:])
         lent = q_other + jnp.where(c == 0, came[:, width:], came[:, :width])
         grad_features = center + (by_core(kept, NODES, 1, -1) + by_core(lent, NODES, 1, -1, True))
     with jax.named_scope("nodes_sum"):

time: 170 us -> 168 us (0.988)
  waiting for transfers between devices: 43.5 us -> 38.3 us
  starting transfers between devices: 108 us -> 110 us
    all_to_all x1, waiting for transfers between devices: 9.99 us -> 0.01 us  [body(): held = jnp.sum(lax.all_to_all(held, 'zh', 0, 0), axis=0)]
    ppermute x9, waiting for transfers between devices: 20.7 us -> 30.1 us  [by_core(): return lax.ppermute(block, axes, route)]
    all_to_all x1, waiting for transfers between devices: 5.31 us -> 0.74 us  [body(): whole = lax.all_to_all(whole, PLANE, 0, 0)]
    ppermute x9, starting transfers between devices: 67.4 us -> 69.2 us  [by_core(): return lax.ppermute(block, axes, route)]
  transfers between devices with their start and end apart: 18 -> 18, of which waited for: 8 -> 8; matrix products, arithmetic and copies ran while one was open for 2% -> 3% of each run, Pallas kernels for 1% -> 1%
where the time goes in v5:
time: 168 us; the launch traced here: 167 us
  starting transfers between devices  110 us (65%)
  waiting for transfers between devices  38.3 us (23%)
  Pallas kernels  9.09 us (5%)
  local copies, waits for them, and re-layouts  5.81 us (3%)
  other arithmetic  2.17 us (1%)
    ppermute x9, starting transfers between devices, by_core(): return lax.ppermute(block, axes, route)  69.2 us
    ppermute x9, waiting for transfers between devices, by_core(): return lax.ppermute(block, axes, route)  30.1 us
    ppermute x5, starting transfers between devices, swap(): return lax.ppermute(block, 'c', [(0, 1), (1, 0)])  23.6 us
    all_to_all x1, starting transfers between devices, body(): held = jnp.sum(lax.all_to_all(held, 'zh', 0, 0), axis=0)  7.12 us
    pallas_call x1, Pallas kernels, body(): call(layer_kernel, [SMEM] * 2 + [VMEM] * 10, [shape_of((rows, 4 * T)), sh...  5.74 us
    ppermute x1, waiting for transfers between devices, body(): theirs = lax.ppermute(half, 'x', [(i, i ^ 1) for i in range(4)])  5.66 us
    all_to_all x1, starting transfers between devices, body(): held = jnp.sum(lax.all_to_all(parts, PLANE, 0, 0), axis=0)  4.01 us
    all_to_all x1, starting transfers between devices, body(): whole = lax.all_to_all(whole, PLANE, 0, 0)  3.87 us
  transfers between devices with their start and end apart: 18, of which 8 were waited for; matrix products, arithmetic and copies ran while one was open for 3% of the time, Pallas kernels for 1%

profile of v5, /device:TPU:1, one launch (start us, length us, event | category | flops | bytes accessed | tf_op | source)
XLA Modules:
  0.0 166.7 jit_solution(16294967791441277093)
XLA Ops:
  0.6 12.4 %collective-permute-start.2 = (f32[512,128]{1,0:T(8,128)}, f32[512,128]{1,0:T(8,128)S(1)}, u32[]{:S(2)}, u32[]{:S(2)}) collective-permute-start(f32[512,128]{1,0:T(8,128)} %own.1), channel_id=1, source_target_pairs={{0,1},{1,0},{2,3},{3,2},{4,5},{5,4},{6,7},{7,6},{8,9},{9,8},{10,11... | collective-permute-start | bytes 786440 | tf_op jit(solution)/shard_map/halo/ppermute | solution.py:191
  13.1 10.4 %collective-permute-start = (f32[512,128]{1,0:T(8,128)}, f32[512,128]{1,0:T(8,128)S(1)}, u32[]{:S(2)}, u32[]{:S(2)}) collective-permute-start(f32[512,128]{1,0:T(8,128)} %own.1), channel_id=1, source_target_pairs={{0,6},{1,763},{6,12},{7,1},{12,18},{13,7},{18,24},{19,13},{24,30},... | collective-permute-start | bytes 786440 | tf_op jit(solution)/shard_map/halo/ppermute | solution.py:187
  23.4 0.0 collective-permute-done.2.other
  23.5 2.8 %collective-permute-start.3 = (f32[512,128]{1,0:T(8,128)S(1)}, f32[512,128]{1,0:T(8,128)S(1)}, u32[]{:S(2)}, u32[]{:S(2)}) collective-permute-start(f32[512,128]{1,0:T(8,128)S(1)} %collective-permute-done.2.other), channel_id=1, source_target_pairs={{0,6},{1,763},{6,12},{7,1},{12,18},{13,7},{18,24},{19,13},{24,30},... | collective-permute-start | bytes 786440 | tf_op jit(solution)/shard_map/halo/ppermute | solution.py:187
  26.2 1.9 %collective-permute-start.5 = (f32[128,512]{1,0:T(8,128)}, f32[128,512]{1,0:T(8,128)S(1)}, u32[]{:S(2)}, u32[]{:S(2)}) collective-permute-start(f32[128,512]{1,0:T(8,128)} %param.8), channel_id=1, source_target_pairs={{0,1},{1,0},{2,3},{3,2},{4,5},{5,4},{6,7},{7,6},{8,9},{9,8},{10,11... | collective-permute-start | bytes 786440 | tf_op jit(solution)/shard_map/weight_gather/ppermute | solution.py:191
  28.2 2.8 %collective-permute-done.near = f32[512,128]{1,0:T(8,128)S(1)} collective-permute-done((f32[512,128]{1,0:T(8,128)}, f32[512,128]{1,0:T(8,128)S(1)}, u32[]{:S(2)}, u32[]{:S(2)}) %collective-permute-start) | collective-permute-done | bytes 262176 | tf_op jit(solution)/shard_map/halo/ppermute | solution.py:187
  31.0 11.0 %collective-permute-start.1 = (f32[512,128]{1,0:T(8,128)S(1)}, f32[512,128]{1,0:T(8,128)S(1)}, u32[]{:S(2)}, u32[]{:S(2)}) collective-permute-start(f32[512,128]{1,0:T(8,128)S(1)} %collective-permute-done.near), channel_id=1, source_target_pairs={{0,6},{1,763},{6,12},{7,1},{12,18},{13,7},{18,24},{19,13},{24,30},... | collective-permute-start | bytes 786440 | tf_op jit(solution)/shard_map/halo/ppermute | solution.py:187
  42.0 0.0 collective-permute-done.3.near2
  42.0 11.2 %collective-permute-start.4 = (f32[512,128]{1,0:T(8,128)S(1)}, f32[512,128]{1,0:T(8,128)S(1)}, u32[]{:S(2)}, u32[]{:S(2)}) collective-permute-start(f32[512,128]{1,0:T(8,128)S(1)} %collective-permute-done.3.near2), channel_id=1, source_target_pairs={{0,6},{1,763},{6,12},{7,1},{12,18},{13,7},{18,24},{19,13},{24,30},... | collective-permute-start | bytes 786440 | tf_op jit(solution)/shard_map/halo/ppermute | solution.py:187
  53.3 0.6 copy-done.3
  53.9 1.2 copy-done
  55.2 1.0 prepare.1
  56.2 0.1 pad_add_fusion.where
  56.3 0.7 copy-done.9
  57.0 6.6 %collective-permute-done.4.far2 = f32[512,128]{1,0:T(8,128)S(1)} collective-permute-done((f32[512,128]{1,0:T(8,128)S(1)}, f32[512,128]{1,0:T(8,128)S(1)}, u32[]{:S(2)}, u32[]{:S(2)}) %collective-permute-start.4) | collective-permute-done | bytes 262176 | tf_op jit(solution)/shard_map/halo/ppermute | solution.py:187
  63.6 1.6 mix.1
  65.2 1.9 %collective-permute-start.6 = (f32[2,512,128]{2,1,0:T(8,128)S(1)}, f32[2,512,128]{2,1,0:T(8,128)S(1)}, u32[]{:S(2)}, u32[]{:S(2)}) collective-permute-start(f32[2,512,128]{2,1,0:T(8,128)S(1)} %get-tuple-element.24), channel_id=1, source_target_pairs={{0,1},{1,0},{2,3},{3,2},{4,5},{5,4},{6,7},{7,6},{8,9},{9,8},{10,11... | collective-permute-start | bytes 1572872 | tf_op jit(solution)/shard_map/mixed_gather/ppermute | solution.py:191
  67.1 3.9 %collective-permute-start.9 = (f32[2,64,512]{2,1,0:T(8,128)S(1)}, f32[2,64,512]{2,1,0:T(8,128)}, u32[]{:S(2)}, u32[]{:S(2)}) collective-permute-start(f32[2,64,512]{2,1,0:T(8,128)S(1)} %fusion), channel_id=1, source_target_pairs={{0,2},{1,5},{2,4},{3,1},{4,0},{5,3},{6,8},{7,11},{8,10},{9,7},{10,... | collective-permute-start | bytes 786440 | tf_op jit(solution)/shard_map/weight_gather/ppermute | solution.py:187
  71.0 0.1 add_multiply_fusion.mixed
  71.1 2.1 %collective-permute-start.7 = (f32[2,512,128]{2,1,0:T(8,128)S(1)}, f32[2,512,128]{2,1,0:T(8,128)S(1)}, u32[]{:S(2)}, u32[]{:S(2)}) collective-permute-start(f32[2,512,128]{2,1,0:T(8,128)S(1)} %add_multiply_fusion.mixed), channel_id=1, source_target_pairs={{0,2},{1,5},{2,4},{3,1},{4,0},{5,3},{6,8},{7,11},{8,10},{9,7},{10,... | collective-permute-start | bytes 1572872 | tf_op jit(solution)/shard_map/mixed_gather/ppermute | solution.py:187
  73.2 3.8 %collective-permute-done.9 = f32[2,64,512]{2,1,0:T(8,128)} collective-permute-done((f32[2,64,512]{2,1,0:T(8,128)S(1)}, f32[2,64,512]{2,1,0:T(8,128)}, u32[]{:S(2)}, u32[]{:S(2)}) %collective-permute-start.9) | collective-permute-done | bytes 262176 | tf_op jit(solution)/shard_map/weight_gather/ppermute | solution.py:187
  77.0 1.9 %collective-permute-start.10 = (f32[2,64,512]{2,1,0:T(8,128)}, f32[2,64,512]{2,1,0:T(8,128)S(1)}, u32[]{:S(2)}, u32[]{:S(2)}) collective-permute-start(f32[2,64,512]{2,1,0:T(8,128)} %collective-permute-done.9), channel_id=1, source_target_pairs={{0,192},{192,0},{384,576},{576,384},{1,193},{193,1},{385,577},{577... | collective-permute-start | bytes 786440 | tf_op jit(solution)/shard_map/weight_gather/ppermute | solution.py:213
  79.0 0.0 copy-start.10
  79.0 0.0 copy-start.4
  79.0 5.7 %collective-permute-done.10 = f32[2,64,512]{2,1,0:T(8,128)S(1)} collective-permute-done((f32[2,64,512]{2,1,0:T(8,128)}, f32[2,64,512]{2,1,0:T(8,128)S(1)}, u32[]{:S(2)}, u32[]{:S(2)}) %collective-permute-start.10) | collective-permute-done | bytes 262176 | tf_op jit(solution)/shard_map/weight_gather/ppermute | solution.py:213
  84.7 1.1 maximum_select_fusion.weight_got
  85.7 5.4 %collective-permute-start.11 = (f32[2,128,512]{2,1,0:T(8,128)S(1)}, f32[2,128,512]{2,1,0:T(8,128)S(1)}, u32[]{:S(2)}, u32[]{:S(2)}) collective-permute-start(f32[2,128,512]{2,1,0:T(8,128)S(1)} %maximum_select_fusion.weight_got), channel_id=1, source_target_pairs={{0,1},{1,0},{2,3},{3,2},{4,5},{5,4},{6,7},{7,6},{8,9},{9,8},{10,11... | collective-permute-start | bytes 1572872 | tf_op jit(solution)/shard_map/weight_gather/ppermute | solution.py:191
  91.2 0.0 collective-permute-done.7.got
  91.2 1.9 %collective-permute-start.8 = (f32[2,512,128]{2,1,0:T(8,128)S(1)}, f32[2,512,128]{2,1,0:T(8,128)S(1)}, u32[]{:S(2)}, u32[]{:S(2)}) collective-permute-start(f32[2,512,128]{2,1,0:T(8,128)S(1)} %collective-permute-done.7.got), channel_id=1, source_target_pairs={{0,1},{1,0},{2,3},{3,2},{4,5},{5,4},{6,7},{7,6},{8,9},{9,8},{10,11... | collective-permute-start | bytes 1572872 | tf_op jit(solution)/shard_map/mixed_gather/ppermute | solution.py:191
  93.2 0.0 copy-start.7
  93.2 1.8 %collective-permute-done.8.swapped = f32[2,512,128]{2,1,0:T(8,128)S(1)} collective-permute-done((f32[2,512,128]{2,1,0:T(8,128)S(1)}, f32[2,512,128]{2,1,0:T(8,128)S(1)}, u32[]{:S(2)}, u32[]{:S(2)}) %collective-permute-start.8) | collective-permute-done | bytes 524320 | tf_op jit(solution)/shard_map/mixed_gather/ppermute | solution.py:191
  95.0 5.7 %layer.1 = (f32[512,512]{1,0:T(8,128)}, f32[32,24,128]{2,1,0:T(8,128)}, f32[512,256]{1,0:T(8,128)S(1)}, f32[512,128]{1,0:T(8,128)S(1)}, f32[512,128]{1,0:T(8,128)S(1)}, /*index=5*/f32[512,128]{1,0:T(8,128)S(1)}) custom-call(s32[2]{0:T(128)S(1)} %pad_add_fusion.where, s32[4,4]{1,0:T(4,128)S(1)} %copy-done.2, f32[2,512,128]{2,1,0:T(8,128)S(1)} %add_multiply_fusion.mixed, ...), custom_call_target="tpu_custom_call" | custom-call | flops 1500000000 | bytes 10000000 | tf_op jit(solution)/shard_map/layer/pallas_call | solution.py:248
  100.7 0.8 copy-done.5
  101.5 4.0 %all-to-all-start = ((f32[32,24,128]{2,1,0:T(8,128)}), f32[32,24,128]{2,1,0:T(8,128)S(1)}, u32[]{:S(2)}, u32[]{:S(2)}) async-start(f32[32,24,128]{2,1,0:T(8,128)} %get-tuple-element.31), calls=%async_computation | async-start | bytes 786432 | tf_op jit(solution)/shard_map/nodes_sum/all_to_all | solution.py:272
  105.6 13.1 %collective-permute-start.12 = (f32[512,256]{1,0:T(8,128)S(1)}, f32[512,256]{1,0:T(8,128)S(1)}, u32[]{:S(2)}, u32[]{:S(2)}) collective-permute-start(f32[512,256]{1,0:T(8,128)S(1)} %copy-done.6), channel_id=1, source_target_pairs={{0,6},{1,763},{6,12},{7,1},{12,18},{13,7},{18,24},{19,13},{24,30},... | collective-permute-start | bytes 1572872 | tf_op jit(solution)/shard_map/back_halo/ppermute | solution.py:187
  118.7 0.5 slice.28
  119.3 0.6 broadcast_in_dim.4
  119.9 7.1 %all-to-all-start.1 = ((f32[4,24,128]{2,1,0:T(8,128)}), f32[4,24,128]{2,1,0:T(8,128)S(1)}, u32[]{:S(2)}, u32[]{:S(2)}) async-start(f32[4,24,128]{2,1,0:T(8,128)} %broadcast_in_dim.4), calls=%async_computation.1 | async-start | bytes 98304 | tf_op jit(solution)/shard_map/nodes_sum/all_to_all | solution.py:278
  127.7 8.7 %collective-permute-done.12 = f32[512,256]{1,0:T(8,128)S(1)} collective-permute-done((f32[512,256]{1,0:T(8,128)S(1)}, f32[512,256]{1,0:T(8,128)S(1)}, u32[]{:S(2)}, u32[]{:S(2)}) %collective-permute-start.12) | collective-permute-done | bytes 524320 | tf_op jit(solution)/shard_map/back_halo/ppermute | solution.py:187
  136.4 11.2 %collective-permute-start.13 = (f32[512,128]{1,0:T(8,128)S(1)}, f32[512,128]{1,0:T(8,128)S(1)}, u32[]{:S(2)}, u32[]{:S(2)}) collective-permute-start(f32[512,128]{1,0:T(8,128)S(1)} %fusion.1), channel_id=1, source_target_pairs={{0,6},{1,763},{6,12},{7,1},{12,18},{13,7},{18,24},{19,13},{24,30},... | collective-permute-start | bytes 786440 | tf_op jit(solution)/shard_map/back_halo/ppermute | solution.py:187
  147.7 3.4 %collective-permute-start.14 = (f32[512,128]{1,0:T(8,128)S(1)}, f32[512,128]{1,0:T(8,128)S(1)}, u32[]{:S(2)}, u32[]{:S(2)}) collective-permute-start(f32[512,128]{1,0:T(8,128)S(1)} %select_add_fusion), channel_id=1, source_target_pairs={{0,7},{1,762},{6,13},{7,0},{12,19},{13,6},{18,25},{19,12},{24,31},... | collective-permute-start | bytes 786440 | tf_op jit(solution)/shard_map/back_halo/ppermute | solution.py:187
  151.1 0.7 broadcast_in_dim.5
  151.9 3.9 %all-to-all-start.2 = ((f32[32,16,128]{2,1,0:T(8,128)}), f32[32,16,128]{2,1,0:T(8,128)S(1)}, u32[]{:S(2)}, u32[]{:S(2)}) async-start(f32[32,16,128]{2,1,0:T(8,128)} %broadcast_in_dim.5), calls=%async_computation.2 | async-start | bytes 524288 | tf_op jit(solution)/shard_map/nodes_sum/all_to_all | solution.py:287
  155.7 0.6 slice_bitcast_fusion
  156.3 8.2 %collective-permute-done.14 = f32[512,128]{1,0:T(8,128)S(1)} collective-permute-done((f32[512,128]{1,0:T(8,128)S(1)}, f32[512,128]{1,0:T(8,128)S(1)}, u32[]{:S(2)}, u32[]{:S(2)}) %collective-permute-start.14) | collective-permute-done | bytes 262176 | tf_op jit(solution)/shard_map/back_halo/ppermute | solution.py:187
  164.5 0.7 add_add_fusion
  165.3 0.7 all-to-all-done.2.pieces
  166.0 0.7 arrange.1
  (29 shorter events, 0.2 us)
Async XLA Ops:
  0.6 22.8 %collective-permute-start.2 = (f32[512,128]{1,0:T(8,128)}, f32[512,128]{1,0:T(8,128)S(1)}, u32[]{:S(2)}, u32[]{:S(2)}) collective-permute-start(f32[512,128]{1,0:T(8,128)} %own.1), channel_id=1, source_target_pairs={{0,1},{1,0},{2,3},{3,2},{4,5},{5,4},{6,7},{7,6},{8,9},{9,8},{10,11... | collective-permute-start | bytes 786440 | tf_op jit(solution)/shard_map/halo/ppermute | solution.py:191
  13.1 17.9 %collective-permute-start = (f32[512,128]{1,0:T(8,128)}, f32[512,128]{1,0:T(8,128)S(1)}, u32[]{:S(2)}, u32[]{:S(2)}) collective-permute-start(f32[512,128]{1,0:T(8,128)} %own.1), channel_id=1, source_target_pairs={{0,6},{1,763},{6,12},{7,1},{12,18},{13,7},{18,24},{19,13},{24,30},... | collective-permute-start | bytes 786440 | tf_op jit(solution)/shard_map/halo/ppermute | solution.py:187
  23.5 18.5 %collective-permute-start.3 = (f32[512,128]{1,0:T(8,128)S(1)}, f32[512,128]{1,0:T(8,128)S(1)}, u32[]{:S(2)}, u32[]{:S(2)}) collective-permute-start(f32[512,128]{1,0:T(8,128)S(1)} %collective-permute-done.2.other), channel_id=1, source_target_pairs={{0,6},{1,763},{6,12},{7,1},{12,18},{13,7},{18,24},{19,13},{24,30},... | collective-permute-start | bytes 786440 | tf_op jit(solution)/shard_map/halo/ppermute | solution.py:187
  26.2 30.0 %collective-permute-start.5 = (f32[128,512]{1,0:T(8,128)}, f32[128,512]{1,0:T(8,128)S(1)}, u32[]{:S(2)}, u32[]{:S(2)}) collective-permute-start(f32[128,512]{1,0:T(8,128)} %param.8), channel_id=1, source_target_pairs={{0,1},{1,0},{2,3},{3,2},{4,5},{5,4},{6,7},{7,6},{8,9},{9,8},{10,11... | collective-permute-start | bytes 786440 | tf_op jit(solution)/shard_map/weight_gather/ppermute | solution.py:191
  31.0 26.0 %collective-permute-start.1 = (f32[512,128]{1,0:T(8,128)S(1)}, f32[512,128]{1,0:T(8,128)S(1)}, u32[]{:S(2)}, u32[]{:S(2)}) collective-permute-start(f32[512,128]{1,0:T(8,128)S(1)} %collective-permute-done.near), channel_id=1, source_target_pairs={{0,6},{1,763},{6,12},{7,1},{12,18},{13,7},{18,24},{19,13},{24,30},... | collective-permute-start | bytes 786440 | tf_op jit(solution)/shard_map/halo/ppermute | solution.py:187
  42.0 21.6 %collective-permute-start.4 = (f32[512,128]{1,0:T(8,128)S(1)}, f32[512,128]{1,0:T(8,128)S(1)}, u32[]{:S(2)}, u32[]{:S(2)}) collective-permute-start(f32[512,128]{1,0:T(8,128)S(1)} %collective-permute-done.3.near2), channel_id=1, source_target_pairs={{0,6},{1,763},{6,12},{7,1},{12,18},{13,7},{18,24},{19,13},{24,30},... | collective-permute-start | bytes 786440 | tf_op jit(solution)/shard_map/halo/ppermute | solution.py:187
  53.3 0.7 copy-start.3
  53.9 1.2 copy-start
  55.1 1.1 copy-start.8
  56.3 0.7 copy-start.9
  56.3 7.3 %copy-start.1 = (f32[512,128]{1,0:T(8,128)S(1)}, f32[512,128]{1,0:T(8,128)}, u32[]{:S(2)}) copy-start(f32[512,128]{1,0:T(8,128)} %own.1) | copy-start | bytes 786436
  57.0 6.6 %copy-start.2 = (s32[4,4]{1,0:T(4,128)S(1)}, s32[4,4]{1,0:T(4,128)}, u32[]{:S(2)}) copy-start(s32[4,4]{1,0:T(4,128)} %offset.3) | copy-start | bytes 196
  65.2 5.8 %collective-permute-start.6 = (f32[2,512,128]{2,1,0:T(8,128)S(1)}, f32[2,512,128]{2,1,0:T(8,128)S(1)}, u32[]{:S(2)}, u32[]{:S(2)}) collective-permute-start(f32[2,512,128]{2,1,0:T(8,128)S(1)} %get-tuple-element.24), channel_id=1, source_target_pairs={{0,1},{1,0},{2,3},{3,2},{4,5},{5,4},{6,7},{7,6},{8,9},{9,8},{10,11... | collective-permute-start | bytes 1572872 | tf_op jit(solution)/shard_map/mixed_gather/ppermute | solution.py:191
  67.1 9.9 %collective-permute-start.9 = (f32[2,64,512]{2,1,0:T(8,128)S(1)}, f32[2,64,512]{2,1,0:T(8,128)}, u32[]{:S(2)}, u32[]{:S(2)}) collective-permute-start(f32[2,64,512]{2,1,0:T(8,128)S(1)} %fusion), channel_id=1, source_target_pairs={{0,2},{1,5},{2,4},{3,1},{4,0},{5,3},{6,8},{7,11},{8,10},{9,7},{10,... | collective-permute-start | bytes 786440 | tf_op jit(solution)/shard_map/weight_gather/ppermute | solution.py:187
  71.1 20.1 %collective-permute-start.7 = (f32[2,512,128]{2,1,0:T(8,128)S(1)}, f32[2,512,128]{2,1,0:T(8,128)S(1)}, u32[]{:S(2)}, u32[]{:S(2)}) collective-permute-start(f32[2,512,128]{2,1,0:T(8,128)S(1)} %add_multiply_fusion.mixed), channel_id=1, source_target_pairs={{0,2},{1,5},{2,4},{3,1},{4,0},{5,3},{6,8},{7,11},{8,10},{9,7},{10,... | collective-permute-start | bytes 1572872 | tf_op jit(solution)/shard_map/mixed_gather/ppermute | solution.py:187
  77.0 7.6 %collective-permute-start.10 = (f32[2,64,512]{2,1,0:T(8,128)}, f32[2,64,512]{2,1,0:T(8,128)S(1)}, u32[]{:S(2)}, u32[]{:S(2)}) collective-permute-start(f32[2,64,512]{2,1,0:T(8,128)} %collective-permute-done.9), channel_id=1, source_target_pairs={{0,192},{192,0},{384,576},{576,384},{1,193},{193,1},{385,577},{577... | collective-permute-start | bytes 786440 | tf_op jit(solution)/shard_map/weight_gather/ppermute | solution.py:213
  79.0 14.1 %copy-start.10 = (f32[128,512]{1,0:T(8,128)S(1)}, f32[128,512]{1,0:T(8,128)}, u32[]{:S(2)}) copy-start(f32[128,512]{1,0:T(8,128)} %copy-done.9) | copy-start | bytes 786436
  79.0 16.0 %copy-start.4 = (f32[512,512]{1,0:T(8,128)S(1)}, f32[512,512]{1,0:T(8,128)}, u32[]{:S(2)}) copy-start(f32[512,512]{1,0:T(8,128)} %gout.1) | copy-start | bytes 3145732
  85.7 7.4 %collective-permute-start.11 = (f32[2,128,512]{2,1,0:T(8,128)S(1)}, f32[2,128,512]{2,1,0:T(8,128)S(1)}, u32[]{:S(2)}, u32[]{:S(2)}) collective-permute-start(f32[2,128,512]{2,1,0:T(8,128)S(1)} %maximum_select_fusion.weight_got), channel_id=1, source_target_pairs={{0,1},{1,0},{2,3},{3,2},{4,5},{5,4},{6,7},{7,6},{8,9},{9,8},{10,11... | collective-permute-start | bytes 1572872 | tf_op jit(solution)/shard_map/weight_gather/ppermute | solution.py:191
  91.2 3.8 %collective-permute-start.8 = (f32[2,512,128]{2,1,0:T(8,128)S(1)}, f32[2,512,128]{2,1,0:T(8,128)S(1)}, u32[]{:S(2)}, u32[]{:S(2)}) collective-permute-start(f32[2,512,128]{2,1,0:T(8,128)S(1)} %collective-permute-done.7.got), channel_id=1, source_target_pairs={{0,1},{1,0},{2,3},{3,2},{4,5},{5,4},{6,7},{7,6},{8,9},{9,8},{10,11... | collective-permute-start | bytes 1572872 | tf_op jit(solution)/shard_map/mixed_gather/ppermute | solution.py:191
  93.2 1.8 %copy-start.7 = (f32[512]{0:T(512)S(1)}, f32[512]{0:T(512)}, u32[]{:S(2)}) copy-start(f32[512]{0:T(512)} %param.9) | copy-start | bytes 6148
  100.7 0.8 copy-start.5
  101.5 4.0 %copy-start.6 = (f32[512,256]{1,0:T(8,128)S(1)}, f32[512,256]{1,0:T(8,128)}, u32[]{:S(2)}) copy-start(f32[512,256]{1,0:T(8,128)} %copy-done.5) | copy-start | bytes 1572868
  101.5 17.2 %all-to-all-start = ((f32[32,24,128]{2,1,0:T(8,128)}), f32[32,24,128]{2,1,0:T(8,128)S(1)}, u32[]{:S(2)}, u32[]{:S(2)}) async-start(f32[32,24,128]{2,1,0:T(8,128)} %get-tuple-element.31), calls=%async_computation | async-start | bytes 786432 | tf_op jit(solution)/shard_map/nodes_sum/all_to_all | solution.py:272
  105.6 30.7 %collective-permute-start.12 = (f32[512,256]{1,0:T(8,128)S(1)}, f32[512,256]{1,0:T(8,128)S(1)}, u32[]{:S(2)}, u32[]{:S(2)}) collective-permute-start(f32[512,256]{1,0:T(8,128)S(1)} %copy-done.6), channel_id=1, source_target_pairs={{0,6},{1,763},{6,12},{7,1},{12,18},{13,7},{18,24},{19,13},{24,30},... | collective-permute-start | bytes 1572872 | tf_op jit(solution)/shard_map/back_halo/ppermute | solution.py:187
  119.9 27.7 %all-to-all-start.1 = ((f32[4,24,128]{2,1,0:T(8,128)}), f32[4,24,128]{2,1,0:T(8,128)S(1)}, u32[]{:S(2)}, u32[]{:S(2)}) async-start(f32[4,24,128]{2,1,0:T(8,128)} %broadcast_in_dim.4), calls=%async_computation.1 | async-start | bytes 98304 | tf_op jit(solution)/shard_map/nodes_sum/all_to_all | solution.py:278
  136.4 20.0 %collective-permute-start.13 = (f32[512,128]{1,0:T(8,128)S(1)}, f32[512,128]{1,0:T(8,128)S(1)}, u32[]{:S(2)}, u32[]{:S(2)}) collective-permute-start(f32[512,128]{1,0:T(8,128)S(1)} %fusion.1), channel_id=1, source_target_pairs={{0,6},{1,763},{6,12},{7,1},{12,18},{13,7},{18,24},{19,13},{24,30},... | collective-permute-start | bytes 786440 | tf_op jit(solution)/shard_map/back_halo/ppermute | solution.py:187
  147.7 16.9 %collective-permute-start.14 = (f32[512,128]{1,0:T(8,128)S(1)}, f32[512,128]{1,0:T(8,128)S(1)}, u32[]{:S(2)}, u32[]{:S(2)}) collective-permute-start(f32[512,128]{1,0:T(8,128)S(1)} %select_add_fusion), channel_id=1, source_target_pairs={{0,7},{1,762},{6,13},{7,0},{12,19},{13,6},{18,25},{19,12},{24,31},... | collective-permute-start | bytes 786440 | tf_op jit(solution)/shard_map/back_halo/ppermute | solution.py:187
  151.9 14.2 %all-to-all-start.2 = ((f32[32,16,128]{2,1,0:T(8,128)}), f32[32,16,128]{2,1,0:T(8,128)S(1)}, u32[]{:S(2)}, u32[]{:S(2)}) async-start(f32[32,16,128]{2,1,0:T(8,128)} %broadcast_in_dim.5), calls=%async_computation.2 | async-start | bytes 524288 | tf_op jit(solution)/shard_map/nodes_sum/all_to_all | solution.py:287

commit v6 on v5

--- a/solution.py
+++ b/solution.py
@@ -277,9 +277,9 @@
         held = jnp.broadcast_to(held[None], (4, 24, T))
         held = jnp.sum(lax.all_to_all(held, "zh", 0, 0), axis=0)
     with jax.named_scope("back_halo"):
-        kept = q_near + plane[:1, :1] * 0.0 + jnp.where(c == 0, came[:, :width], came[:, width:])
-        came, held = lax.optimization_barrier((came, held))
-        lent = q_other + jnp.where(c == 0, came[:, width:], came[:, :width])
+        after = plane[:1, :1] * 0.0
+        kept = q_near + after + jnp.where(c == 0, came[:, :width], came[:, width:])
+        lent = q_other + after + jnp.where(c == 0, came[:, width:], came[:, :width])
         grad_features = center + (by_core(kept, NODES, 1, -1) + by_core(lent, NODES, 1, -1, True))
     with jax.named_scope("nodes_sum"):
         grad_bias = held[16:20].reshape(-1)

time: 168 us -> 167 us (level)
  starting transfers between devices: 110 us -> 108 us
    all_to_all x1, waiting for transfers between devices: 0.74 us -> 3.8 us  [body(): whole = lax.all_to_all(whole, PLANE, 0, 0)]
    ppermute x9, waiting for transfers between devices: 30.1 us -> 28.3 us  [by_core(): return lax.ppermute(block, axes, route)]
  transfers between devices with their start and end apart: 18 -> 18, of which waited for: 8 -> 9; matrix products, arithmetic and copies ran while one was open for 3% -> 3% of each run, Pallas kernels for 1% -> 1%
where the time goes in v6:
time: 167 us; the launch traced here: 166 us
  starting transfers between devices  108 us (65%)
  waiting for transfers between devices  39.6 us (24%)
  Pallas kernels  9.1 us (5%)
  local copies, waits for them, and re-layouts  5.83 us (3%)
  other arithmetic  2.15 us (1%)
    ppermute x9, starting transfers between devices, by_core(): return lax.ppermute(block, axes, route)  67.6 us
    ppermute x9, waiting for transfers between devices, by_core(): return lax.ppermute(block, axes, route)  28.3 us
    ppermute x5, starting transfers between devices, swap(): return lax.ppermute(block, 'c', [(0, 1), (1, 0)])  23.6 us
    all_to_all x1, starting transfers between devices, body(): held = jnp.sum(lax.all_to_all(held, 'zh', 0, 0), axis=0)  7.12 us
    pallas_call x1, Pallas kernels, body(): call(layer_kernel, [SMEM] * 2 + [VMEM] * 10, [shape_of((rows, 4 * T)), sh...  5.74 us
    ppermute x1, waiting for transfers between devices, body(): theirs = lax.ppermute(half, 'x', [(i, i ^ 1) for i in range(4)])  5.66 us
    all_to_all x1, starting transfers between devices, body(): held = jnp.sum(lax.all_to_all(parts, PLANE, 0, 0), axis=0)  4.01 us
    all_to_all x1, starting transfers between devices, body(): whole = lax.all_to_all(whole, PLANE, 0, 0)  3.87 us
  transfers between devices with their start and end apart: 18, of which 9 were waited for; matrix products, arithmetic and copies ran while one was open for 3% of the time, Pallas kernels for 1%

profile of v6, /device:TPU:1, one launch (start us, length us, event | category | flops | bytes accessed | tf_op | source)
XLA Modules:
  0.0 166.4 jit_solution(8173094700167554651)
XLA Ops:
  0.6 12.4 %collective-permute-start.2 = (f32[512,128]{1,0:T(8,128)}, f32[512,128]{1,0:T(8,128)S(1)}, u32[]{:S(2)}, u32[]{:S(2)}) collective-permute-start(f32[512,128]{1,0:T(8,128)} %own.1), channel_id=1, source_target_pairs={{0,1},{1,0},{2,3},{3,2},{4,5},{5,4},{6,7},{7,6},{8,9},{9,8},{10,11... | collective-permute-start | bytes 786440 | tf_op jit(solution)/shard_map/halo/ppermute | solution.py:191
  13.1 10.4 %collective-permute-start = (f32[512,128]{1,0:T(8,128)}, f32[512,128]{1,0:T(8,128)S(1)}, u32[]{:S(2)}, u32[]{:S(2)}) collective-permute-start(f32[512,128]{1,0:T(8,128)} %own.1), channel_id=1, source_target_pairs={{0,6},{1,763},{6,12},{7,1},{12,18},{13,7},{18,24},{19,13},{24,30},... | collective-permute-start | bytes 786440 | tf_op jit(solution)/shard_map/halo/ppermute | solution.py:187
  23.5 2.8 %collective-permute-start.3 = (f32[512,128]{1,0:T(8,128)S(1)}, f32[512,128]{1,0:T(8,128)S(1)}, u32[]{:S(2)}, u32[]{:S(2)}) collective-permute-start(f32[512,128]{1,0:T(8,128)S(1)} %collective-permute-done.2.other), channel_id=1, source_target_pairs={{0,6},{1,763},{6,12},{7,1},{12,18},{13,7},{18,24},{19,13},{24,30},... | collective-permute-start | bytes 786440 | tf_op jit(solution)/shard_map/halo/ppermute | solution.py:187
  26.2 1.9 %collective-permute-start.5 = (f32[128,512]{1,0:T(8,128)}, f32[128,512]{1,0:T(8,128)S(1)}, u32[]{:S(2)}, u32[]{:S(2)}) collective-permute-start(f32[128,512]{1,0:T(8,128)} %param.8), channel_id=1, source_target_pairs={{0,1},{1,0},{2,3},{3,2},{4,5},{5,4},{6,7},{7,6},{8,9},{9,8},{10,11... | collective-permute-start | bytes 786440 | tf_op jit(solution)/shard_map/weight_gather/ppermute | solution.py:191
  28.2 2.8 %collective-permute-done.near = f32[512,128]{1,0:T(8,128)S(1)} collective-permute-done((f32[512,128]{1,0:T(8,128)}, f32[512,128]{1,0:T(8,128)S(1)}, u32[]{:S(2)}, u32[]{:S(2)}) %collective-permute-start) | collective-permute-done | bytes 262176 | tf_op jit(solution)/shard_map/halo/ppermute | solution.py:187
  31.0 11.0 %collective-permute-start.1 = (f32[512,128]{1,0:T(8,128)S(1)}, f32[512,128]{1,0:T(8,128)S(1)}, u32[]{:S(2)}, u32[]{:S(2)}) collective-permute-start(f32[512,128]{1,0:T(8,128)S(1)} %collective-permute-done.near), channel_id=1, source_target_pairs={{0,6},{1,763},{6,12},{7,1},{12,18},{13,7},{18,24},{19,13},{24,30},... | collective-permute-start | bytes 786440 | tf_op jit(solution)/shard_map/halo/ppermute | solution.py:187
  42.0 0.0 collective-permute-done.3.near2
  42.0 11.2 %collective-permute-start.4 = (f32[512,128]{1,0:T(8,128)S(1)}, f32[512,128]{1,0:T(8,128)S(1)}, u32[]{:S(2)}, u32[]{:S(2)}) collective-permute-start(f32[512,128]{1,0:T(8,128)S(1)} %collective-permute-done.3.near2), channel_id=1, source_target_pairs={{0,6},{1,763},{6,12},{7,1},{12,18},{13,7},{18,24},{19,13},{24,30},... | collective-permute-start | bytes 786440 | tf_op jit(solution)/shard_map/halo/ppermute | solution.py:187
  53.3 0.6 copy-done.3
  53.9 1.2 copy-done
  55.2 1.0 prepare.1
  56.2 0.1 pad_add_fusion.where
  56.3 0.7 copy-done.9
  57.0 6.6 %collective-permute-done.4.far2 = f32[512,128]{1,0:T(8,128)S(1)} collective-permute-done((f32[512,128]{1,0:T(8,128)S(1)}, f32[512,128]{1,0:T(8,128)S(1)}, u32[]{:S(2)}, u32[]{:S(2)}) %collective-permute-start.4) | collective-permute-done | bytes 262176 | tf_op jit(solution)/shard_map/halo/ppermute | solution.py:187
  63.6 1.6 mix.1
  65.2 1.9 %collective-permute-start.6 = (f32[2,512,128]{2,1,0:T(8,128)S(1)}, f32[2,512,128]{2,1,0:T(8,128)S(1)}, u32[]{:S(2)}, u32[]{:S(2)}) collective-permute-start(f32[2,512,128]{2,1,0:T(8,128)S(1)} %get-tuple-element.22), channel_id=1, source_target_pairs={{0,1},{1,0},{2,3},{3,2},{4,5},{5,4},{6,7},{7,6},{8,9},{9,8},{10,11... | collective-permute-start | bytes 1572872 | tf_op jit(solution)/shard_map/mixed_gather/ppermute | solution.py:191
  67.1 3.9 %collective-permute-start.9 = (f32[2,64,512]{2,1,0:T(8,128)S(1)}, f32[2,64,512]{2,1,0:T(8,128)}, u32[]{:S(2)}, u32[]{:S(2)}) collective-permute-start(f32[2,64,512]{2,1,0:T(8,128)S(1)} %fusion), channel_id=1, source_target_pairs={{0,2},{1,5},{2,4},{3,1},{4,0},{5,3},{6,8},{7,11},{8,10},{9,7},{10,... | collective-permute-start | bytes 786440 | tf_op jit(solution)/shard_map/weight_gather/ppermute | solution.py:187
  71.0 0.1 add_multiply_fusion.mixed
  71.1 2.1 %collective-permute-start.7 = (f32[2,512,128]{2,1,0:T(8,128)S(1)}, f32[2,512,128]{2,1,0:T(8,128)S(1)}, u32[]{:S(2)}, u32[]{:S(2)}) collective-permute-start(f32[2,512,128]{2,1,0:T(8,128)S(1)} %add_multiply_fusion.mixed), channel_id=1, source_target_pairs={{0,2},{1,5},{2,4},{3,1},{4,0},{5,3},{6,8},{7,11},{8,10},{9,7},{10,... | collective-permute-start | bytes 1572872 | tf_op jit(solution)/shard_map/mixed_gather/ppermute | solution.py:187
  73.2 3.8 %collective-permute-done.9 = f32[2,64,512]{2,1,0:T(8,128)} collective-permute-done((f32[2,64,512]{2,1,0:T(8,128)S(1)}, f32[2,64,512]{2,1,0:T(8,128)}, u32[]{:S(2)}, u32[]{:S(2)}) %collective-permute-start.9) | collective-permute-done | bytes 262176 | tf_op jit(solution)/shard_map/weight_gather/ppermute | solution.py:187
  77.0 1.9 %collective-permute-start.10 = (f32[2,64,512]{2,1,0:T(8,128)}, f32[2,64,512]{2,1,0:T(8,128)S(1)}, u32[]{:S(2)}, u32[]{:S(2)}) collective-permute-start(f32[2,64,512]{2,1,0:T(8,128)} %collective-permute-done.9), channel_id=1, source_target_pairs={{0,192},{192,0},{384,576},{576,384},{1,193},{193,1},{385,577},{577... | collective-permute-start | bytes 786440 | tf_op jit(solution)/shard_map/weight_gather/ppermute | solution.py:213
  79.0 0.0 copy-start.10
  79.0 0.0 copy-start.4
  79.0 5.7 %collective-permute-done.10 = f32[2,64,512]{2,1,0:T(8,128)S(1)} collective-permute-done((f32[2,64,512]{2,1,0:T(8,128)}, f32[2,64,512]{2,1,0:T(8,128)S(1)}, u32[]{:S(2)}, u32[]{:S(2)}) %collective-permute-start.10) | collective-permute-done | bytes 262176 | tf_op jit(solution)/shard_map/weight_gather/ppermute | solution.py:213
  84.7 1.1 maximum_select_fusion.weight_got
  85.7 5.4 %collective-permute-start.11 = (f32[2,128,512]{2,1,0:T(8,128)S(1)}, f32[2,128,512]{2,1,0:T(8,128)S(1)}, u32[]{:S(2)}, u32[]{:S(2)}) collective-permute-start(f32[2,128,512]{2,1,0:T(8,128)S(1)} %maximum_select_fusion.weight_got), channel_id=1, source_target_pairs={{0,1},{1,0},{2,3},{3,2},{4,5},{5,4},{6,7},{7,6},{8,9},{9,8},{10,11... | collective-permute-start | bytes 1572872 | tf_op jit(solution)/shard_map/weight_gather/ppermute | solution.py:191
  91.2 1.9 %collective-permute-start.8 = (f32[2,512,128]{2,1,0:T(8,128)S(1)}, f32[2,512,128]{2,1,0:T(8,128)S(1)}, u32[]{:S(2)}, u32[]{:S(2)}) collective-permute-start(f32[2,512,128]{2,1,0:T(8,128)S(1)} %collective-permute-done.7.got), channel_id=1, source_target_pairs={{0,1},{1,0},{2,3},{3,2},{4,5},{5,4},{6,7},{7,6},{8,9},{9,8},{10,11... | collective-permute-start | bytes 1572872 | tf_op jit(solution)/shard_map/mixed_gather/ppermute | solution.py:191
  93.2 0.0 copy-start.7
  93.2 1.8 %collective-permute-done.8.swapped = f32[2,512,128]{2,1,0:T(8,128)S(1)} collective-permute-done((f32[2,512,128]{2,1,0:T(8,128)S(1)}, f32[2,512,128]{2,1,0:T(8,128)S(1)}, u32[]{:S(2)}, u32[]{:S(2)}) %collective-permute-start.8) | collective-permute-done | bytes 524320 | tf_op jit(solution)/shard_map/mixed_gather/ppermute | solution.py:191
  95.0 5.7 %layer.1 = (f32[512,512]{1,0:T(8,128)}, f32[32,24,128]{2,1,0:T(8,128)}, f32[512,256]{1,0:T(8,128)S(1)}, f32[512,128]{1,0:T(8,128)S(1)}, f32[512,128]{1,0:T(8,128)S(1)}, /*index=5*/f32[512,128]{1,0:T(8,128)S(1)}) custom-call(s32[2]{0:T(128)S(1)} %pad_add_fusion.where, s32[4,4]{1,0:T(4,128)S(1)} %copy-done.2, f32[2,512,128]{2,1,0:T(8,128)S(1)} %add_multiply_fusion.mixed, ...), custom_call_target="tpu_custom_call" | custom-call | flops 1500000000 | bytes 10000000 | tf_op jit(solution)/shard_map/layer/pallas_call | solution.py:248
  100.7 0.8 copy-done.5
  101.6 4.0 %all-to-all-start = ((f32[32,24,128]{2,1,0:T(8,128)}), f32[32,24,128]{2,1,0:T(8,128)S(1)}, u32[]{:S(2)}, u32[]{:S(2)}) async-start(f32[32,24,128]{2,1,0:T(8,128)} %get-tuple-element.29), calls=%async_computation | async-start | bytes 786432 | tf_op jit(solution)/shard_map/nodes_sum/all_to_all | solution.py:272
  105.6 13.1 %collective-permute-start.12 = (f32[512,256]{1,0:T(8,128)S(1)}, f32[512,256]{1,0:T(8,128)S(1)}, u32[]{:S(2)}, u32[]{:S(2)}) collective-permute-start(f32[512,256]{1,0:T(8,128)S(1)} %copy-done.6), channel_id=1, source_target_pairs={{0,6},{1,763},{6,12},{7,1},{12,18},{13,7},{18,24},{19,13},{24,30},... | collective-permute-start | bytes 1572872 | tf_op jit(solution)/shard_map/back_halo/ppermute | solution.py:187
  118.8 0.5 slice.22
  119.3 0.6 broadcast_in_dim.4
  119.9 7.1 %all-to-all-start.1 = ((f32[4,24,128]{2,1,0:T(8,128)}), f32[4,24,128]{2,1,0:T(8,128)S(1)}, u32[]{:S(2)}, u32[]{:S(2)}) async-start(f32[4,24,128]{2,1,0:T(8,128)} %broadcast_in_dim.4), calls=%async_computation.1 | async-start | bytes 98304 | tf_op jit(solution)/shard_map/nodes_sum/all_to_all | solution.py:278
  127.7 8.7 %collective-permute-done.12 = f32[512,256]{1,0:T(8,128)S(1)} collective-permute-done((f32[512,256]{1,0:T(8,128)S(1)}, f32[512,256]{1,0:T(8,128)S(1)}, u32[]{:S(2)}, u32[]{:S(2)}) %collective-permute-start.12) | collective-permute-done | bytes 524320 | tf_op jit(solution)/shard_map/back_halo/ppermute | solution.py:187
  136.3 0.1 select_add_fusion
  136.4 6.9 %collective-permute-start.14 = (f32[512,128]{1,0:T(8,128)S(1)}, f32[512,128]{1,0:T(8,128)S(1)}, u32[]{:S(2)}, u32[]{:S(2)}) collective-permute-start(f32[512,128]{1,0:T(8,128)S(1)} %get-tuple-element.32), channel_id=1, source_target_pairs={{0,7},{1,762},{6,13},{7,0},{12,19},{13,6},{18,25},{19,12},{24,31},... | collective-permute-start | bytes 786440 | tf_op jit(solution)/shard_map/back_halo/ppermute | solution.py:187
  143.3 6.2 %collective-permute-start.13 = (f32[512,128]{1,0:T(8,128)S(1)}, f32[512,128]{1,0:T(8,128)S(1)}, u32[]{:S(2)}, u32[]{:S(2)}) collective-permute-start(f32[512,128]{1,0:T(8,128)S(1)} %get-tuple-element.33), channel_id=1, source_target_pairs={{0,6},{1,763},{6,12},{7,1},{12,18},{13,7},{18,24},{19,13},{24,30},... | collective-permute-start | bytes 786440 | tf_op jit(solution)/shard_map/back_halo/ppermute | solution.py:187
  149.5 0.7 broadcast_in_dim.5
  150.2 3.9 %all-to-all-start.2 = ((f32[32,16,128]{2,1,0:T(8,128)}), f32[32,16,128]{2,1,0:T(8,128)S(1)}, u32[]{:S(2)}, u32[]{:S(2)}) async-start(f32[32,16,128]{2,1,0:T(8,128)} %broadcast_in_dim.5), calls=%async_computation.2 | async-start | bytes 524288 | tf_op jit(solution)/shard_map/nodes_sum/all_to_all | solution.py:287
  154.1 0.6 slice_bitcast_fusion
  154.7 1.5 collective-permute-done.14
  156.2 5.0 %collective-permute-done.13 = f32[512,128]{1,0:T(8,128)S(1)} collective-permute-done((f32[512,128]{1,0:T(8,128)S(1)}, f32[512,128]{1,0:T(8,128)S(1)}, u32[]{:S(2)}, u32[]{:S(2)}) %collective-permute-start.13) | collective-permute-done | bytes 262176 | tf_op jit(solution)/shard_map/back_halo/ppermute | solution.py:187
  161.2 0.7 add_add_fusion
  161.9 3.8 %all-to-all-done.2.pieces = f32[32,16,128]{2,1,0:T(8,128)S(1)} async-done(((f32[32,16,128]{2,1,0:T(8,128)}), f32[32,16,128]{2,1,0:T(8,128)S(1)}, u32[]{:S(2)}, u32[]{:S(2)}) %all-to-all-start.2) | async-done | bytes 262176 | tf_op jit(solution)/shard_map/nodes_sum/all_to_all | solution.py:287
  165.7 0.7 arrange.1
  (28 shorter events, 0.2 us)
Async XLA Ops:
  0.6 22.8 %collective-permute-start.2 = (f32[512,128]{1,0:T(8,128)}, f32[512,128]{1,0:T(8,128)S(1)}, u32[]{:S(2)}, u32[]{:S(2)}) collective-permute-start(f32[512,128]{1,0:T(8,128)} %own.1), channel_id=1, source_target_pairs={{0,1},{1,0},{2,3},{3,2},{4,5},{5,4},{6,7},{7,6},{8,9},{9,8},{10,11... | collective-permute-start | bytes 786440 | tf_op jit(solution)/shard_map/halo/ppermute | solution.py:191
  13.1 17.9 %collective-permute-start = (f32[512,128]{1,0:T(8,128)}, f32[512,128]{1,0:T(8,128)S(1)}, u32[]{:S(2)}, u32[]{:S(2)}) collective-permute-start(f32[512,128]{1,0:T(8,128)} %own.1), channel_id=1, source_target_pairs={{0,6},{1,763},{6,12},{7,1},{12,18},{13,7},{18,24},{19,13},{24,30},... | collective-permute-start | bytes 786440 | tf_op jit(solution)/shard_map/halo/ppermute | solution.py:187
  23.5 18.5 %collective-permute-start.3 = (f32[512,128]{1,0:T(8,128)S(1)}, f32[512,128]{1,0:T(8,128)S(1)}, u32[]{:S(2)}, u32[]{:S(2)}) collective-permute-start(f32[512,128]{1,0:T(8,128)S(1)} %collective-permute-done.2.other), channel_id=1, source_target_pairs={{0,6},{1,763},{6,12},{7,1},{12,18},{13,7},{18,24},{19,13},{24,30},... | collective-permute-start | bytes 786440 | tf_op jit(solution)/shard_map/halo/ppermute | solution.py:187
  26.2 30.0 %collective-permute-start.5 = (f32[128,512]{1,0:T(8,128)}, f32[128,512]{1,0:T(8,128)S(1)}, u32[]{:S(2)}, u32[]{:S(2)}) collective-permute-start(f32[128,512]{1,0:T(8,128)} %param.8), channel_id=1, source_target_pairs={{0,1},{1,0},{2,3},{3,2},{4,5},{5,4},{6,7},{7,6},{8,9},{9,8},{10,11... | collective-permute-start | bytes 786440 | tf_op jit(solution)/shard_map/weight_gather/ppermute | solution.py:191
  31.0 26.0 %collective-permute-start.1 = (f32[512,128]{1,0:T(8,128)S(1)}, f32[512,128]{1,0:T(8,128)S(1)}, u32[]{:S(2)}, u32[]{:S(2)}) collective-permute-start(f32[512,128]{1,0:T(8,128)S(1)} %collective-permute-done.near), channel_id=1, source_target_pairs={{0,6},{1,763},{6,12},{7,1},{12,18},{13,7},{18,24},{19,13},{24,30},... | collective-permute-start | bytes 786440 | tf_op jit(solution)/shard_map/halo/ppermute | solution.py:187
  42.0 21.6 %collective-permute-start.4 = (f32[512,128]{1,0:T(8,128)S(1)}, f32[512,128]{1,0:T(8,128)S(1)}, u32[]{:S(2)}, u32[]{:S(2)}) collective-permute-start(f32[512,128]{1,0:T(8,128)S(1)} %collective-permute-done.3.near2), channel_id=1, source_target_pairs={{0,6},{1,763},{6,12},{7,1},{12,18},{13,7},{18,24},{19,13},{24,30},... | collective-permute-start | bytes 786440 | tf_op jit(solution)/shard_map/halo/ppermute | solution.py:187
  53.3 0.7 copy-start.3
  53.9 1.2 copy-start
  55.1 1.1 copy-start.8
  56.3 0.7 copy-start.9
  56.3 7.3 %copy-start.1 = (f32[512,128]{1,0:T(8,128)S(1)}, f32[512,128]{1,0:T(8,128)}, u32[]{:S(2)}) copy-start(f32[512,128]{1,0:T(8,128)} %own.1) | copy-start | bytes 786436
  57.0 6.6 %copy-start.2 = (s32[4,4]{1,0:T(4,128)S(1)}, s32[4,4]{1,0:T(4,128)}, u32[]{:S(2)}) copy-start(s32[4,4]{1,0:T(4,128)} %offset.3) | copy-start | bytes 196
  65.2 5.8 %collective-permute-start.6 = (f32[2,512,128]{2,1,0:T(8,128)S(1)}, f32[2,512,128]{2,1,0:T(8,128)S(1)}, u32[]{:S(2)}, u32[]{:S(2)}) collective-permute-start(f32[2,512,128]{2,1,0:T(8,128)S(1)} %get-tuple-element.22), channel_id=1, source_target_pairs={{0,1},{1,0},{2,3},{3,2},{4,5},{5,4},{6,7},{7,6},{8,9},{9,8},{10,11... | collective-permute-start | bytes 1572872 | tf_op jit(solution)/shard_map/mixed_gather/ppermute | solution.py:191
  67.1 9.9 %collective-permute-start.9 = (f32[2,64,512]{2,1,0:T(8,128)S(1)}, f32[2,64,512]{2,1,0:T(8,128)}, u32[]{:S(2)}, u32[]{:S(2)}) collective-permute-start(f32[2,64,512]{2,1,0:T(8,128)S(1)} %fusion), channel_id=1, source_target_pairs={{0,2},{1,5},{2,4},{3,1},{4,0},{5,3},{6,8},{7,11},{8,10},{9,7},{10,... | collective-permute-start | bytes 786440 | tf_op jit(solution)/shard_map/weight_gather/ppermute | solution.py:187
  71.1 20.1 %collective-permute-start.7 = (f32[2,512,128]{2,1,0:T(8,128)S(1)}, f32[2,512,128]{2,1,0:T(8,128)S(1)}, u32[]{:S(2)}, u32[]{:S(2)}) collective-permute-start(f32[2,512,128]{2,1,0:T(8,128)S(1)} %add_multiply_fusion.mixed), channel_id=1, source_target_pairs={{0,2},{1,5},{2,4},{3,1},{4,0},{5,3},{6,8},{7,11},{8,10},{9,7},{10,... | collective-permute-start | bytes 1572872 | tf_op jit(solution)/shard_map/mixed_gather/ppermute | solution.py:187
  77.0 7.6 %collective-permute-start.10 = (f32[2,64,512]{2,1,0:T(8,128)}, f32[2,64,512]{2,1,0:T(8,128)S(1)}, u32[]{:S(2)}, u32[]{:S(2)}) collective-permute-start(f32[2,64,512]{2,1,0:T(8,128)} %collective-permute-done.9), channel_id=1, source_target_pairs={{0,192},{192,0},{384,576},{576,384},{1,193},{193,1},{385,577},{577... | collective-permute-start | bytes 786440 | tf_op jit(solution)/shard_map/weight_gather/ppermute | solution.py:213
  79.0 14.1 %copy-start.10 = (f32[128,512]{1,0:T(8,128)S(1)}, f32[128,512]{1,0:T(8,128)}, u32[]{:S(2)}) copy-start(f32[128,512]{1,0:T(8,128)} %copy-done.9) | copy-start | bytes 786436
  79.0 16.0 %copy-start.4 = (f32[512,512]{1,0:T(8,128)S(1)}, f32[512,512]{1,0:T(8,128)}, u32[]{:S(2)}) copy-start(f32[512,512]{1,0:T(8,128)} %gout.1) | copy-start | bytes 3145732
  85.7 7.4 %collective-permute-start.11 = (f32[2,128,512]{2,1,0:T(8,128)S(1)}, f32[2,128,512]{2,1,0:T(8,128)S(1)}, u32[]{:S(2)}, u32[]{:S(2)}) collective-permute-start(f32[2,128,512]{2,1,0:T(8,128)S(1)} %maximum_select_fusion.weight_got), channel_id=1, source_target_pairs={{0,1},{1,0},{2,3},{3,2},{4,5},{5,4},{6,7},{7,6},{8,9},{9,8},{10,11... | collective-permute-start | bytes 1572872 | tf_op jit(solution)/shard_map/weight_gather/ppermute | solution.py:191
  91.2 3.8 %collective-permute-start.8 = (f32[2,512,128]{2,1,0:T(8,128)S(1)}, f32[2,512,128]{2,1,0:T(8,128)S(1)}, u32[]{:S(2)}, u32[]{:S(2)}) collective-permute-start(f32[2,512,128]{2,1,0:T(8,128)S(1)} %collective-permute-done.7.got), channel_id=1, source_target_pairs={{0,1},{1,0},{2,3},{3,2},{4,5},{5,4},{6,7},{7,6},{8,9},{9,8},{10,11... | collective-permute-start | bytes 1572872 | tf_op jit(solution)/shard_map/mixed_gather/ppermute | solution.py:191
  93.2 1.8 %copy-start.7 = (f32[512]{0:T(512)S(1)}, f32[512]{0:T(512)}, u32[]{:S(2)}) copy-start(f32[512]{0:T(512)} %param.9) | copy-start | bytes 6148
  100.7 0.8 copy-start.5
  101.6 4.0 %copy-start.6 = (f32[512,256]{1,0:T(8,128)S(1)}, f32[512,256]{1,0:T(8,128)}, u32[]{:S(2)}) copy-start(f32[512,256]{1,0:T(8,128)} %copy-done.5) | copy-start | bytes 1572868
  101.6 17.2 %all-to-all-start = ((f32[32,24,128]{2,1,0:T(8,128)}), f32[32,24,128]{2,1,0:T(8,128)S(1)}, u32[]{:S(2)}, u32[]{:S(2)}) async-start(f32[32,24,128]{2,1,0:T(8,128)} %get-tuple-element.29), calls=%async_computation | async-start | bytes 786432 | tf_op jit(solution)/shard_map/nodes_sum/all_to_all | solution.py:272
  105.6 30.7 %collective-permute-start.12 = (f32[512,256]{1,0:T(8,128)S(1)}, f32[512,256]{1,0:T(8,128)S(1)}, u32[]{:S(2)}, u32[]{:S(2)}) collective-permute-start(f32[512,256]{1,0:T(8,128)S(1)} %copy-done.6), channel_id=1, source_target_pairs={{0,6},{1,763},{6,12},{7,1},{12,18},{13,7},{18,24},{19,13},{24,30},... | collective-permute-start | bytes 1572872 | tf_op jit(solution)/shard_map/back_halo/ppermute | solution.py:187
  119.9 29.6 %all-to-all-start.1 = ((f32[4,24,128]{2,1,0:T(8,128)}), f32[4,24,128]{2,1,0:T(8,128)S(1)}, u32[]{:S(2)}, u32[]{:S(2)}) async-start(f32[4,24,128]{2,1,0:T(8,128)} %broadcast_in_dim.4), calls=%async_computation.1 | async-start | bytes 98304 | tf_op jit(solution)/shard_map/nodes_sum/all_to_all | solution.py:278
  136.4 19.8 %collective-permute-start.14 = (f32[512,128]{1,0:T(8,128)S(1)}, f32[512,128]{1,0:T(8,128)S(1)}, u32[]{:S(2)}, u32[]{:S(2)}) collective-permute-start(f32[512,128]{1,0:T(8,128)S(1)} %get-tuple-element.32), channel_id=1, source_target_pairs={{0,7},{1,762},{6,13},{7,0},{12,19},{13,6},{18,25},{19,12},{24,31},... | collective-permute-start | bytes 786440 | tf_op jit(solution)/shard_map/back_halo/ppermute | solution.py:187
  143.3 17.9 %collective-permute-start.13 = (f32[512,128]{1,0:T(8,128)S(1)}, f32[512,128]{1,0:T(8,128)S(1)}, u32[]{:S(2)}, u32[]{:S(2)}) collective-permute-start(f32[512,128]{1,0:T(8,128)S(1)} %get-tuple-element.33), channel_id=1, source_target_pairs={{0,6},{1,763},{6,12},{7,1},{12,18},{13,7},{18,24},{19,13},{24,30},... | collective-permute-start | bytes 786440 | tf_op jit(solution)/shard_map/back_halo/ppermute | solution.py:187
  150.2 15.5 %all-to-all-start.2 = ((f32[32,16,128]{2,1,0:T(8,128)}), f32[32,16,128]{2,1,0:T(8,128)S(1)}, u32[]{:S(2)}, u32[]{:S(2)}) async-start(f32[32,16,128]{2,1,0:T(8,128)} %broadcast_in_dim.5), calls=%async_computation.2 | async-start | bytes 524288 | tf_op jit(solution)/shard_map/nodes_sum/all_to_all | solution.py:287
